TPU v7x, 128 devices: a whole 4x4x4 slice. The times are simulated.
128 devices in a mesh: row: 8 (over y, core), col: 16 (over x, z).
Axes of the slice: x: 4, y: 4, z: 4, core: 2. Of those that a mesh axis runs over, the one named last changes fastest.
Arguments:
- object_field: float32 [2, 1024, 2048], P(None, 'row', 'col'), may hold values from -4 to 4
- probe_modes: float32 [8, 2, 128, 128], replicated, may hold values from -1.5 to 1.5
- coefficients: float32 [8, 16, 32, 8], P('row', 'col'), may hold values from -4 to 4
- offsets: int32 [8, 16, 32, 2], P('row', 'col'), may hold values from 0 to 128
- counts: int32 [8, 16], P('row', 'col'), may hold values from 16 to 32
- measured: int32 [8, 16, 32, 128, 128], P('row', 'col'), may hold values from 0 to 4095
Outputs:
- object_out: float32 [2, 1024, 2048], P(None, 'row', 'col')
- modes_out: float32 [8, 2, 128, 128], replicated
- coefficients_out: float32 [8, 16, 32, 8], P('row', 'col')
All inputs are finite; a program needn't handle non-finite values.
Results may differ from a plain program's by a relative error of at most 0.0003.
Values sent between devices are 32-bit elements; how exact they have to be, the bound alone decides.
No kernel may reach another device: no remote copies, remote signals or barrier semaphores. Data moves between devices by JAX's collectives and lax.ppermute only.
A program may use at most 128 MiB of HBM per device.

v0:
```python
import math

import jax
import jax.numpy as jnp
from jax import lax
from jax.sharding import PartitionSpec as P

PS = 128
MODES = 8
TILE = 128
PMAX = 32
BLK = 16
ITERS = 2


amp_floor = 0.5
count_scale = 0.03125
highest = lax.Precision.HIGHEST


def extended_2(block, sides, width):
    for axis, dim in sides:
        count = lax.axis_size(axis)
        forward = [(i, i + 1) for i in range(count - 1)]
        backward = [(target, source) for source, target in forward]
        low = lax.ppermute(
            lax.slice_in_dim(block, block.shape[dim] - width, None, axis=dim), axis, forward
        )
        high = lax.ppermute(lax.slice_in_dim(block, 0, width, axis=dim), axis, backward)
        block = jnp.concatenate([low, block, high], axis=dim)
    return block


def dft_tables(length):
    ramp_values = lax.iota(jnp.int32, length)
    phase_index = ramp_values[:, None] * ramp_values[None, :] % length
    angles = phase_index.astype(jnp.float32) * (2.0 * math.pi / length)
    factor = 1.0 / math.sqrt(length)
    return (jnp.cos(angles) * factor, -jnp.sin(angles) * factor)


def left_apply(cos_part, sin_part, real_part, imag_part):
    result_real = jnp.einsum("ab,nbc->nac", cos_part, real_part, precision=highest) - jnp.einsum(
        "ab,nbc->nac", sin_part, imag_part, precision=highest
    )
    result_imag = jnp.einsum("ab,nbc->nac", cos_part, imag_part, precision=highest) + jnp.einsum(
        "ab,nbc->nac", sin_part, real_part, precision=highest
    )
    return (result_real, result_imag)


def right_apply(cos_part, sin_part, real_part, imag_part):
    result_real = jnp.einsum("nab,bc->nac", real_part, cos_part, precision=highest) - jnp.einsum(
        "nab,bc->nac", imag_part, sin_part, precision=highest
    )
    result_imag = jnp.einsum("nab,bc->nac", real_part, sin_part, precision=highest) + jnp.einsum(
        "nab,bc->nac", imag_part, cos_part, precision=highest
    )
    return (result_real, result_imag)


def transform(cos_part, sin_part, real_part, imag_part):
    left_real, left_imag = left_apply(cos_part, sin_part, real_part, imag_part)
    return right_apply(cos_part, sin_part, left_real, left_imag)


def position_terms(patches, coef_rows, in_use, photons, probe_modes, cos_part, sin_part):
    obj_real = patches[:, 0]
    obj_imag = patches[:, 1]
    probes = jnp.einsum("pk,kcxy->pcxy", coef_rows, probe_modes, precision=highest)
    prb_real = probes[:, 0]
    prb_imag = probes[:, 1]
    psi_real = prb_real * obj_real - prb_imag * obj_imag
    psi_imag = prb_real * obj_imag + prb_imag * obj_real
    far_real, far_imag = transform(cos_part, sin_part, psi_real, psi_imag)
    amplitude = jnp.sqrt(far_real * far_real + far_imag * far_imag)
    target = jnp.sqrt(photons.astype(jnp.float32)) * count_scale
    scaling = target / jnp.maximum(amplitude, amp_floor)
    back_real, back_imag = transform(cos_part, -sin_part, far_real * scaling, far_imag * scaling)
    gate_grid = in_use[:, None, None]
    diff_real = (back_real - psi_real) * gate_grid
    diff_imag = (back_imag - psi_imag) * gate_grid
    grad_real = prb_real * diff_real + prb_imag * diff_imag
    grad_imag = prb_real * diff_imag - prb_imag * diff_real
    weight_grid = (prb_real * prb_real + prb_imag * prb_imag) * gate_grid
    cross_real = obj_real * diff_real + obj_imag * diff_imag
    cross_imag = obj_real * diff_imag - obj_imag * diff_real
    obj_power = (obj_real * obj_real + obj_imag * obj_imag) * gate_grid
    used_coef = coef_rows * in_use[:, None]
    moment_real = jnp.einsum("pk,pxy->kxy", used_coef, cross_real, precision=highest)
    moment_imag = jnp.einsum("pk,pxy->kxy", used_coef, cross_imag, precision=highest)
    moment_power = jnp.einsum("pk,pxy->kxy", used_coef * coef_rows, obj_power, precision=highest)
    mode_real = probe_modes[:, 0]
    mode_imag = probe_modes[:, 1]
    numerator = jnp.einsum("pxy,kxy->pk", cross_real, mode_real, precision=highest) + jnp.einsum(
        "pxy,kxy->pk", cross_imag, mode_imag, precision=highest
    )
    denominator = jnp.einsum(
        "pxy,kxy->pk", obj_power, mode_real * mode_real + mode_imag * mode_imag, precision=highest
    )
    coef_new = coef_rows + numerator / (denominator + 1.0)
    pieces = jnp.stack([grad_real, grad_imag, weight_grid], axis=1)
    return (pieces, (moment_real, moment_imag, moment_power), coef_new)


def fold_edges(padded, margin):
    tile_width = padded.shape[1] - 4 * margin
    lower_edge = 2 * margin
    upper_edge = tile_width + 2 * margin
    outer_edge = tile_width + 3 * margin
    inner_end = tile_width - margin
    interior = padded[:, lower_edge:upper_edge, lower_edge:upper_edge]
    interior = interior.at[:, :margin, :].add(padded[:, :margin, lower_edge:upper_edge])
    interior = interior.at[:, inner_end:, :].add(padded[:, outer_edge:, lower_edge:upper_edge])
    interior = interior.at[:, :, :margin].add(padded[:, lower_edge:upper_edge, :margin])
    interior = interior.at[:, :, inner_end:].add(padded[:, lower_edge:upper_edge, outer_edge:])
    interior = interior.at[:, :margin, :margin].add(padded[:, :margin, :margin])
    interior = interior.at[:, :margin, inner_end:].add(padded[:, :margin, outer_edge:])
    interior = interior.at[:, inner_end:, :margin].add(padded[:, outer_edge:, :margin])
    interior = interior.at[:, inner_end:, inner_end:].add(padded[:, outer_edge:, outer_edge:])
    return interior


def selectors(start_index, width, extent):
    pixel_ramp = lax.iota(jnp.int32, width)
    grid_ramp = lax.iota(jnp.int32, extent)
    wanted = start_index[:, None, None] + pixel_ramp[None, :, None]
    return (wanted == grid_ramp[None, None, :]).astype(jnp.float32)


def shards(object_field, probe_modes, coefficients, offsets, counts, measured):
    margin = PS // 2
    extent = TILE + PS
    cos_part, sin_part = dft_tables(PS)
    coef_now = coefficients[0, 0]
    anchor_all = offsets[0, 0]
    count_here = counts[0, 0]
    photon_all = measured[0, 0]
    for iteration in range(ITERS):
        extended = extended_2(object_field, (("row", 1), ("col", 2)), margin)
        modes_now = probe_modes
        coef_start = coef_now

        def run_block(number, running):
            accumulated, moment_real, moment_imag, moment_power, coef_next = running
            first_slot = number * BLK
            anchors = lax.dynamic_slice_in_dim(anchor_all, first_slot, BLK, 0)
            coef_rows = lax.dynamic_slice_in_dim(coef_start, first_slot, BLK, 0)
            photons = lax.dynamic_slice_in_dim(photon_all, first_slot, BLK, 0)
            in_use = (first_slot + lax.iota(jnp.int32, BLK) < count_here).astype(jnp.float32)
            row_select = selectors(anchors[:, 0], PS, extent)
            col_select = selectors(anchors[:, 1], PS, extent)
            row_cut = jnp.einsum("spe,cef->scpf", row_select, extended, precision=highest)
            patches = jnp.einsum("scpf,sqf->scpq", row_cut, col_select, precision=highest)
            pieces, moments, coef_new = position_terms(
                patches, coef_rows, in_use, photons, modes_now, cos_part, sin_part
            )
            placed_cols = jnp.einsum("scpq,sqf->scpf", pieces, col_select, precision=highest)
            accumulated = accumulated + jnp.einsum(
                "spe,scpf->cef", row_select, placed_cols, precision=highest
            )
            coef_next = lax.dynamic_update_slice_in_dim(coef_next, coef_new, first_slot, 0)
            return (
                accumulated,
                moment_real + moments[0],
                moment_imag + moments[1],
                moment_power + moments[2],
                coef_next,
            )

        empty_moment = jnp.zeros((MODES, PS, PS), jnp.float32)
        start_state = (
            jnp.zeros((3, extent, extent), jnp.float32),
            empty_moment,
            empty_moment,
            empty_moment,
            coef_start,
        )
        final_state = lax.fori_loop(0, PMAX // BLK, run_block, start_state)
        accumulated, moment_real, moment_imag, moment_power, coef_now = final_state
        padded = extended_2(accumulated, (("row", 1), ("col", 2)), margin)
        interior = fold_edges(padded, margin)
        object_field = object_field + interior[0:2] / (interior[2:3] + 1.0)
        totals = lax.psum((moment_real, moment_imag, moment_power), ("row", "col"))
        probe_modes = modes_now + jnp.stack([totals[0], totals[1]], axis=1) / (
            totals[2][:, None] + 1.0
        )
    return (object_field, probe_modes, coef_now[None, None])


def solution(mesh):
    placed = (
        P(None, "row", "col"),
        P(),
        P("row", "col", None, None),
        P("row", "col", None, None),
        P("row", "col"),
        P("row", "col", None, None, None),
    )
    return jax.shard_map(
        shards,
        mesh=mesh,
        in_specs=placed,
        out_specs=(P(None, "row", "col"), P(), P("row", "col", None, None)),
        check_vma=False,
    )
```

profile of v0, /device:TPU:2, one launch (start us, length us, event | category | flops | bytes accessed | tf_op | source)
XLA Modules:
  0.0 695.5 jit_solution(3471767451995187834)
XLA Ops:
  14.6 3.8 collective-permute-start.2
  18.5 4.1 collective-permute-start.3
  29.7 162.3 %while.66 = (s32[]{:T(128)}, f32[3,256,256]{1,2,0:T(8,128)}, f32[8,128,128]{2,0,1:T(8,128)}, f32[8,128,128]{2,0,1:T(8,128)}, f32[8,128,128]{2,0,1:T(8,128)}, /*i...) while((s32[]{:T(128)}, f32[3,256,256]{1,2,0:T(8,128)}, ...), condition=%wide.region_1.2_spmd.clone.clone, body=%wide.region_0.1_spmd.clone.clone.sunk | while | flops 18745724928 | bytes 206108528 | solution.py:179
  98.5 3.7 fusion.692
  102.3 3.6 fusion.693
  118.4 3.8 convolution_add_fusion.22
  150.9 3.1 fusion.687
  178.0 3.7 fusion.692
  181.8 3.6 fusion.693
  201.7 6.3 collective-permute-start.7
  211.6 8.9 %collective-permute-done.6 = f32[3,384,64]{1,2,0:T(8,128)S(1)} collective-permute-done((f32[3,384,64]{1,2,0:T(8,128)S(1)}, f32[3,384,64]{1,2,0:T(8,128)S(1)}, u32[]{:S(2)}, u32[]{:S(2)}) %collective-permute-start.6) | collective-permute-done | bytes 294944 | tf_op jit(solution)/shard_map/ppermute | solution.py:26
  229.6 3.8 collective-permute-start.8
  234.8 5.5 collective-permute-done.9
  242.4 6.0 collective-permute-start.11
  251.4 105.5 %all-reduce.7.cloned.1.call-done = (f32[8,1,128,128]{3,2,1,0:T(8,128)}, f32[8,1,128,128]{3,2,1,0:T(8,128)}, f32[8,128,128]{2,0,1:T(8,128)}) async-done(((f32[8,1,128,128]{3,2,1,0:T(8,128)}, f32[8,1,128,128]{3,2,1,0:T(8,128)}, f32[8,128,128]{2,0,1:T(8,128)}), (f32[8,1,128,128]{3,2,1,0:T(8,128)}, f32[8,1,128,128]{3,2,1,0:T(8,128)}, f32[8,128,128]{2,0,1:T(8,128)})) %all-reduce.7.cloned.1.call-update) | async-done | bytes 1572880 | tf_op jit(solution)/shard_map/psum | solution.py:184
  360.7 161.4 %while.67 = (s32[]{:T(128)}, f32[3,256,256]{1,2,0:T(8,128)}, f32[8,128,128]{2,0,1:T(8,128)}, f32[8,128,128]{2,0,1:T(8,128)}, f32[8,128,128]{2,0,1:T(8,128)}, /*i...) while((s32[]{:T(128)}, f32[3,256,256]{1,2,0:T(8,128)}, ...), condition=%wide.region_7.8_spmd.clone.clone, body=%wide.region_6.7_spmd.clone.clone.sunk | while | flops 18745724928 | bytes 206108528 | solution.py:179
  429.7 3.7 fusion.767
  433.5 3.6 fusion.768
  449.6 3.8 convolution_add_fusion.25
  509.3 3.7 fusion.767
  513.1 3.6 fusion.768
  533.1 4.1 collective-permute-start.15
  541.0 9.7 %collective-permute-done.14 = f32[3,384,64]{1,2,0:T(8,128)} collective-permute-done((f32[3,384,64]{1,2,0:T(8,128)}, f32[3,384,64]{1,2,0:T(8,128)}, u32[]{:S(2)}, u32[]{:S(2)}) %collective-permute-start.14) | collective-permute-done | bytes 294944 | tf_op jit(solution)/shard_map/ppermute | solution.py:26
  565.7 118.9 %all-reduce.5.cloned.1.call-done = (f32[8,1,128,128]{3,2,1,0:T(8,128)}, f32[8,1,128,128]{3,2,1,0:T(8,128)}, f32[8,128,128]{2,0,1:T(8,128)}) async-done(((f32[8,1,128,128]{3,2,1,0:T(8,128)}, f32[8,1,128,128]{3,2,1,0:T(8,128)}, f32[8,128,128]{2,0,1:T(8,128)}), (f32[8,1,128,128]{3,2,1,0:T(8,128)}, f32[8,1,128,128]{3,2,1,0:T(8,128)}, f32[8,128,128]{2,0,1:T(8,128)})) %all-reduce.5.cloned.1.call-update) | async-done | bytes 1572880 | tf_op jit(solution)/shard_map/psum | solution.py:184
  (440 shorter events, 350.2 us)
Async XLA Ops:
  7.2 349.7 %all-reduce.7.cloned.1.call-start = ((), (), s32[]{:S(2)}) async-start(), calls=%async_computation.1 | async-start | bytes 3145728 | tf_op jit(solution)/shard_map/psum | solution.py:184
  8.1 6.3 collective-permute-start.1
  9.5 5.0 collective-permute-start
  14.6 12.8 %collective-permute-start.2 = (f32[2,256,64]{2,1,0:T(8,128)S(1)}, f32[2,256,64]{2,1,0:T(8,128)S(1)}, u32[]{:S(2)}, u32[]{:S(2)}) collective-permute-start(f32[2,256,64]{2,1,0:T(8,128)S(1)} %get-tuple-element.1304), channel_id=1, source_target_pairs={{0,1},{1,2},{2,3},{3,4},{4,5},{5,6},{6,7},{7,8},{8,9},{9,10},{10,1... | collective-permute-start | bytes 393224 | tf_op jit(solution)/shard_map/ppermute | solution.py:26
  18.5 10.9 %collective-permute-start.3 = (f32[2,256,64]{2,1,0:T(8,128)S(1)}, f32[2,256,64]{2,1,0:T(8,128)S(1)}, u32[]{:S(2)}, u32[]{:S(2)}) collective-permute-start(f32[2,256,64]{2,1,0:T(8,128)S(1)} %get-tuple-element.1305), channel_id=1, source_target_pairs={{1,0},{2,1},{3,2},{4,3},{5,4},{6,5},{7,6},{8,7},{9,8},{10,9},{11,1... | collective-permute-start | bytes 393224 | tf_op jit(solution)/shard_map/ppermute | solution.py:29
  194.5 6.9 collective-permute-start.5
  195.8 5.6 collective-permute-start.4
  201.3 483.4 %all-reduce.5.cloned.1.call-start = ((), (), s32[]{:S(2)}) async-start(), calls=%async_computation | async-start | bytes 3145728 | tf_op jit(solution)/shard_map/psum | solution.py:184
  201.7 18.9 %collective-permute-start.7 = (f32[3,384,64]{1,2,0:T(8,128)S(1)}, f32[3,384,64]{1,2,0:T(8,128)S(1)}, u32[]{:S(2)}, u32[]{:S(2)}) collective-permute-start(f32[3,384,64]{1,2,0:T(8,128)S(1)} %get-tuple-element.1296), channel_id=1, source_target_pairs={{1,0},{2,1},{3,2},{4,3},{5,4},{6,5},{7,6},{8,7},{9,8},{10,9},{11,1... | collective-permute-start | bytes 884744 | tf_op jit(solution)/shard_map/ppermute | solution.py:29
  207.9 12.6 %collective-permute-start.6 = (f32[3,384,64]{1,2,0:T(8,128)S(1)}, f32[3,384,64]{1,2,0:T(8,128)S(1)}, u32[]{:S(2)}, u32[]{:S(2)}) collective-permute-start(f32[3,384,64]{1,2,0:T(8,128)S(1)} %get-tuple-element.1297), channel_id=1, source_target_pairs={{0,1},{1,2},{2,3},{3,4},{4,5},{5,6},{6,7},{7,8},{8,9},{9,10},{10,1... | collective-permute-start | bytes 884744 | tf_op jit(solution)/shard_map/ppermute | solution.py:26
  229.5 128.6 %copy-start.39 = (f32[8,2,128,128]{3,2,1,0:T(8,128)S(1)}, f32[8,2,128,128]{3,2,1,0:T(8,128)}, u32[]{:S(2)}) copy-start(f32[8,2,128,128]{3,2,1,0:T(8,128)} %param.43) | copy-start | bytes 3145732
  229.6 5.2 collective-permute-start.8
  233.5 6.8 collective-permute-start.9
  240.5 9.1 %collective-permute-start.10 = (f32[2,256,64]{1,2,0:T(8,128)S(1)}, f32[2,256,64]{1,2,0:T(8,128)S(1)}, u32[]{:S(2)}, u32[]{:S(2)}) collective-permute-start(f32[2,256,64]{1,2,0:T(8,128)S(1)} %get-tuple-element.1302), channel_id=1, source_target_pairs={{0,1},{1,2},{2,3},{3,4},{4,5},{5,6},{6,7},{7,8},{8,9},{9,10},{10,1... | collective-permute-start | bytes 393224 | tf_op jit(solution)/shard_map/ppermute | solution.py:26
  242.4 8.6 %collective-permute-start.11 = (f32[2,256,64]{1,2,0:T(8,128)S(1)}, f32[2,256,64]{1,2,0:T(8,128)S(1)}, u32[]{:S(2)}, u32[]{:S(2)}) collective-permute-start(f32[2,256,64]{1,2,0:T(8,128)S(1)} %get-tuple-element.1303), channel_id=1, source_target_pairs={{1,0},{2,1},{3,2},{4,3},{5,4},{6,5},{7,6},{8,7},{9,8},{10,9},{11,1... | collective-permute-start | bytes 393224 | tf_op jit(solution)/shard_map/ppermute | solution.py:29
  523.6 8.4 %collective-permute-start.13 = (f32[3,64,256]{1,2,0:T(8,128)S(1)}, f32[3,64,256]{1,2,0:T(8,128)S(1)}, u32[]{:S(2)}, u32[]{:S(2)}) collective-permute-start(f32[3,64,256]{1,2,0:T(8,128)S(1)} %get-tuple-element.1298), channel_id=1, source_target_pairs={{16,0},{32,16},{48,32},{64,48},{80,64},{96,80},{112,96},{17,1},{33... | collective-permute-start | bytes 589832 | tf_op jit(solution)/shard_map/ppermute | solution.py:29
  524.9 7.1 %collective-permute-start.12 = (f32[3,64,256]{1,2,0:T(8,128)S(1)}, f32[3,64,256]{1,2,0:T(8,128)S(1)}, u32[]{:S(2)}, u32[]{:S(2)}) collective-permute-start(f32[3,64,256]{1,2,0:T(8,128)S(1)} %get-tuple-element.1299), channel_id=1, source_target_pairs={{0,16},{16,32},{32,48},{48,64},{64,80},{80,96},{96,112},{1,17},{17... | collective-permute-start | bytes 589832 | tf_op jit(solution)/shard_map/ppermute | solution.py:26
  532.0 32.9 %copy-start.44 = (f32[2,128,128]{1,2,0:T(8,128)S(1)}, f32[2,128,128]{1,2,0:T(8,128)}, u32[]{:S(2)}) copy-start(f32[2,128,128]{1,2,0:T(8,128)} %copy-done.43) | copy-start | bytes 393220
  533.1 18.5 %collective-permute-start.15 = (f32[3,384,64]{1,2,0:T(8,128)}, f32[3,384,64]{1,2,0:T(8,128)}, u32[]{:S(2)}, u32[]{:S(2)}) collective-permute-start(f32[3,384,64]{1,2,0:T(8,128)} %get-tuple-element.1294), channel_id=1, source_target_pairs={{1,0},{2,1},{3,2},{4,3},{5,4},{6,5},{7,6},{8,7},{9,8},{10,9},{11,1... | collective-permute-start | bytes 884744 | tf_op jit(solution)/shard_map/ppermute | solution.py:29
  537.2 13.4 %collective-permute-start.14 = (f32[3,384,64]{1,2,0:T(8,128)}, f32[3,384,64]{1,2,0:T(8,128)}, u32[]{:S(2)}, u32[]{:S(2)}) collective-permute-start(f32[3,384,64]{1,2,0:T(8,128)} %get-tuple-element.1295), channel_id=1, source_target_pairs={{0,1},{1,2},{2,3},{3,4},{4,5},{5,6},{6,7},{7,8},{8,9},{9,10},{10,1... | collective-permute-start | bytes 884744 | tf_op jit(solution)/shard_map/ppermute | solution.py:26
  539.7 146.1 %copy-start.40 = (f32[8,2,128,128]{3,2,1,0:T(8,128)S(1)}, f32[8,2,128,128]{3,2,1,0:T(8,128)}, u32[]{:S(2)}) copy-start(f32[8,2,128,128]{3,2,1,0:T(8,128)} %param.43) | copy-start | bytes 3145732
  539.8 146.1 %copy-start.42 = (f32[8,128,128]{2,1,0:T(8,128)S(1)}, f32[8,128,128]{2,1,0:T(8,128)}, u32[]{:S(2)}) copy-start(f32[8,128,128]{2,1,0:T(8,128)} %copy-done.41) | copy-start | bytes 1572868
  539.8 146.1 %copy-start.46 = (f32[8,1,128,128]{3,2,1,0:T(8,128)S(1)}, f32[8,1,128,128]{3,2,1,0:T(8,128)}, u32[]{:S(2)}) copy-start(f32[8,1,128,128]{3,2,1,0:T(8,128)} %get-tuple-element.1259) | copy-start | bytes 1572868
  539.8 146.1 %copy-start.47 = (f32[8,1,128,128]{3,2,1,0:T(8,128)S(1)}, f32[8,1,128,128]{3,2,1,0:T(8,128)}, u32[]{:S(2)}) copy-start(f32[8,1,128,128]{3,2,1,0:T(8,128)} %get-tuple-element.1260) | copy-start | bytes 1572868
  (87 other events, 463.0 us)
Sparse Core Ops, SparseCore 0:
  201.4 155.4 all-reduce.6
  532.1 152.5 all-reduce.4
where the time goes:
time: 701 us; the launch traced here: 696 us
  waiting for transfers between devices  256 us (37%)
  matrix products  249 us (36%)
  local copies, waits for them, and re-layouts  75.5 us (11%)
  starting transfers between devices  48.3 us (7%)
  other arithmetic  38.4 us (5%)
  between operations  15.2 us (2%)
  loops' own time  13.2 us (2%)
    psum x2, waiting for transfers between devices, shards(): totals = lax.psum((moment_real, moment_imag, moment_power), ('row', 'col'))  224 us
    ppermute x8, starting transfers between devices, extended_2(): lax.ppermute(lax.slice_in_dim(block, 0, width, axis=dim), axis, backward)  25.7 us
    dot_general x8, matrix products, right_apply(): jnp.einsum('nab,bc->nac', imag_part, cos_part, precision=highest)  22.7 us
    ppermute x8, starting transfers between devices, extended_2(): lax.ppermute(lax.slice_in_dim(block, block.shape[dim] - width, None, axis...  22.6 us
    ppermute x8, waiting for transfers between devices, extended_2(): lax.ppermute(lax.slice_in_dim(block, block.shape[dim] - width, None, axis...  22.3 us
    dot_general x8, matrix products, left_apply(): jnp.einsum('ab,nbc->nac', sin_part, real_part, precision=highest)  21.5 us
    dot_general x8, matrix products, right_apply(): jnp.einsum('nab,bc->nac', real_part, sin_part, precision=highest)  19.2 us
    dot_general x8, matrix products, right_apply(): jnp.einsum('nab,bc->nac', real_part, cos_part, precision=highest)  18.1 us
  transfers between devices with their start and end apart: 18, of which 9 were waited for; matrix products, arithmetic and copies ran while one was open for 6% of the time, Pallas kernels for 0%

commit v1 on v0

v1 whole, which is shorter than its diff:
```python
import functools
import math

import jax
import jax.numpy as jnp
import numpy as np
from jax import lax
from jax.experimental import pallas as pl
from jax.experimental.pallas import tpu as pltpu
from jax.sharding import PartitionSpec as P

PS = 128
MODES = 8
TILE = 128
PMAX = 32
ITERS = 2
EXT = TILE + PS
F32 = jnp.float32
BF16 = jnp.bfloat16
DEVICES = 128


def split(x):
    hi = x.astype(BF16)
    lo = (x - hi.astype(F32)).astype(BF16)
    return hi, lo


def triple(x, axis):
    hi, lo = split(x)
    return jnp.concatenate([hi, lo, hi], axis=axis)


def dft_constants():
    ramp = np.arange(PS)
    angles = (ramp[:, None] * ramp[None, :] % PS) * (2.0 * math.pi / PS)
    cos = np.cos(angles) / math.sqrt(PS)
    sin = -np.sin(angles) / math.sqrt(PS)
    ahead = np.block([[cos, sin], [-sin, cos]])
    back = np.block([[cos, -sin], [sin, cos]])

    def parts(table):
        table = table.astype(np.float32)
        hi = table.astype(jnp.bfloat16)
        lo = (table - hi.astype(np.float32)).astype(jnp.bfloat16)
        return hi, lo

    def tall(table):
        hi, lo = parts(table)
        return np.concatenate([hi, hi, lo], axis=0)

    def wide(table):
        hi, lo = parts(table)
        return np.concatenate([hi, hi, lo], axis=1)

    return tall(ahead), wide(back), wide(ahead), tall(back)


def dot(a, b):
    return jnp.dot(a, b, preferred_element_type=F32)


def patch_kernel(offs, ext, coef, patches, powers, moment, pw):
    lane = lax.broadcasted_iota(jnp.int32, (PS, PS), 1)

    def cut(p, _):
        top = offs[p, 0]
        left = offs[p, 1]
        turn = (PS - left) & (PS - 1)
        inside = lane < PS - left
        total = None
        for c in range(2):
            a = pltpu.roll(ext[c, 0, pl.ds(top, PS), :], turn, 1)
            b = pltpu.roll(ext[c, 1, pl.ds(top, PS), :], turn, 1)
            patch = jnp.where(inside, a, b)
            patches[p, c] = patch
            total = patch * patch if total is None else total + patch * patch
        pw[pl.ds(p, PS, stride=PMAX), :] = total
        return 0

    lax.fori_loop(0, PMAX, cut, 0)
    powers[...] = pw[...]
    square = coef[...] * coef[...]
    hi, lo = split(square.T)
    zero = jnp.zeros_like(hi)
    left = jnp.concatenate(
        [jnp.concatenate([hi, hi], axis=1), jnp.concatenate([lo, zero], axis=1)], axis=0
    )

    def rows(y, _):
        pair = jnp.concatenate(
            [pw[pl.ds(2 * y * PMAX, PMAX), :], pw[pl.ds((2 * y + 1) * PMAX, PMAX), :]], axis=1
        )
        h, l = split(pair)
        out = dot(left, jnp.concatenate([h, l], axis=0))
        out = out[:MODES] + out[MODES:]
        moment[2 * y] = out[:, :PS]
        moment[2 * y + 1] = out[:, PS:]
        return 0

    lax.fori_loop(0, PS // 2, rows, 0, unroll=4)


def wave_kernel(
    offs, patches, photons, modes, coef, ahead_t, back_w, ahead_w, back_t,
    acc, cross_r, cross_i, moment, probe_r, probe_i, field, wave,
):
    step = pl.program_id(0)
    lane = lax.broadcasted_iota(jnp.int32, (PS, PS), 1)

    @pl.when(step == 0)
    def _():
        acc[...] = jnp.zeros_like(acc)
        left = triple(coef[...], 1)

        def rows(y, _):
            m = modes[y]
            h = m.astype(BF16).astype(F32)
            right = jnp.concatenate([h, h, m - h], axis=0).astype(BF16)
            out = dot(left, right)
            start = pl.multiple_of(y * PMAX, PMAX)
            probe_r[pl.ds(start, PMAX), :] = out[:, :PS]
            probe_i[pl.ds(start, PMAX), :] = out[:, PS:]
            return 0

        lax.fori_loop(0, PS, rows, 0, unroll=8)

    for q in range(2):
        p = 2 * step + q
        pr = probe_r[pl.ds(p, PS, stride=PMAX), :]
        pi = probe_i[pl.ds(p, PS, stride=PMAX), :]
        obj_r = patches[q, 0]
        obj_i = patches[q, 1]
        rows = slice(q * PS, (q + 1) * PS)
        wave[rows, :PS] = pr * obj_r - pi * obj_i
        wave[rows, PS:] = pr * obj_i + pi * obj_r

    def regroup(x):
        top = jnp.concatenate([x[:PS, :PS], x[PS:, :PS]], axis=1)
        low = jnp.concatenate([x[:PS, PS:], x[PS:, PS:]], axis=1)
        return jnp.concatenate([top, low], axis=0)

    out = dot(triple(wave[...], 1), ahead_t[...])
    far = dot(back_w[...], triple(regroup(out), 0))
    count = jnp.concatenate([photons[0], photons[1]], axis=1).astype(F32)
    far_r = far[:PS]
    far_i = far[PS:]
    size = jnp.maximum(far_r * far_r + far_i * far_i, 0.25)
    scale = count * lax.rsqrt(jnp.maximum(count * size, 0.0625)) * 0.03125
    fixed = jnp.concatenate([far_r * scale, far_i * scale], axis=0)
    out = dot(ahead_w[...], triple(fixed, 0))
    field[...] = dot(triple(regroup(out), 1), back_t[...]) - wave[...]

    for q in range(2):
        p = 2 * step + q
        top = offs[p, 0]
        left = offs[p, 1]
        turn = left & (PS - 1)
        inside = lane >= left
        rows = slice(q * PS, (q + 1) * PS)
        diff_r = field[rows, :PS]
        diff_i = field[rows, PS:]
        obj_r = patches[q, 0]
        obj_i = patches[q, 1]
        cross_r[pl.ds(p, PS, stride=PMAX), :] = obj_r * diff_r + obj_i * diff_i
        cross_i[pl.ds(p, PS, stride=PMAX), :] = obj_r * diff_i - obj_i * diff_r
        pr = probe_r[pl.ds(p, PS, stride=PMAX), :]
        pi = probe_i[pl.ds(p, PS, stride=PMAX), :]
        pieces = (
            pr * diff_r + pi * diff_i,
            pr * diff_i - pi * diff_r,
            pr * pr + pi * pi,
        )
        for c in range(3):
            turned = pltpu.roll(pieces[c], turn, 1)
            near = jnp.where(inside, turned, 0.0)
            acc[c, 0, pl.ds(top, PS), :] += near
            acc[c, 1, pl.ds(top, PS), :] += turned - near

    @pl.when(step == PMAX // 2 - 1)
    def _():
        hi, lo = split(coef[...].T)
        zero = jnp.zeros_like(hi)
        left = jnp.concatenate(
            [jnp.concatenate([hi, hi], axis=1), jnp.concatenate([lo, zero], axis=1)], axis=0
        )

        def rows(y, _):
            start = pl.multiple_of(y * PMAX, PMAX)
            pair = jnp.concatenate(
                [cross_r[pl.ds(start, PMAX), :], cross_i[pl.ds(start, PMAX), :]], axis=1
            )
            h, l = split(pair)
            out = dot(left, jnp.concatenate([h, l], axis=0))
            moment[y] = out[:MODES] + out[MODES:]
            return 0

        lax.fori_loop(0, PS, rows, 0, unroll=8)


CHUNK = 16


def coef_kernel(cross_r, cross_i, powers, modes, coef, out, num, den):
    step = pl.program_id(0)

    @pl.when(step == 0)
    def _():
        num[...] = jnp.zeros_like(num)
        den[...] = jnp.zeros_like(den)

    dims = (((1,), (1,)), ((), ()))

    def wide_dot(a, b):
        return lax.dot_general(a, b, dims, preferred_element_type=F32)

    top = jnp.zeros((PMAX, MODES), F32)
    low = jnp.zeros((PMAX, MODES), F32)
    for y in range(CHUNK):
        rows = slice(y * PMAX, (y + 1) * PMAX)
        cross = jnp.concatenate([cross_r[rows, :], cross_i[rows, :]], axis=1)
        m = modes[y]
        power = m[:, :PS] * m[:, :PS] + m[:, PS:] * m[:, PS:]
        h, l = split(m)
        top += wide_dot(triple(cross, 1), jnp.concatenate([h, h, l], axis=1))
        h, l = split(power)
        low += wide_dot(triple(powers[rows, :], 1), jnp.concatenate([h, h, l], axis=1))
    num[...] += top
    den[...] += low

    @pl.when(step == PS // CHUNK - 1)
    def _():
        out[...] = coef[...] + num[...] / (den[...] + 1.0)


SMEM = pl.BlockSpec(memory_space=pltpu.SMEM)
VMEM = pl.BlockSpec(memory_space=pltpu.VMEM)


def cut_patches(offs, ext, coef):
    return pl.pallas_call(
        patch_kernel,
        out_shape=(
            jax.ShapeDtypeStruct((PMAX, 2, PS, PS), F32),
            jax.ShapeDtypeStruct((PS * PMAX, PS), F32),
            jax.ShapeDtypeStruct((PS, MODES, PS), F32),
        ),
        in_specs=[SMEM, VMEM, VMEM],
        out_specs=(VMEM, VMEM, VMEM),
        scratch_shapes=[pltpu.VMEM((PS * PMAX, PS), F32)],
        compiler_params=pltpu.CompilerParams(vmem_limit_bytes=24 << 20),
        name="cut",
    )(offs, ext, coef)


def waves(offs, patches, photons, modes, coef, tables):
    whole = lambda *shape: pl.BlockSpec(shape, lambda i: (0,) * len(shape))
    table_specs = [whole(*t.shape) for t in tables]
    return pl.pallas_call(
        wave_kernel,
        grid=(PMAX // 2,),
        out_shape=(
            jax.ShapeDtypeStruct((3, 2, EXT, PS), F32),
            jax.ShapeDtypeStruct((PS * PMAX, PS), F32),
            jax.ShapeDtypeStruct((PS * PMAX, PS), F32),
            jax.ShapeDtypeStruct((PS, MODES, 2 * PS), F32),
        ),
        in_specs=[
            SMEM,
            pl.BlockSpec((2, 2, PS, PS), lambda i: (i, 0, 0, 0)),
            pl.BlockSpec((2, PS, PS), lambda i: (i, 0, 0)),
            whole(PS, MODES, 2 * PS),
            whole(PMAX, MODES),
            *table_specs,
        ],
        out_specs=(
            whole(3, 2, EXT, PS),
            whole(PS * PMAX, PS),
            whole(PS * PMAX, PS),
            whole(PS, MODES, 2 * PS),
        ),
        scratch_shapes=[
            pltpu.VMEM((PS * PMAX, PS), F32),
            pltpu.VMEM((PS * PMAX, PS), F32),
            pltpu.VMEM((2 * PS, 2 * PS), F32),
            pltpu.VMEM((2 * PS, 2 * PS), F32),
        ],
        compiler_params=pltpu.CompilerParams(
            dimension_semantics=("arbitrary",), vmem_limit_bytes=40 << 20
        ),
        name="waves",
    )(offs, patches, photons, modes, coef, *tables)


def new_coefficients(cross_r, cross_i, powers, modes, coef):
    rows = pl.BlockSpec((CHUNK * PMAX, PS), lambda i: (i, 0))
    whole = pl.BlockSpec((PMAX, MODES), lambda i: (0, 0))
    return pl.pallas_call(
        coef_kernel,
        grid=(PS // CHUNK,),
        out_shape=jax.ShapeDtypeStruct((PMAX, MODES), F32),
        in_specs=[
            rows,
            rows,
            rows,
            pl.BlockSpec((CHUNK, MODES, 2 * PS), lambda i: (i, 0, 0)),
            whole,
        ],
        out_specs=whole,
        scratch_shapes=[pltpu.VMEM((PMAX, MODES), F32)] * 2,
        compiler_params=pltpu.CompilerParams(
            dimension_semantics=("arbitrary",), vmem_limit_bytes=16 << 20
        ),
        name="coefs",
    )(cross_r, cross_i, powers, modes, coef)


def swap_sides(low_part, high_part, axis):
    count = lax.axis_size(axis)
    up = [(i, i + 1) for i in range(count - 1)]
    down = [(i + 1, i) for i in range(count - 1)]
    from_below = lax.ppermute(high_part, axis, up)
    from_above = lax.ppermute(low_part, axis, down)
    return from_below, from_above


def extend(block):
    margin = PS // 2
    low, high = swap_sides(block[:, :margin], block[:, -margin:], "row")
    block = jnp.concatenate([low, block, high], axis=1)
    low, high = swap_sides(block[:, :, :margin], block[:, :, -margin:], "col")
    return jnp.concatenate([low, block, high], axis=2)


def fold(acc):
    margin = PS // 2
    full = jnp.concatenate([acc[:, 0], acc[:, 1]], axis=2)
    low, high = swap_sides(full[:, :margin], full[:, -margin:], "row")
    mid = full[:, margin:-margin]
    mid = jnp.concatenate([mid[:, :margin] + low, mid[:, margin:] + high], axis=1)
    low, high = swap_sides(mid[:, :, :margin], mid[:, :, -margin:], "col")
    mid = mid[:, :, margin:-margin]
    return jnp.concatenate([mid[:, :, :margin] + low, mid[:, :, margin:] + high], axis=2)


def shards(object_field, probe_modes, coefficients, offsets, counts, measured):
    tables = tuple(jnp.asarray(t) for t in dft_constants())
    offs = offsets[0, 0]
    photons = measured[0, 0]
    coef = coefficients[0, 0]
    live = (lax.iota(jnp.int32, PMAX) < counts[0, 0]).astype(F32)[:, None]
    me = lax.axis_index("row") * lax.axis_size("col") + lax.axis_index("col")
    modes = probe_modes.transpose(2, 0, 1, 3).reshape(PS, MODES, 2 * PS)
    for iteration in range(ITERS):
        ext = extend(object_field)
        ext = jnp.stack([ext[:, :, :PS], ext[:, :, PS:]], axis=1)
        used = coef * live
        patches, powers, power_moment = cut_patches(offs, ext, used)
        acc, cross_r, cross_i, moment = waves(offs, patches, photons, modes, used, tables)
        sent = jnp.concatenate([moment, power_moment], axis=2)
        got = lax.all_to_all(sent, ("row", "col"), 0, 0, tiled=True)
        total = jnp.sum(got, axis=0)
        power = total[:, 2 * PS:] + 1.0
        mine = lax.dynamic_index_in_dim(modes, me, 0, keepdims=False)
        mine = mine + total[:, : 2 * PS] / jnp.concatenate([power, power], axis=1)
        coef = new_coefficients(cross_r, cross_i, powers, modes, coef)
        copies = jnp.broadcast_to(mine[None], (DEVICES, MODES, 2 * PS))
        modes = lax.all_to_all(copies, ("row", "col"), 0, 0, tiled=True)
        interior = fold(acc)
        object_field = object_field + interior[0:2] / (interior[2:3] + 1.0)
    probe_modes = modes.reshape(PS, MODES, 2, PS).transpose(1, 2, 0, 3)
    return (object_field, probe_modes, coef[None, None])


def solution(mesh):
    placed = (
        P(None, "row", "col"),
        P(),
        P("row", "col", None, None),
        P("row", "col", None, None),
        P("row", "col"),
        P("row", "col", None, None, None),
    )
    return jax.shard_map(
        shards,
        mesh=mesh,
        in_specs=placed,
        out_specs=(P(None, "row", "col"), P(), P("row", "col", None, None)),
        check_vma=False,
    )
```

time: 701 us -> 295 us (0.42)
  matrix products: 249 us -> 0 us
  waiting for transfers between devices: 256 us -> 46 us
  Pallas kernels: 0 us -> 103 us
  starting transfers between devices: 48.3 us -> 96.1 us
  local copies, waits for them, and re-layouts: 75.5 us -> 33.4 us
  other arithmetic: 38.4 us -> 13.3 us
  between operations: 15.2 us -> 1.95 us
  loops' own time: 13.2 us -> 0 us
    dot_general x108 -> x0, matrix products: 249 us -> none  [the longest x8 22.7 us: right_apply(): jnp.einsum('nab,bc->nac', imag_part, cos_part, precision=highest)]
    psum x2 -> x0, waiting for transfers between devices: 224 us -> none  [shards(): totals = lax.psum((moment_real, moment_imag, moment_power), ('row', 'col'))]
    pallas_call x0 -> x6, Pallas kernels: none -> 103 us  [the longest x2 76.9 us: waves(): pl.pallas_call(wave_kernel, grid=(PMAX // 2,), out_shape=(jax.ShapeDtypeS...]
    all_to_all x0 -> x4, starting transfers between devices: none -> 48.5 us  [the longest x2 24.9 us: shards(): modes = lax.all_to_all(copies, ('row', 'col'), 0, 0, tiled=True)]
    unnamed x44 -> x65, local copies, waits for them, and re-layouts: 4.58 us -> 27.4 us
    all_to_all x0 -> x4, waiting for transfers between devices: none -> 17.8 us  [the longest x2 17.8 us: shards(): got = lax.all_to_all(sent, ('row', 'col'), 0, 0, tiled=True)]
    scatter-add x12 -> x0, local copies, waits for them, and re-layouts: 16.1 us -> none  [the longest x2 4.02 us: fold_edges(): interior.at[:, :margin, inner_end:].add(padded[:, :margin, outer_edge:])]
    sub x8 -> x0, local copies, waits for them, and re-layouts: 16.1 us -> none  [the longest x4 10.5 us: left_apply(): jnp.einsum('ab,nbc->nac', cos_part, real_part, precision=highest)]
  transfers between devices with their start and end apart: 18 -> 20, of which waited for: 9 -> 10; matrix products, arithmetic and copies ran while one was open for 6% -> 5% of each run, Pallas kernels for 0% -> 6%
where the time goes in v1:
time: 295 us; the launch traced here: 294 us
  Pallas kernels  103 us (35%)
  starting transfers between devices  96.1 us (33%)
  waiting for transfers between devices  46 us (16%)
  local copies, waits for them, and re-layouts  33.4 us (11%)
  other arithmetic  13.3 us (5%)
    pallas_call x2, Pallas kernels, waves(): pl.pallas_call(wave_kernel, grid=(PMAX // 2,), out_shape=(jax.ShapeDtypeS...  76.9 us
    unnamed x65, local copies, waits for them, and re-layouts  27.4 us
    all_to_all x2, starting transfers between devices, shards(): modes = lax.all_to_all(copies, ('row', 'col'), 0, 0, tiled=True)  24.9 us
    ppermute x8, starting transfers between devices, swap_sides(): from_above = lax.ppermute(low_part, axis, down)  24.3 us
    all_to_all x2, starting transfers between devices, shards(): got = lax.all_to_all(sent, ('row', 'col'), 0, 0, tiled=True)  23.6 us
    ppermute x8, starting transfers between devices, swap_sides(): from_below = lax.ppermute(high_part, axis, up)  23.2 us
    pallas_call x2, Pallas kernels, cut_patches(): pl.pallas_call(patch_kernel, out_shape=(jax.ShapeDtypeStruct((PMAX, 2, PS...  18.5 us
    all_to_all x2, waiting for transfers between devices, shards(): got = lax.all_to_all(sent, ('row', 'col'), 0, 0, tiled=True)  17.8 us
  transfers between devices with their start and end apart: 20, of which 10 were waited for; matrix products, arithmetic and copies ran while one was open for 5% of the time, Pallas kernels for 6%

profile of v1, /device:TPU:2, one launch (start us, length us, event | category | flops | bytes accessed | tf_op | source)
XLA Modules:
  0.0 293.6 jit_solution(5244420495111181191)
XLA Ops:
  2.9 3.0 %collective-permute-start = (f32[2,64,128]{2,1,0:T(8,128)S(1)}, f32[2,64,128]{2,1,0:T(8,128)S(1)}, u32[]{:S(2)}, u32[]{:S(2)}) collective-permute-start(f32[2,64,128]{2,1,0:T(8,128)S(1)} %get-tuple-element.66), channel_id=1, source_target_pairs={{0,16},{16,32},{32,48},{48,64},{64,80},{80,96},{96,112},{1,17},{17... | collective-permute-start | bytes 196616 | tf_op jit(solution)/shard_map/ppermute | solution.py:322
  10.2 4.1 %collective-permute-start.2 = (f32[2,256,64]{2,1,0:T(8,128)S(1)}, f32[2,256,64]{2,1,0:T(8,128)S(1)}, u32[]{:S(2)}, u32[]{:S(2)}) collective-permute-start(f32[2,256,64]{2,1,0:T(8,128)S(1)} %get-tuple-element.61), channel_id=1, source_target_pairs={{0,1},{1,2},{2,3},{3,4},{4,5},{5,6},{6,7},{7,8},{8,9},{9,10},{10,1... | collective-permute-start | bytes 393224 | tf_op jit(solution)/shard_map/ppermute | solution.py:322
  14.3 4.1 %collective-permute-start.3 = (f32[2,256,64]{2,1,0:T(8,128)S(1)}, f32[2,256,64]{2,1,0:T(8,128)S(1)}, u32[]{:S(2)}, u32[]{:S(2)}) collective-permute-start(f32[2,256,64]{2,1,0:T(8,128)S(1)} %get-tuple-element.62), channel_id=1, source_target_pairs={{1,0},{2,1},{3,2},{4,3},{5,4},{6,5},{7,6},{8,7},{9,8},{10,9},{11,1... | collective-permute-start | bytes 393224 | tf_op jit(solution)/shard_map/ppermute | solution.py:323
  18.5 4.7 %collective-permute-done.2 = f32[2,256,64]{2,1,0:T(8,128)S(1)} collective-permute-done((f32[2,256,64]{2,1,0:T(8,128)S(1)}, f32[2,256,64]{2,1,0:T(8,128)S(1)}, u32[]{:S(2)}, u32[]{:S(2)}) %collective-permute-start.2) | collective-permute-done | bytes 131104 | tf_op jit(solution)/shard_map/ppermute | solution.py:322
  25.6 9.2 %cut.2 = (f32[32,2,128,128]{3,2,1,0:T(8,128)S(1)}, f32[4096,128]{1,0:T(8,128)S(1)}, f32[128,8,128]{2,1,0:T(8,128)S(1)}) custom-call(s32[32,2]{1,0:T(8,128)S(1)} %copy.29.offs, f32[2,2,256,128]{3,2,1,0:T(8,128)S(1)} %pad_maximum_fusion.2.ext, f32[32,8]{1,0:T(8,128)S(1)} %broadcast_multiply_fusion.1.coef), custom_call_target="tpu_custom_call" | custom-call | tf_op jit(solution)/shard_map/cut/pallas_call | solution.py:241
  38.2 38.4 %waves.2 = (f32[3,2,256,128]{3,2,1,0:T(8,128)S(1)}, f32[4096,128]{1,0:T(8,128)S(1)}, f32[4096,128]{1,0:T(8,128)S(1)}, f32[128,8,256]{2,1,0:T(8,128)S(1)}) custom-call(s32[32,2]{1,0:T(8,128)S(1)} %copy.29.offs, f32[32,2,128,128]{3,2,1,0:T(8,128)} %copy-done.3, s32[32,128,128]{2,1,0:T(8,128)S(1)} %bitcast.43, f32[128,8,256]{2,1,0:T(8,128)S(1)} %bitcast.40, ...), custom_call_target="tpu_custom_call" | custom-call | tf_op jit(solution)/shard_map/waves/pallas_call | solution.py:259
  81.5 11.2 %all-to-all-start = ((f32[128,8,384]{2,1,0:T(8,128)}), f32[128,8,384]{2,1,0:T(8,128)}, u32[]{:S(2)}, u32[]{:S(2)}) async-start(f32[128,8,384]{2,1,0:T(8,128)} %pad_maximum_fusion), calls=%async_computation | async-start | bytes 3145728 | tf_op jit(solution)/shard_map/all_to_all | solution.py:361
  94.0 3.0 %collective-permute-start.4 = (f32[3,64,256]{2,1,0:T(8,128)S(1)}, f32[3,64,256]{2,1,0:T(8,128)S(1)}, u32[]{:S(2)}, u32[]{:S(2)}) collective-permute-start(f32[3,64,256]{2,1,0:T(8,128)S(1)} %get-tuple-element.44), channel_id=1, source_target_pairs={{0,16},{16,32},{32,48},{48,64},{64,80},{80,96},{96,112},{1,17},{17... | collective-permute-start | bytes 589832 | tf_op jit(solution)/shard_map/ppermute | solution.py:322
  98.3 5.2 %collective-permute-start.7 = (f32[3,128,64]{2,1,0:T(8,128)S(1)}, f32[3,128,64]{2,1,0:T(8,128)S(1)}, u32[]{:S(2)}, u32[]{:S(2)}) collective-permute-start(f32[3,128,64]{2,1,0:T(8,128)S(1)} %get-tuple-element.53), channel_id=1, source_target_pairs={{1,0},{2,1},{3,2},{4,3},{5,4},{6,5},{7,6},{8,7},{9,8},{10,9},{11,1... | collective-permute-start | bytes 294920 | tf_op jit(solution)/shard_map/ppermute | solution.py:323
  105.5 8.3 %collective-permute-done.7 = f32[3,128,64]{2,1,0:T(8,128)S(1)} collective-permute-done((f32[3,128,64]{2,1,0:T(8,128)S(1)}, f32[3,128,64]{2,1,0:T(8,128)S(1)}, u32[]{:S(2)}, u32[]{:S(2)}) %collective-permute-start.7) | collective-permute-done | bytes 98336 | tf_op jit(solution)/shard_map/ppermute | solution.py:323
  113.8 2.8 collective-permute-done.6
  120.5 19.0 %all-to-all-start.1 = ((f32[128,8,256]{2,1,0:T(8,128)}), f32[128,8,256]{2,1,0:T(8,128)S(1)}, u32[]{:S(2)}, u32[]{:S(2)}) async-start(f32[128,8,256]{2,1,0:T(8,128)} %broadcast_in_dim.6), calls=%async_computation.1 | async-start | bytes 2097152 | tf_op jit(solution)/shard_map/all_to_all | solution.py:368
  147.6 3.8 %coefs.2.coef = f32[32,8]{1,0:T(8,128)S(1)} custom-call(f32[4096,128]{1,0:T(8,128)S(1)} %copy-done.7, f32[4096,128]{1,0:T(8,128)S(1)} %copy-done.9, f32[4096,128]{1,0:T(8,128)S(1)} %copy-done.5, f32[128,8,256]{2,1,0:T(8,128)S(1)} %bitcast.42, f32[32,8]{1,0:T(8,128)S(1)} %bitcast.45), custom_call_target="tpu_custom_call" | custom-call | tf_op jit(solution)/shard_map/coefs/pallas_call | solution.py:298
  151.6 3.5 %collective-permute-start.10 = (f32[2,256,64]{2,1,0:T(8,128)S(1)}, f32[2,256,64]{2,1,0:T(8,128)S(1)}, u32[]{:S(2)}, u32[]{:S(2)}) collective-permute-start(f32[2,256,64]{2,1,0:T(8,128)S(1)} %get-tuple-element.57), channel_id=1, source_target_pairs={{0,1},{1,2},{2,3},{3,4},{4,5},{5,6},{6,7},{7,8},{8,9},{9,10},{10,1... | collective-permute-start | bytes 393224 | tf_op jit(solution)/shard_map/ppermute | solution.py:322
  155.1 4.5 %collective-permute-start.11 = (f32[2,256,64]{2,1,0:T(8,128)S(1)}, f32[2,256,64]{2,1,0:T(8,128)S(1)}, u32[]{:S(2)}, u32[]{:S(2)}) collective-permute-start(f32[2,256,64]{2,1,0:T(8,128)S(1)} %get-tuple-element.58), channel_id=1, source_target_pairs={{1,0},{2,1},{3,2},{4,3},{5,4},{6,5},{7,6},{8,7},{9,8},{10,9},{11,1... | collective-permute-start | bytes 393224 | tf_op jit(solution)/shard_map/ppermute | solution.py:323
  159.6 4.0 %collective-permute-done.10 = f32[2,256,64]{2,1,0:T(8,128)S(1)} collective-permute-done((f32[2,256,64]{2,1,0:T(8,128)S(1)}, f32[2,256,64]{2,1,0:T(8,128)S(1)}, u32[]{:S(2)}, u32[]{:S(2)}) %collective-permute-start.10) | collective-permute-done | bytes 131104 | tf_op jit(solution)/shard_map/ppermute | solution.py:322
  165.8 9.2 %cut.3 = (f32[32,2,128,128]{3,2,1,0:T(8,128)S(1)}, f32[4096,128]{1,0:T(8,128)S(1)}, f32[128,8,128]{2,1,0:T(8,128)S(1)}) custom-call(s32[32,2]{1,0:T(8,128)S(1)} %copy.29.offs, f32[2,2,256,128]{3,2,1,0:T(8,128)S(1)} %copy.33.ext, f32[32,8]{1,0:T(8,128)S(1)} %broadcast_multiply_fusion.coef), custom_call_target="tpu_custom_call" | custom-call | tf_op jit(solution)/shard_map/cut/pallas_call | solution.py:241
  179.9 38.4 %waves.3 = (f32[3,2,256,128]{3,2,1,0:T(8,128)S(1)}, f32[4096,128]{1,0:T(8,128)S(1)}, f32[4096,128]{1,0:T(8,128)S(1)}, f32[128,8,256]{2,1,0:T(8,128)S(1)}) custom-call(s32[32,2]{1,0:T(8,128)S(1)} %copy.29.offs, f32[32,2,128,128]{3,2,1,0:T(8,128)} %copy-done.2, s32[32,128,128]{2,1,0:T(8,128)S(1)} %bitcast.44, f32[128,8,256]{2,1,0:T(8,128)S(1)} %all-to-all-done.1.modes, ...), custom_call_target="tpu_custom_call" | custom-call | tf_op jit(solution)/shard_map/waves/pallas_call | solution.py:259
  223.2 12.4 %all-to-all-start.2 = ((f32[128,8,384]{2,1,0:T(8,128)}), f32[128,8,384]{2,1,0:T(8,128)}, u32[]{:S(2)}, u32[]{:S(2)}) async-start(f32[128,8,384]{2,1,0:T(8,128)} %pad_maximum_fusion.1), calls=%async_computation.2 | async-start | bytes 3145728 | tf_op jit(solution)/shard_map/all_to_all | solution.py:361
  237.9 3.7 %collective-permute-start.12 = (f32[3,64,256]{2,1,0:T(8,128)}, f32[3,64,256]{2,1,0:T(8,128)}, u32[]{:S(2)}, u32[]{:S(2)}) collective-permute-start(f32[3,64,256]{2,1,0:T(8,128)} %get-tuple-element.40), channel_id=1, source_target_pairs={{0,16},{16,32},{32,48},{48,64},{64,80},{80,96},{96,112},{1,17},{17... | collective-permute-start | bytes 589832 | tf_op jit(solution)/shard_map/ppermute | solution.py:322
  241.6 17.8 %all-to-all-done.2 = f32[128,8,384]{2,1,0:T(8,128)} async-done(((f32[128,8,384]{2,1,0:T(8,128)}), f32[128,8,384]{2,1,0:T(8,128)}, u32[]{:S(2)}, u32[]{:S(2)}) %all-to-all-start.2) | async-done | bytes 1572896 | tf_op jit(solution)/shard_map/all_to_all | solution.py:361
  262.1 5.9 %all-to-all-start.3 = ((f32[128,8,256]{2,1,0:T(8,128)}), f32[128,8,256]{2,1,0:T(8,128)}, u32[]{:S(2)}, u32[]{:S(2)}) async-start(f32[128,8,256]{2,1,0:T(8,128)} %broadcast_in_dim.7), calls=%async_computation.3 | async-start | bytes 2097152 | tf_op jit(solution)/shard_map/all_to_all | solution.py:368
  270.3 5.4 %collective-permute-start.15 = (f32[3,128,64]{2,1,0:T(8,128)}, f32[3,128,64]{2,1,0:T(8,128)}, u32[]{:S(2)}, u32[]{:S(2)}) collective-permute-start(f32[3,128,64]{2,1,0:T(8,128)} %get-tuple-element.49), channel_id=1, source_target_pairs={{1,0},{2,1},{3,2},{4,3},{5,4},{6,5},{7,6},{8,7},{9,8},{10,9},{11,1... | collective-permute-start | bytes 294920 | tf_op jit(solution)/shard_map/ppermute | solution.py:323
  280.9 3.8 %coefs.3 = f32[32,8]{1,0:T(8,128)S(1)} custom-call(f32[4096,128]{1,0:T(8,128)S(1)} %copy-done.13, f32[4096,128]{1,0:T(8,128)S(1)} %copy-done.15, f32[4096,128]{1,0:T(8,128)S(1)} %copy-done.11, f32[128,8,256]{2,1,0:T(8,128)S(1)} %all-to-all-done.1.modes, f32[32,8]{1,0:T(8,128)S(1)} %coefs.2.coef), custom_call_target="tpu_custom_call" | custom-call | tf_op jit(solution)/shard_map/coefs/pallas_call | solution.py:298
  (128 shorter events, 66.0 us)
Async XLA Ops:
  1.6 8.4 %collective-permute-start.1 = (f32[2,64,128]{2,1,0:T(8,128)S(1)}, f32[2,64,128]{2,1,0:T(8,128)S(1)}, u32[]{:S(2)}, u32[]{:S(2)}) collective-permute-start(f32[2,64,128]{2,1,0:T(8,128)S(1)} %get-tuple-element.65), channel_id=1, source_target_pairs={{16,0},{32,16},{48,32},{64,48},{80,64},{96,80},{112,96},{17,1},{33... | collective-permute-start | bytes 196616 | tf_op jit(solution)/shard_map/ppermute | solution.py:323
  2.9 7.1 %collective-permute-start = (f32[2,64,128]{2,1,0:T(8,128)S(1)}, f32[2,64,128]{2,1,0:T(8,128)S(1)}, u32[]{:S(2)}, u32[]{:S(2)}) collective-permute-start(f32[2,64,128]{2,1,0:T(8,128)S(1)} %get-tuple-element.66), channel_id=1, source_target_pairs={{0,16},{16,32},{32,48},{48,64},{64,80},{80,96},{96,112},{1,17},{17... | collective-permute-start | bytes 196616 | tf_op jit(solution)/shard_map/ppermute | solution.py:322
  10.0 28.2 %copy-start.18 = (bf16[256,768]{1,0:T(8,128)(2,1)S(1)}, bf16[256,768]{1,0:T(8,128)(2,1)}, u32[]{:S(2)}) copy-start(bf16[256,768]{1,0:T(8,128)(2,1)} %constant.33.clone.back_w) | copy-start | bytes 1179652
  10.0 28.1 %copy-start.19 = (bf16[768,256]{1,0:T(8,128)(2,1)S(1)}, bf16[768,256]{1,0:T(8,128)(2,1)}, u32[]{:S(2)}) copy-start(bf16[768,256]{1,0:T(8,128)(2,1)} %constant.32.clone.ahead_t) | copy-start | bytes 1179652
  10.2 28.0 %copy-start = (s32[1,1,32,128,128]{4,3,2,1,0:T(8,128)S(1)}, s32[1,1,32,128,128]{4,3,2,1,0:T(8,128)}, u32[]{:S(2)}) copy-start(s32[1,1,32,128,128]{4,3,2,1,0:T(8,128)} %param.15) | copy-start | bytes 6291460
  10.2 28.0 %copy-start.16 = (bf16[768,256]{1,0:T(8,128)(2,1)S(1)}, bf16[768,256]{1,0:T(8,128)(2,1)}, u32[]{:S(2)}) copy-start(bf16[768,256]{1,0:T(8,128)(2,1)} %constant.35.clone.back_t) | copy-start | bytes 1179652
  10.2 13.1 %collective-permute-start.2 = (f32[2,256,64]{2,1,0:T(8,128)S(1)}, f32[2,256,64]{2,1,0:T(8,128)S(1)}, u32[]{:S(2)}, u32[]{:S(2)}) collective-permute-start(f32[2,256,64]{2,1,0:T(8,128)S(1)} %get-tuple-element.61), channel_id=1, source_target_pairs={{0,1},{1,2},{2,3},{3,4},{4,5},{5,6},{6,7},{7,8},{8,9},{9,10},{10,1... | collective-permute-start | bytes 393224 | tf_op jit(solution)/shard_map/ppermute | solution.py:322
  14.3 10.9 %collective-permute-start.3 = (f32[2,256,64]{2,1,0:T(8,128)S(1)}, f32[2,256,64]{2,1,0:T(8,128)S(1)}, u32[]{:S(2)}, u32[]{:S(2)}) collective-permute-start(f32[2,256,64]{2,1,0:T(8,128)S(1)} %get-tuple-element.62), channel_id=1, source_target_pairs={{1,0},{2,1},{3,2},{4,3},{5,4},{6,5},{7,6},{8,7},{9,8},{10,9},{11,1... | collective-permute-start | bytes 393224 | tf_op jit(solution)/shard_map/ppermute | solution.py:323
  81.5 36.4 %all-to-all-start = ((f32[128,8,384]{2,1,0:T(8,128)}), f32[128,8,384]{2,1,0:T(8,128)}, u32[]{:S(2)}, u32[]{:S(2)}) async-start(f32[128,8,384]{2,1,0:T(8,128)} %pad_maximum_fusion), calls=%async_computation | async-start | bytes 3145728 | tf_op jit(solution)/shard_map/all_to_all | solution.py:361
  92.7 4.4 %collective-permute-start.5 = (f32[3,64,256]{2,1,0:T(8,128)S(1)}, f32[3,64,256]{2,1,0:T(8,128)S(1)}, u32[]{:S(2)}, u32[]{:S(2)}) collective-permute-start(f32[3,64,256]{2,1,0:T(8,128)S(1)} %get-tuple-element.43), channel_id=1, source_target_pairs={{16,0},{32,16},{48,32},{64,48},{80,64},{96,80},{112,96},{17,1},{33... | collective-permute-start | bytes 589832 | tf_op jit(solution)/shard_map/ppermute | solution.py:323
  94.0 4.1 %collective-permute-start.4 = (f32[3,64,256]{2,1,0:T(8,128)S(1)}, f32[3,64,256]{2,1,0:T(8,128)S(1)}, u32[]{:S(2)}, u32[]{:S(2)}) collective-permute-start(f32[3,64,256]{2,1,0:T(8,128)S(1)} %get-tuple-element.44), channel_id=1, source_target_pairs={{0,16},{16,32},{32,48},{48,64},{64,80},{80,96},{96,112},{1,17},{17... | collective-permute-start | bytes 589832 | tf_op jit(solution)/shard_map/ppermute | solution.py:322
  98.3 15.4 %collective-permute-start.7 = (f32[3,128,64]{2,1,0:T(8,128)S(1)}, f32[3,128,64]{2,1,0:T(8,128)S(1)}, u32[]{:S(2)}, u32[]{:S(2)}) collective-permute-start(f32[3,128,64]{2,1,0:T(8,128)S(1)} %get-tuple-element.53), channel_id=1, source_target_pairs={{1,0},{2,1},{3,2},{4,3},{5,4},{6,5},{7,6},{8,7},{9,8},{10,9},{11,1... | collective-permute-start | bytes 294920 | tf_op jit(solution)/shard_map/ppermute | solution.py:323
  103.6 13.0 %collective-permute-start.6 = (f32[3,128,64]{2,1,0:T(8,128)S(1)}, f32[3,128,64]{2,1,0:T(8,128)}, u32[]{:S(2)}, u32[]{:S(2)}) collective-permute-start(f32[3,128,64]{2,1,0:T(8,128)S(1)} %get-tuple-element.54), channel_id=1, source_target_pairs={{0,1},{1,2},{2,3},{3,4},{4,5},{5,6},{6,7},{7,8},{8,9},{9,10},{10,1... | collective-permute-start | bytes 294920 | tf_op jit(solution)/shard_map/ppermute | solution.py:322
  120.5 57.8 %all-to-all-start.1 = ((f32[128,8,256]{2,1,0:T(8,128)}), f32[128,8,256]{2,1,0:T(8,128)S(1)}, u32[]{:S(2)}, u32[]{:S(2)}) async-start(f32[128,8,256]{2,1,0:T(8,128)} %broadcast_in_dim.6), calls=%async_computation.1 | async-start | bytes 2097152 | tf_op jit(solution)/shard_map/all_to_all | solution.py:368
  139.5 11.9 %collective-permute-start.8 = (f32[2,64,128]{2,1,0:T(8,128)S(1)}, f32[2,64,128]{2,1,0:T(8,128)S(1)}, u32[]{:S(2)}, u32[]{:S(2)}) collective-permute-start(f32[2,64,128]{2,1,0:T(8,128)S(1)} %get-tuple-element.63), channel_id=1, source_target_pairs={{0,16},{16,32},{32,48},{48,64},{64,80},{80,96},{96,112},{1,17},{17... | collective-permute-start | bytes 196616 | tf_op jit(solution)/shard_map/ppermute | solution.py:322
  141.5 9.9 %collective-permute-start.9 = (f32[2,64,128]{2,1,0:T(8,128)S(1)}, f32[2,64,128]{2,1,0:T(8,128)S(1)}, u32[]{:S(2)}, u32[]{:S(2)}) collective-permute-start(f32[2,64,128]{2,1,0:T(8,128)S(1)} %get-tuple-element.64), channel_id=1, source_target_pairs={{16,0},{32,16},{48,32},{64,48},{80,64},{96,80},{112,96},{17,1},{33... | collective-permute-start | bytes 196616 | tf_op jit(solution)/shard_map/ppermute | solution.py:323
  151.6 12.1 %collective-permute-start.10 = (f32[2,256,64]{2,1,0:T(8,128)S(1)}, f32[2,256,64]{2,1,0:T(8,128)S(1)}, u32[]{:S(2)}, u32[]{:S(2)}) collective-permute-start(f32[2,256,64]{2,1,0:T(8,128)S(1)} %get-tuple-element.57), channel_id=1, source_target_pairs={{0,1},{1,2},{2,3},{3,4},{4,5},{5,6},{6,7},{7,8},{8,9},{9,10},{10,1... | collective-permute-start | bytes 393224 | tf_op jit(solution)/shard_map/ppermute | solution.py:322
  155.1 10.3 %collective-permute-start.11 = (f32[2,256,64]{2,1,0:T(8,128)S(1)}, f32[2,256,64]{2,1,0:T(8,128)S(1)}, u32[]{:S(2)}, u32[]{:S(2)}) collective-permute-start(f32[2,256,64]{2,1,0:T(8,128)S(1)} %get-tuple-element.58), channel_id=1, source_target_pairs={{1,0},{2,1},{3,2},{4,3},{5,4},{6,5},{7,6},{8,7},{9,8},{10,9},{11,1... | collective-permute-start | bytes 393224 | tf_op jit(solution)/shard_map/ppermute | solution.py:323
  223.2 36.2 %all-to-all-start.2 = ((f32[128,8,384]{2,1,0:T(8,128)}), f32[128,8,384]{2,1,0:T(8,128)}, u32[]{:S(2)}, u32[]{:S(2)}) async-start(f32[128,8,384]{2,1,0:T(8,128)} %pad_maximum_fusion.1), calls=%async_computation.2 | async-start | bytes 3145728 | tf_op jit(solution)/shard_map/all_to_all | solution.py:361
  236.6 31.4 %collective-permute-start.13 = (f32[3,64,256]{2,1,0:T(8,128)}, f32[3,64,256]{2,1,0:T(8,128)}, u32[]{:S(2)}, u32[]{:S(2)}) collective-permute-start(f32[3,64,256]{2,1,0:T(8,128)} %get-tuple-element.39), channel_id=1, source_target_pairs={{16,0},{32,16},{48,32},{64,48},{80,64},{96,80},{112,96},{17,1},{33... | collective-permute-start | bytes 589832 | tf_op jit(solution)/shard_map/ppermute | solution.py:323
  237.9 30.1 %collective-permute-start.12 = (f32[3,64,256]{2,1,0:T(8,128)}, f32[3,64,256]{2,1,0:T(8,128)}, u32[]{:S(2)}, u32[]{:S(2)}) collective-permute-start(f32[3,64,256]{2,1,0:T(8,128)} %get-tuple-element.40), channel_id=1, source_target_pairs={{0,16},{16,32},{32,48},{48,64},{64,80},{80,96},{96,112},{1,17},{17... | collective-permute-start | bytes 589832 | tf_op jit(solution)/shard_map/ppermute | solution.py:322
  262.1 29.0 %all-to-all-start.3 = ((f32[128,8,256]{2,1,0:T(8,128)}), f32[128,8,256]{2,1,0:T(8,128)}, u32[]{:S(2)}, u32[]{:S(2)}) async-start(f32[128,8,256]{2,1,0:T(8,128)} %broadcast_in_dim.7), calls=%async_computation.3 | async-start | bytes 2097152 | tf_op jit(solution)/shard_map/all_to_all | solution.py:368
  270.3 15.9 %collective-permute-start.15 = (f32[3,128,64]{2,1,0:T(8,128)}, f32[3,128,64]{2,1,0:T(8,128)}, u32[]{:S(2)}, u32[]{:S(2)}) collective-permute-start(f32[3,128,64]{2,1,0:T(8,128)} %get-tuple-element.49), channel_id=1, source_target_pairs={{1,0},{2,1},{3,2},{4,3},{5,4},{6,5},{7,6},{8,7},{9,8},{10,9},{11,1... | collective-permute-start | bytes 294920 | tf_op jit(solution)/shard_map/ppermute | solution.py:323
  275.7 13.1 %collective-permute-start.14 = (f32[3,128,64]{2,1,0:T(8,128)}, f32[3,128,64]{2,1,0:T(8,128)}, u32[]{:S(2)}, u32[]{:S(2)}) collective-permute-start(f32[3,128,64]{2,1,0:T(8,128)} %get-tuple-element.50), channel_id=1, source_target_pairs={{0,1},{1,2},{2,3},{3,4},{4,5},{5,6},{6,7},{7,8},{8,9},{9,10},{10,1... | collective-permute-start | bytes 294920 | tf_op jit(solution)/shard_map/ppermute | solution.py:322
  (26 other events, 174.7 us)

commit v2 on v1

--- a/solution.py
+++ b/solution.py
@@ -18,6 +18,8 @@
 F32 = jnp.float32
 BF16 = jnp.bfloat16
 DEVICES = 128
+PAIRS = 4
+LEAD = 33
 
 
 def split(x):
@@ -60,7 +62,7 @@
     return jnp.dot(a, b, preferred_element_type=F32)
 
 
-def patch_kernel(offs, ext, coef, patches, powers, moment, pw):
+def patch_kernel(offs, ext, coef, patches, pw, moment):
     lane = lax.broadcasted_iota(jnp.int32, (PS, PS), 1)
 
     def cut(p, _):
@@ -75,11 +77,10 @@
             patch = jnp.where(inside, a, b)
             patches[p, c] = patch
             total = patch * patch if total is None else total + patch * patch
-        pw[pl.ds(p, PS, stride=PMAX), :] = total
+        pw[pl.ds(p, PS, stride=LEAD), :] = total
         return 0
 
-    lax.fori_loop(0, PMAX, cut, 0)
-    powers[...] = pw[...]
+    lax.fori_loop(0, PMAX, cut, 0, unroll=4)
     square = coef[...] * coef[...]
     hi, lo = split(square.T)
     zero = jnp.zeros_like(hi)
@@ -89,7 +90,7 @@
 
     def rows(y, _):
         pair = jnp.concatenate(
-            [pw[pl.ds(2 * y * PMAX, PMAX), :], pw[pl.ds((2 * y + 1) * PMAX, PMAX), :]], axis=1
+            [pw[pl.ds(2 * y * LEAD, PMAX), :], pw[pl.ds((2 * y + 1) * LEAD, PMAX), :]], axis=1
         )
         h, l = split(pair)
         out = dot(left, jnp.concatenate([h, l], axis=0))
@@ -98,86 +99,106 @@
         moment[2 * y + 1] = out[:, PS:]
         return 0
 
-    lax.fori_loop(0, PS // 2, rows, 0, unroll=4)
+    lax.fori_loop(0, PS // 2, rows, 0, unroll=8)
+
+
+def probe_kernel(modes, coef, probe_r, probe_i):
+    left = triple(coef[...], 1)
+
+    def rows(y, _):
+        m = modes[y]
+        h = m.astype(BF16).astype(F32)
+        right = jnp.concatenate([h, h, m - h], axis=0).astype(BF16)
+        out = dot(left, right)
+        start = y * LEAD
+        probe_r[pl.ds(start, PMAX), :] = out[:, :PS]
+        probe_i[pl.ds(start, PMAX), :] = out[:, PS:]
+        return 0
+
+    lax.fori_loop(0, PS, rows, 0, unroll=8)
 
 
 def wave_kernel(
-    offs, patches, photons, modes, coef, ahead_t, back_w, ahead_w, back_t,
-    acc, cross_r, cross_i, moment, probe_r, probe_i, field, wave,
+    offs, patches, photons, probe_r, probe_i, coef, ahead_t, back_w, ahead_w, back_t,
+    acc_rl, acc_rh, acc_il, acc_ih, acc_pl, acc_ph, cross_r, cross_i, moment,
+    wave, field,
 ):
     step = pl.program_id(0)
     lane = lax.broadcasted_iota(jnp.int32, (PS, PS), 1)
+    sums = ((acc_rl, acc_rh), (acc_il, acc_ih), (acc_pl, acc_ph))
 
     @pl.when(step == 0)
     def _():
-        acc[...] = jnp.zeros_like(acc)
-        left = triple(coef[...], 1)
-
-        def rows(y, _):
-            m = modes[y]
-            h = m.astype(BF16).astype(F32)
-            right = jnp.concatenate([h, h, m - h], axis=0).astype(BF16)
-            out = dot(left, right)
-            start = pl.multiple_of(y * PMAX, PMAX)
-            probe_r[pl.ds(start, PMAX), :] = out[:, :PS]
-            probe_i[pl.ds(start, PMAX), :] = out[:, PS:]
-            return 0
-
-        lax.fori_loop(0, PS, rows, 0, unroll=8)
-
-    for q in range(2):
-        p = 2 * step + q
-        pr = probe_r[pl.ds(p, PS, stride=PMAX), :]
-        pi = probe_i[pl.ds(p, PS, stride=PMAX), :]
-        obj_r = patches[q, 0]
-        obj_i = patches[q, 1]
-        rows = slice(q * PS, (q + 1) * PS)
-        wave[rows, :PS] = pr * obj_r - pi * obj_i
-        wave[rows, PS:] = pr * obj_i + pi * obj_r
+        for low, high in sums:
+            low[...] = jnp.zeros_like(low)
+            high[...] = jnp.zeros_like(high)
 
     def regroup(x):
         top = jnp.concatenate([x[:PS, :PS], x[PS:, :PS]], axis=1)
         low = jnp.concatenate([x[:PS, PS:], x[PS:, PS:]], axis=1)
         return jnp.concatenate([top, low], axis=0)
 
-    out = dot(triple(wave[...], 1), ahead_t[...])
-    far = dot(back_w[...], triple(regroup(out), 0))
-    count = jnp.concatenate([photons[0], photons[1]], axis=1).astype(F32)
-    far_r = far[:PS]
-    far_i = far[PS:]
-    size = jnp.maximum(far_r * far_r + far_i * far_i, 0.25)
-    scale = count * lax.rsqrt(jnp.maximum(count * size, 0.0625)) * 0.03125
-    fixed = jnp.concatenate([far_r * scale, far_i * scale], axis=0)
-    out = dot(ahead_w[...], triple(fixed, 0))
-    field[...] = dot(triple(regroup(out), 1), back_t[...]) - wave[...]
-
-    for q in range(2):
-        p = 2 * step + q
-        top = offs[p, 0]
-        left = offs[p, 1]
-        turn = left & (PS - 1)
-        inside = lane >= left
-        rows = slice(q * PS, (q + 1) * PS)
-        diff_r = field[rows, :PS]
-        diff_i = field[rows, PS:]
-        obj_r = patches[q, 0]
-        obj_i = patches[q, 1]
-        cross_r[pl.ds(p, PS, stride=PMAX), :] = obj_r * diff_r + obj_i * diff_i
-        cross_i[pl.ds(p, PS, stride=PMAX), :] = obj_r * diff_i - obj_i * diff_r
-        pr = probe_r[pl.ds(p, PS, stride=PMAX), :]
-        pi = probe_i[pl.ds(p, PS, stride=PMAX), :]
-        pieces = (
-            pr * diff_r + pi * diff_i,
-            pr * diff_i - pi * diff_r,
-            pr * pr + pi * pi,
+    def take(j, q):
+        p = 2 * PAIRS * step + 2 * j + q
+        return (
+            probe_r[pl.ds(p, PS, stride=LEAD), :],
+            probe_i[pl.ds(p, PS, stride=LEAD), :],
+            patches[2 * j + q, 0],
+            patches[2 * j + q, 1],
         )
-        for c in range(3):
-            turned = pltpu.roll(pieces[c], turn, 1)
-            near = jnp.where(inside, turned, 0.0)
-            acc[c, 0, pl.ds(top, PS), :] += near
-            acc[c, 1, pl.ds(top, PS), :] += turned - near
-
-    @pl.when(step == PMAX // 2 - 1)
+
+    def start(j):
+        for q in range(2):
+            pr, pi, obj_r, obj_i = take(j, q)
+            rows = slice(q * PS, (q + 1) * PS)
+            wave[j, rows, :PS] = pr * obj_r - pi * obj_i
+            wave[j, rows, PS:] = pr * obj_i + pi * obj_r
+
+    def correct(j, far):
+        count = jnp.concatenate([photons[2 * j], photons[2 * j + 1]], axis=1).astype(F32)
+        far_r = far[:PS]
+        far_i = far[PS:]
+        size = jnp.maximum(far_r * far_r + far_i * far_i, 0.25)
+        scale = count * lax.rsqrt(jnp.maximum(count * size, 0.0625)) * 0.03125
+        return jnp.concatenate([far_r * scale, far_i * scale], axis=0)
+
+    def finish(j):
+        for q in range(2):
+            p = 2 * PAIRS * step + 2 * j + q
+            top = offs[p, 0]
+            left = offs[p, 1]
+            turn = left & (PS - 1)
+            inside = lane >= left
+            rows = slice(q * PS, (q + 1) * PS)
+            diff_r = field[j, rows, :PS]
+            diff_i = field[j, rows, PS:]
+            pr, pi, obj_r, obj_i = take(j, q)
+            cross_r[pl.ds(p, PS, stride=LEAD), :] = obj_r * diff_r + obj_i * diff_i
+            cross_i[pl.ds(p, PS, stride=LEAD), :] = obj_r * diff_i - obj_i * diff_r
+            pieces = (
+                pr * diff_r + pi * diff_i,
+                pr * diff_i - pi * diff_r,
+                pr * pr + pi * pi,
+            )
+            for (low, high), piece in zip(sums, pieces):
+                turned = pltpu.roll(piece, turn, 1)
+                near = jnp.where(inside, turned, 0.0)
+                low[pl.ds(top, PS), :] += near
+                high[pl.ds(top, PS), :] += turned - near
+
+    pairs = range(PAIRS)
+    for j in pairs:
+        start(j)
+    x = [dot(triple(wave[j], 1), ahead_t[...]) for j in pairs]
+    x = [dot(back_w[...], triple(regroup(x[j]), 0)) for j in pairs]
+    x = [correct(j, x[j]) for j in pairs]
+    x = [dot(ahead_w[...], triple(x[j], 0)) for j in pairs]
+    for j in pairs:
+        field[j] = dot(triple(regroup(x[j]), 1), back_t[...]) - wave[j]
+    for j in pairs:
+        finish(j)
+
+    @pl.when(step == PMAX // (2 * PAIRS) - 1)
     def _():
         hi, lo = split(coef[...].T)
         zero = jnp.zeros_like(hi)
@@ -186,7 +207,7 @@
         )
 
         def rows(y, _):
-            start = pl.multiple_of(y * PMAX, PMAX)
+            start = y * LEAD
             pair = jnp.concatenate(
                 [cross_r[pl.ds(start, PMAX), :], cross_i[pl.ds(start, PMAX), :]], axis=1
             )
@@ -217,7 +238,7 @@
     top = jnp.zeros((PMAX, MODES), F32)
     low = jnp.zeros((PMAX, MODES), F32)
     for y in range(CHUNK):
-        rows = slice(y * PMAX, (y + 1) * PMAX)
+        rows = slice(y * LEAD, y * LEAD + PMAX)
         cross = jnp.concatenate([cross_r[rows, :], cross_i[rows, :]], axis=1)
         m = modes[y]
         power = m[:, :PS] * m[:, :PS] + m[:, PS:] * m[:, PS:]
@@ -242,58 +263,58 @@
         patch_kernel,
         out_shape=(
             jax.ShapeDtypeStruct((PMAX, 2, PS, PS), F32),
-            jax.ShapeDtypeStruct((PS * PMAX, PS), F32),
+            jax.ShapeDtypeStruct((PS * LEAD, PS), F32),
             jax.ShapeDtypeStruct((PS, MODES, PS), F32),
         ),
         in_specs=[SMEM, VMEM, VMEM],
         out_specs=(VMEM, VMEM, VMEM),
-        scratch_shapes=[pltpu.VMEM((PS * PMAX, PS), F32)],
-        compiler_params=pltpu.CompilerParams(vmem_limit_bytes=24 << 20),
+        compiler_params=pltpu.CompilerParams(vmem_limit_bytes=4 << 20),
         name="cut",
     )(offs, ext, coef)
 
 
-def waves(offs, patches, photons, modes, coef, tables):
-    whole = lambda *shape: pl.BlockSpec(shape, lambda i: (0,) * len(shape))
-    table_specs = [whole(*t.shape) for t in tables]
+def mix_probes(modes, coef):
+    grid = jax.ShapeDtypeStruct((PS * LEAD, PS), F32)
+    return pl.pallas_call(
+        probe_kernel,
+        out_shape=(grid, grid),
+        in_specs=[VMEM, VMEM],
+        out_specs=(VMEM, VMEM),
+        compiler_params=pltpu.CompilerParams(vmem_limit_bytes=2 << 20),
+        name="probes",
+    )(modes, coef)
+
+
+def waves(offs, patches, photons, probe_r, probe_i, coef, tables):
+    half = jax.ShapeDtypeStruct((EXT, PS), F32)
+    grid = jax.ShapeDtypeStruct((PS * LEAD, PS), F32)
     return pl.pallas_call(
         wave_kernel,
-        grid=(PMAX // 2,),
-        out_shape=(
-            jax.ShapeDtypeStruct((3, 2, EXT, PS), F32),
-            jax.ShapeDtypeStruct((PS * PMAX, PS), F32),
-            jax.ShapeDtypeStruct((PS * PMAX, PS), F32),
-            jax.ShapeDtypeStruct((PS, MODES, 2 * PS), F32),
-        ),
+        grid=(PMAX // (2 * PAIRS),),
+        out_shape=(*[half] * 6, grid, grid, jax.ShapeDtypeStruct((PS, MODES, 2 * PS), F32)),
         in_specs=[
             SMEM,
-            pl.BlockSpec((2, 2, PS, PS), lambda i: (i, 0, 0, 0)),
-            pl.BlockSpec((2, PS, PS), lambda i: (i, 0, 0)),
-            whole(PS, MODES, 2 * PS),
-            whole(PMAX, MODES),
-            *table_specs,
+            pl.BlockSpec((2 * PAIRS, 2, PS, PS), lambda i: (i, 0, 0, 0)),
+            pl.BlockSpec((2 * PAIRS, PS, PS), lambda i: (i, 0, 0)),
+            VMEM,
+            VMEM,
+            VMEM,
+            *[VMEM] * len(tables),
         ],
-        out_specs=(
-            whole(3, 2, EXT, PS),
-            whole(PS * PMAX, PS),
-            whole(PS * PMAX, PS),
-            whole(PS, MODES, 2 * PS),
-        ),
+        out_specs=(VMEM,) * 9,
         scratch_shapes=[
-            pltpu.VMEM((PS * PMAX, PS), F32),
-            pltpu.VMEM((PS * PMAX, PS), F32),
-            pltpu.VMEM((2 * PS, 2 * PS), F32),
-            pltpu.VMEM((2 * PS, 2 * PS), F32),
+            pltpu.VMEM((PAIRS, 2 * PS, 2 * PS), F32),
+            pltpu.VMEM((PAIRS, 2 * PS, 2 * PS), F32),
         ],
         compiler_params=pltpu.CompilerParams(
-            dimension_semantics=("arbitrary",), vmem_limit_bytes=40 << 20
+            dimension_semantics=("arbitrary",), vmem_limit_bytes=20 << 20
         ),
         name="waves",
-    )(offs, patches, photons, modes, coef, *tables)
+    )(offs, patches, photons, probe_r, probe_i, coef, *tables)
 
 
 def new_coefficients(cross_r, cross_i, powers, modes, coef):
-    rows = pl.BlockSpec((CHUNK * PMAX, PS), lambda i: (i, 0))
+    rows = pl.BlockSpec((CHUNK * LEAD, PS), lambda i: (i, 0))
     whole = pl.BlockSpec((PMAX, MODES), lambda i: (0, 0))
     return pl.pallas_call(
         coef_kernel,
@@ -309,7 +330,7 @@
         out_specs=whole,
         scratch_shapes=[pltpu.VMEM((PMAX, MODES), F32)] * 2,
         compiler_params=pltpu.CompilerParams(
-            dimension_semantics=("arbitrary",), vmem_limit_bytes=16 << 20
+            dimension_semantics=("arbitrary",), vmem_limit_bytes=6 << 20
         ),
         name="coefs",
     )(cross_r, cross_i, powers, modes, coef)
@@ -334,7 +355,7 @@
 
 def fold(acc):
     margin = PS // 2
-    full = jnp.concatenate([acc[:, 0], acc[:, 1]], axis=2)
+    full = jnp.concatenate([jnp.stack(acc[::2]), jnp.stack(acc[1::2])], axis=2)
     low, high = swap_sides(full[:, :margin], full[:, -margin:], "row")
     mid = full[:, margin:-margin]
     mid = jnp.concatenate([mid[:, :margin] + low, mid[:, margin:] + high], axis=1)
@@ -356,7 +377,10 @@
         ext = jnp.stack([ext[:, :, :PS], ext[:, :, PS:]], axis=1)
         used = coef * live
         patches, powers, power_moment = cut_patches(offs, ext, used)
-        acc, cross_r, cross_i, moment = waves(offs, patches, photons, modes, used, tables)
+        probe_r, probe_i = mix_probes(modes, used)
+        *acc, cross_r, cross_i, moment = waves(
+            offs, patches, photons, probe_r, probe_i, used, tables
+        )
         sent = jnp.concatenate([moment, power_moment], axis=2)
         got = lax.all_to_all(sent, ("row", "col"), 0, 0, tiled=True)
         total = jnp.sum(got, axis=0)

time: 295 us -> 245 us (0.83)
  Pallas kernels: 103 us -> 50.7 us
  waiting for transfers between devices: 46 us -> 29.8 us
  starting transfers between devices: 96.1 us -> 112 us
  local copies, waits for them, and re-layouts: 33.4 us -> 36.9 us
    pallas_call x2 -> x4, Pallas kernels: 76.9 us -> 33.3 us  [the longest x2 27.8 us: waves(): pl.pallas_call(wave_kernel, grid=(PMAX // (2 * PAIRS),), out_shape=(*[hal...]
    all_to_all x2, waiting for transfers between devices: 17.8 us -> 1.27 us  [shards(): got = lax.all_to_all(sent, ('row', 'col'), 0, 0, tiled=True)]
    ppermute x8, starting transfers between devices: 23.2 us -> 37.5 us  [swap_sides(): from_below = lax.ppermute(high_part, axis, up)]
    pallas_call x2, Pallas kernels: 18.5 us -> 9.87 us  [cut_patches(): pl.pallas_call(patch_kernel, out_shape=(jax.ShapeDtypeStruct((PMAX, 2, PS...]
    unnamed x65 -> x73, local copies, waits for them, and re-layouts: 27.4 us -> 31 us
    ppermute x8, waiting for transfers between devices: 13 us -> 16.1 us  [swap_sides(): from_above = lax.ppermute(low_part, axis, down)]
  transfers between devices with their start and end apart: 20 -> 20, of which waited for: 10 -> 11; matrix products, arithmetic and copies ran while one was open for 5% -> 6% of each run, Pallas kernels for 6% -> 6%
where the time goes in v2:
time: 245 us; the launch traced here: 243 us
  starting transfers between devices  112 us (46%)
  Pallas kernels  50.7 us (21%)
  local copies, waits for them, and re-layouts  36.9 us (15%)
  waiting for transfers between devices  29.8 us (12%)
  other arithmetic  11.9 us (5%)
    ppermute x8, starting transfers between devices, swap_sides(): from_below = lax.ppermute(high_part, axis, up)  37.5 us
    unnamed x73, local copies, waits for them, and re-layouts  31 us
    pallas_call x2, Pallas kernels, waves(): pl.pallas_call(wave_kernel, grid=(PMAX // (2 * PAIRS),), out_shape=(*[hal...  27.8 us
    all_to_all x2, starting transfers between devices, shards(): modes = lax.all_to_all(copies, ('row', 'col'), 0, 0, tiled=True)  25.9 us
    all_to_all x2, starting transfers between devices, shards(): got = lax.all_to_all(sent, ('row', 'col'), 0, 0, tiled=True)  24.5 us
    ppermute x8, starting transfers between devices, swap_sides(): from_above = lax.ppermute(low_part, axis, down)  24.2 us
    ppermute x8, waiting for transfers between devices, swap_sides(): from_above = lax.ppermute(low_part, axis, down)  16.1 us
    ppermute x8, waiting for transfers between devices, swap_sides(): from_below = lax.ppermute(high_part, axis, up)  12.4 us
  transfers between devices with their start and end apart: 20, of which 11 were waited for; matrix products, arithmetic and copies ran while one was open for 6% of the time, Pallas kernels for 6%

profile of v2, /device:TPU:2, one launch (start us, length us, event | category | flops | bytes accessed | tf_op | source)
XLA Modules:
  0.0 243.5 jit_solution(8585126911390421144)
XLA Ops:
  2.9 3.0 %collective-permute-start = (f32[2,64,128]{2,1,0:T(8,128)S(1)}, f32[2,64,128]{2,1,0:T(8,128)S(1)}, u32[]{:S(2)}, u32[]{:S(2)}) collective-permute-start(f32[2,64,128]{2,1,0:T(8,128)S(1)} %get-tuple-element.88), channel_id=1, source_target_pairs={{0,16},{16,32},{32,48},{48,64},{64,80},{80,96},{96,112},{1,17},{17... | collective-permute-start | bytes 196616 | tf_op jit(solution)/shard_map/ppermute | solution.py:343
  10.2 4.1 %collective-permute-start.2 = (f32[2,256,64]{2,1,0:T(8,128)S(1)}, f32[2,256,64]{2,1,0:T(8,128)S(1)}, u32[]{:S(2)}, u32[]{:S(2)}) collective-permute-start(f32[2,256,64]{2,1,0:T(8,128)S(1)} %get-tuple-element.83), channel_id=1, source_target_pairs={{0,1},{1,2},{2,3},{3,4},{4,5},{5,6},{6,7},{7,8},{8,9},{9,10},{10,1... | collective-permute-start | bytes 393224 | tf_op jit(solution)/shard_map/ppermute | solution.py:343
  14.3 4.1 %collective-permute-start.3 = (f32[2,256,64]{2,1,0:T(8,128)S(1)}, f32[2,256,64]{2,1,0:T(8,128)S(1)}, u32[]{:S(2)}, u32[]{:S(2)}) collective-permute-start(f32[2,256,64]{2,1,0:T(8,128)S(1)} %get-tuple-element.84), channel_id=1, source_target_pairs={{1,0},{2,1},{3,2},{4,3},{5,4},{6,5},{7,6},{8,7},{9,8},{10,9},{11,1... | collective-permute-start | bytes 393224 | tf_op jit(solution)/shard_map/ppermute | solution.py:344
  18.5 2.7 %probes.2 = (f32[4224,128]{1,0:T(8,128)S(1)}, f32[4224,128]{1,0:T(8,128)S(1)}) custom-call(f32[128,8,256]{2,1,0:T(8,128)S(1)} %bitcast.44, f32[32,8]{1,0:T(8,128)S(1)} %broadcast_multiply_fusion.1.coef), custom_call_target="tpu_custom_call" | custom-call | tf_op jit(solution)/shard_map/probes/pallas_call | solution.py:278
  25.6 4.9 %cut.2 = (f32[32,2,128,128]{3,2,1,0:T(8,128)S(1)}, f32[4224,128]{1,0:T(8,128)S(1)}, f32[128,8,128]{2,1,0:T(8,128)S(1)}) custom-call(s32[32,2]{1,0:T(8,128)S(1)} %copy.26.offs, f32[2,2,256,128]{3,2,1,0:T(8,128)S(1)} %pad_maximum_fusion.2.ext, f32[32,8]{1,0:T(8,128)S(1)} %broadcast_multiply_fusion.1.coef), custom_call_target="tpu_custom_call" | custom-call | tf_op jit(solution)/shard_map/cut/pallas_call | solution.py:262
  31.9 13.9 %waves.2 = (f32[256,128]{1,0:T(8,128)S(1)}, f32[256,128]{1,0:T(8,128)S(1)}, f32[256,128]{1,0:T(8,128)S(1)}, f32[256,128]{1,0:T(8,128)S(1)}, f32[256,128]{1,0:T(8...) custom-call(s32[32,2]{1,0:T(8,128)S(1)} %copy.26.offs, ...), custom_call_target="tpu_custom_call" | custom-call | tf_op jit(solution)/shard_map/waves/pallas_call | solution.py:291
  51.2 12.1 %all-to-all-start = ((f32[128,8,384]{2,1,0:T(8,128)}), f32[128,8,384]{2,1,0:T(8,128)}, u32[]{:S(2)}, u32[]{:S(2)}) async-start(f32[128,8,384]{2,1,0:T(8,128)} %pad_maximum_fusion), calls=%async_computation | async-start | bytes 3145728 | tf_op jit(solution)/shard_map/all_to_all | solution.py:385
  67.5 5.2 %collective-permute-start.7 = (f32[3,128,64]{2,1,0:T(8,128)S(1)}, f32[3,128,64]{2,1,0:T(8,128)S(1)}, u32[]{:S(2)}, u32[]{:S(2)}) collective-permute-start(f32[3,128,64]{2,1,0:T(8,128)S(1)} %get-tuple-element.75), channel_id=1, source_target_pairs={{1,0},{2,1},{3,2},{4,3},{5,4},{6,5},{7,6},{8,7},{9,8},{10,9},{11,1... | collective-permute-start | bytes 294920 | tf_op jit(solution)/shard_map/ppermute | solution.py:344
  74.7 9.6 %collective-permute-done.7 = f32[3,128,64]{2,1,0:T(8,128)S(1)} collective-permute-done((f32[3,128,64]{2,1,0:T(8,128)S(1)}, f32[3,128,64]{2,1,0:T(8,128)S(1)}, u32[]{:S(2)}, u32[]{:S(2)}) %collective-permute-start.7) | collective-permute-done | bytes 98336 | tf_op jit(solution)/shard_map/ppermute | solution.py:344
  84.4 2.8 %collective-permute-done.6 = f32[3,128,64]{2,1,0:T(8,128)S(1)} collective-permute-done((f32[3,128,64]{2,1,0:T(8,128)S(1)}, f32[3,128,64]{2,1,0:T(8,128)S(1)}, u32[]{:S(2)}, u32[]{:S(2)}) %collective-permute-start.6) | collective-permute-done | bytes 98336 | tf_op jit(solution)/shard_map/ppermute | solution.py:343
  91.0 17.6 %all-to-all-start.1 = ((f32[128,8,256]{2,1,0:T(8,128)}), f32[128,8,256]{2,1,0:T(8,128)S(1)}, u32[]{:S(2)}, u32[]{:S(2)}) async-start(f32[128,8,256]{2,1,0:T(8,128)} %broadcast_in_dim.6), calls=%async_computation.1 | async-start | bytes 2097152 | tf_op jit(solution)/shard_map/all_to_all | solution.py:392
  116.8 3.8 %coefs.2.coef = f32[32,8]{1,0:T(8,128)S(1)} custom-call(f32[4224,128]{1,0:T(8,128)S(1)} %copy-done.7, f32[4224,128]{1,0:T(8,128)S(1)} %copy-done.9, f32[4224,128]{1,0:T(8,128)S(1)} %copy-done.5, f32[128,8,256]{2,1,0:T(8,128)S(1)} %bitcast.46, f32[32,8]{1,0:T(8,128)S(1)} %bitcast.49), custom_call_target="tpu_custom_call" | custom-call | tf_op jit(solution)/shard_map/coefs/pallas_call | solution.py:319
  120.8 3.5 %collective-permute-start.10 = (f32[2,256,64]{2,1,0:T(8,128)S(1)}, f32[2,256,64]{2,1,0:T(8,128)S(1)}, u32[]{:S(2)}, u32[]{:S(2)}) collective-permute-start(f32[2,256,64]{2,1,0:T(8,128)S(1)} %get-tuple-element.79), channel_id=1, source_target_pairs={{0,1},{1,2},{2,3},{3,4},{4,5},{5,6},{6,7},{7,8},{8,9},{9,10},{10,1... | collective-permute-start | bytes 393224 | tf_op jit(solution)/shard_map/ppermute | solution.py:343
  124.3 4.4 %collective-permute-start.11 = (f32[2,256,64]{2,1,0:T(8,128)S(1)}, f32[2,256,64]{2,1,0:T(8,128)S(1)}, u32[]{:S(2)}, u32[]{:S(2)}) collective-permute-start(f32[2,256,64]{2,1,0:T(8,128)S(1)} %get-tuple-element.80), channel_id=1, source_target_pairs={{1,0},{2,1},{3,2},{4,3},{5,4},{6,5},{7,6},{8,7},{9,8},{10,9},{11,1... | collective-permute-start | bytes 393224 | tf_op jit(solution)/shard_map/ppermute | solution.py:344
  128.8 4.0 %collective-permute-done.10 = f32[2,256,64]{2,1,0:T(8,128)S(1)} collective-permute-done((f32[2,256,64]{2,1,0:T(8,128)S(1)}, f32[2,256,64]{2,1,0:T(8,128)S(1)}, u32[]{:S(2)}, u32[]{:S(2)}) %collective-permute-start.10) | collective-permute-done | bytes 131104 | tf_op jit(solution)/shard_map/ppermute | solution.py:343
  134.9 4.9 %cut.3 = (f32[32,2,128,128]{3,2,1,0:T(8,128)S(1)}, f32[4224,128]{1,0:T(8,128)S(1)}, f32[128,8,128]{2,1,0:T(8,128)S(1)}) custom-call(s32[32,2]{1,0:T(8,128)S(1)} %copy.26.offs, f32[2,2,256,128]{3,2,1,0:T(8,128)S(1)} %copy.28.ext, f32[32,8]{1,0:T(8,128)S(1)} %broadcast_multiply_fusion.coef), custom_call_target="tpu_custom_call" | custom-call | tf_op jit(solution)/shard_map/cut/pallas_call | solution.py:262
  143.3 2.7 %probes.3 = (f32[4224,128]{1,0:T(8,128)S(1)}, f32[4224,128]{1,0:T(8,128)S(1)}) custom-call(f32[128,8,256]{2,1,0:T(8,128)S(1)} %all-to-all-done.1.modes, f32[32,8]{1,0:T(8,128)S(1)} %broadcast_multiply_fusion.coef), custom_call_target="tpu_custom_call" | custom-call | tf_op jit(solution)/shard_map/probes/pallas_call | solution.py:278
  149.8 13.9 %waves.3 = (f32[256,128]{1,0:T(8,128)S(1)}, f32[256,128]{1,0:T(8,128)S(1)}, f32[256,128]{1,0:T(8,128)S(1)}, f32[256,128]{1,0:T(8,128)S(1)}, f32[256,128]{1,0:T(8...) custom-call(s32[32,2]{1,0:T(8,128)S(1)} %copy.26.offs, ...), custom_call_target="tpu_custom_call" | custom-call | tf_op jit(solution)/shard_map/waves/pallas_call | solution.py:291
  171.0 12.5 %all-to-all-start.2 = ((f32[128,8,384]{2,1,0:T(8,128)}), f32[128,8,384]{2,1,0:T(8,128)}, u32[]{:S(2)}, u32[]{:S(2)}) async-start(f32[128,8,384]{2,1,0:T(8,128)} %pad_maximum_fusion.1), calls=%async_computation.2 | async-start | bytes 3145728 | tf_op jit(solution)/shard_map/all_to_all | solution.py:385
  187.0 19.0 %collective-permute-start.12 = (f32[3,64,256]{2,1,0:T(8,128)S(1)}, f32[3,64,256]{2,1,0:T(8,128)S(1)}, u32[]{:S(2)}, u32[]{:S(2)}) collective-permute-start(f32[3,64,256]{2,1,0:T(8,128)S(1)} %get-tuple-element.66), channel_id=1, source_target_pairs={{0,16},{16,32},{32,48},{48,64},{64,80},{80,96},{96,112},{1,17},{17... | collective-permute-start | bytes 589832 | tf_op jit(solution)/shard_map/ppermute | solution.py:343
  209.9 8.3 %all-to-all-start.3 = ((f32[128,8,256]{2,1,0:T(8,128)}), f32[128,8,256]{2,1,0:T(8,128)}, u32[]{:S(2)}, u32[]{:S(2)}) async-start(f32[128,8,256]{2,1,0:T(8,128)} %broadcast_in_dim.7), calls=%async_computation.3 | async-start | bytes 2097152 | tf_op jit(solution)/shard_map/all_to_all | solution.py:392
  219.1 5.2 %collective-permute-start.15 = (f32[3,128,64]{2,1,0:T(8,128)}, f32[3,128,64]{2,1,0:T(8,128)}, u32[]{:S(2)}, u32[]{:S(2)}) collective-permute-start(f32[3,128,64]{2,1,0:T(8,128)} %get-tuple-element.71), channel_id=1, source_target_pairs={{1,0},{2,1},{3,2},{4,3},{5,4},{6,5},{7,6},{8,7},{9,8},{10,9},{11,1... | collective-permute-start | bytes 294920 | tf_op jit(solution)/shard_map/ppermute | solution.py:344
  231.1 3.8 %coefs.3 = f32[32,8]{1,0:T(8,128)S(1)} custom-call(f32[4224,128]{1,0:T(8,128)S(1)} %copy-done.13, f32[4224,128]{1,0:T(8,128)S(1)} %copy-done.15, f32[4224,128]{1,0:T(8,128)S(1)} %copy-done.11, f32[128,8,256]{2,1,0:T(8,128)S(1)} %all-to-all-done.1.modes, f32[32,8]{1,0:T(8,128)S(1)} %coefs.2.coef), custom_call_target="tpu_custom_call" | custom-call | tf_op jit(solution)/shard_map/coefs/pallas_call | solution.py:319
  240.9 2.5 %copy.30 = f32[8,2,128,128]{3,2,1,0:T(8,128)} copy(f32[8,2,128,128]{3,0,1,2:T(8,128)} %bitcast.28) | data formatting | bytes 2097152
  (139 shorter events, 72.7 us)
Async XLA Ops:
  1.6 8.4 %collective-permute-start.1 = (f32[2,64,128]{2,1,0:T(8,128)S(1)}, f32[2,64,128]{2,1,0:T(8,128)S(1)}, u32[]{:S(2)}, u32[]{:S(2)}) collective-permute-start(f32[2,64,128]{2,1,0:T(8,128)S(1)} %get-tuple-element.87), channel_id=1, source_target_pairs={{16,0},{32,16},{48,32},{64,48},{80,64},{96,80},{112,96},{17,1},{33... | collective-permute-start | bytes 196616 | tf_op jit(solution)/shard_map/ppermute | solution.py:344
  2.9 7.1 %collective-permute-start = (f32[2,64,128]{2,1,0:T(8,128)S(1)}, f32[2,64,128]{2,1,0:T(8,128)S(1)}, u32[]{:S(2)}, u32[]{:S(2)}) collective-permute-start(f32[2,64,128]{2,1,0:T(8,128)S(1)} %get-tuple-element.88), channel_id=1, source_target_pairs={{0,16},{16,32},{32,48},{48,64},{64,80},{80,96},{96,112},{1,17},{17... | collective-permute-start | bytes 196616 | tf_op jit(solution)/shard_map/ppermute | solution.py:343
  10.1 21.8 %copy-start = (s32[1,1,32,128,128]{4,3,2,1,0:T(8,128)S(1)}, s32[1,1,32,128,128]{4,3,2,1,0:T(8,128)}, u32[]{:S(2)}) copy-start(s32[1,1,32,128,128]{4,3,2,1,0:T(8,128)} %param.15) | copy-start | bytes 6291460
  10.2 21.8 %copy-start.16 = (bf16[768,256]{1,0:T(8,128)(2,1)S(1)}, bf16[768,256]{1,0:T(8,128)(2,1)}, u32[]{:S(2)}) copy-start(bf16[768,256]{1,0:T(8,128)(2,1)} %constant.35.clone.back_t) | copy-start | bytes 1179652
  10.2 21.7 %copy-start.17 = (bf16[256,768]{1,0:T(8,128)(2,1)S(1)}, bf16[256,768]{1,0:T(8,128)(2,1)}, u32[]{:S(2)}) copy-start(bf16[256,768]{1,0:T(8,128)(2,1)} %constant.34.clone.ahead_w) | copy-start | bytes 1179652
  10.2 13.1 %collective-permute-start.2 = (f32[2,256,64]{2,1,0:T(8,128)S(1)}, f32[2,256,64]{2,1,0:T(8,128)S(1)}, u32[]{:S(2)}, u32[]{:S(2)}) collective-permute-start(f32[2,256,64]{2,1,0:T(8,128)S(1)} %get-tuple-element.83), channel_id=1, source_target_pairs={{0,1},{1,2},{2,3},{3,4},{4,5},{5,6},{6,7},{7,8},{8,9},{9,10},{10,1... | collective-permute-start | bytes 393224 | tf_op jit(solution)/shard_map/ppermute | solution.py:343
  14.3 10.9 %collective-permute-start.3 = (f32[2,256,64]{2,1,0:T(8,128)S(1)}, f32[2,256,64]{2,1,0:T(8,128)S(1)}, u32[]{:S(2)}, u32[]{:S(2)}) collective-permute-start(f32[2,256,64]{2,1,0:T(8,128)S(1)} %get-tuple-element.84), channel_id=1, source_target_pairs={{1,0},{2,1},{3,2},{4,3},{5,4},{6,5},{7,6},{8,7},{9,8},{10,9},{11,1... | collective-permute-start | bytes 393224 | tf_op jit(solution)/shard_map/ppermute | solution.py:344
  48.7 14.6 %collective-permute-start.5 = (f32[3,64,256]{2,1,0:T(8,128)S(1)}, f32[3,64,256]{2,1,0:T(8,128)}, u32[]{:S(2)}, u32[]{:S(2)}) collective-permute-start(f32[3,64,256]{2,1,0:T(8,128)S(1)} %slice.165), channel_id=1, source_target_pairs={{16,0},{32,16},{48,32},{64,48},{80,64},{96,80},{112,96},{17,1},{33... | collective-permute-start | bytes 589832 | tf_op jit(solution)/shard_map/ppermute | solution.py:344
  51.2 37.2 %all-to-all-start = ((f32[128,8,384]{2,1,0:T(8,128)}), f32[128,8,384]{2,1,0:T(8,128)}, u32[]{:S(2)}, u32[]{:S(2)}) async-start(f32[128,8,384]{2,1,0:T(8,128)} %pad_maximum_fusion), calls=%async_computation | async-start | bytes 3145728 | tf_op jit(solution)/shard_map/all_to_all | solution.py:385
  64.3 3.1 %collective-permute-start.4 = (f32[3,64,256]{2,1,0:T(8,128)S(1)}, f32[3,64,256]{2,1,0:T(8,128)S(1)}, u32[]{:S(2)}, u32[]{:S(2)}) collective-permute-start(f32[3,64,256]{2,1,0:T(8,128)S(1)} %get-tuple-element.68), channel_id=1, source_target_pairs={{0,16},{16,32},{32,48},{48,64},{64,80},{80,96},{96,112},{1,17},{17... | collective-permute-start | bytes 589832 | tf_op jit(solution)/shard_map/ppermute | solution.py:343
  67.5 16.8 %collective-permute-start.7 = (f32[3,128,64]{2,1,0:T(8,128)S(1)}, f32[3,128,64]{2,1,0:T(8,128)S(1)}, u32[]{:S(2)}, u32[]{:S(2)}) collective-permute-start(f32[3,128,64]{2,1,0:T(8,128)S(1)} %get-tuple-element.75), channel_id=1, source_target_pairs={{1,0},{2,1},{3,2},{4,3},{5,4},{6,5},{7,6},{8,7},{9,8},{10,9},{11,1... | collective-permute-start | bytes 294920 | tf_op jit(solution)/shard_map/ppermute | solution.py:344
  72.8 14.4 %collective-permute-start.6 = (f32[3,128,64]{2,1,0:T(8,128)S(1)}, f32[3,128,64]{2,1,0:T(8,128)S(1)}, u32[]{:S(2)}, u32[]{:S(2)}) collective-permute-start(f32[3,128,64]{2,1,0:T(8,128)S(1)} %get-tuple-element.76), channel_id=1, source_target_pairs={{0,1},{1,2},{2,3},{3,4},{4,5},{5,6},{6,7},{7,8},{8,9},{9,10},{10,1... | collective-permute-start | bytes 294920 | tf_op jit(solution)/shard_map/ppermute | solution.py:343
  91.0 52.2 %all-to-all-start.1 = ((f32[128,8,256]{2,1,0:T(8,128)}), f32[128,8,256]{2,1,0:T(8,128)S(1)}, u32[]{:S(2)}, u32[]{:S(2)}) async-start(f32[128,8,256]{2,1,0:T(8,128)} %broadcast_in_dim.6), calls=%async_computation.1 | async-start | bytes 2097152 | tf_op jit(solution)/shard_map/all_to_all | solution.py:392
  108.7 11.9 %collective-permute-start.8 = (f32[2,64,128]{2,1,0:T(8,128)S(1)}, f32[2,64,128]{2,1,0:T(8,128)S(1)}, u32[]{:S(2)}, u32[]{:S(2)}) collective-permute-start(f32[2,64,128]{2,1,0:T(8,128)S(1)} %get-tuple-element.85), channel_id=1, source_target_pairs={{0,16},{16,32},{32,48},{48,64},{64,80},{80,96},{96,112},{1,17},{17... | collective-permute-start | bytes 196616 | tf_op jit(solution)/shard_map/ppermute | solution.py:343
  110.7 9.9 %collective-permute-start.9 = (f32[2,64,128]{2,1,0:T(8,128)S(1)}, f32[2,64,128]{2,1,0:T(8,128)S(1)}, u32[]{:S(2)}, u32[]{:S(2)}) collective-permute-start(f32[2,64,128]{2,1,0:T(8,128)S(1)} %get-tuple-element.86), channel_id=1, source_target_pairs={{16,0},{32,16},{48,32},{64,48},{80,64},{96,80},{112,96},{17,1},{33... | collective-permute-start | bytes 196616 | tf_op jit(solution)/shard_map/ppermute | solution.py:344
  120.8 12.1 %collective-permute-start.10 = (f32[2,256,64]{2,1,0:T(8,128)S(1)}, f32[2,256,64]{2,1,0:T(8,128)S(1)}, u32[]{:S(2)}, u32[]{:S(2)}) collective-permute-start(f32[2,256,64]{2,1,0:T(8,128)S(1)} %get-tuple-element.79), channel_id=1, source_target_pairs={{0,1},{1,2},{2,3},{3,4},{4,5},{5,6},{6,7},{7,8},{8,9},{9,10},{10,1... | collective-permute-start | bytes 393224 | tf_op jit(solution)/shard_map/ppermute | solution.py:343
  124.3 10.3 %collective-permute-start.11 = (f32[2,256,64]{2,1,0:T(8,128)S(1)}, f32[2,256,64]{2,1,0:T(8,128)S(1)}, u32[]{:S(2)}, u32[]{:S(2)}) collective-permute-start(f32[2,256,64]{2,1,0:T(8,128)S(1)} %get-tuple-element.80), channel_id=1, source_target_pairs={{1,0},{2,1},{3,2},{4,3},{5,4},{6,5},{7,6},{8,7},{9,8},{10,9},{11,1... | collective-permute-start | bytes 393224 | tf_op jit(solution)/shard_map/ppermute | solution.py:344
  171.0 36.3 %all-to-all-start.2 = ((f32[128,8,384]{2,1,0:T(8,128)}), f32[128,8,384]{2,1,0:T(8,128)}, u32[]{:S(2)}, u32[]{:S(2)}) async-start(f32[128,8,384]{2,1,0:T(8,128)} %pad_maximum_fusion.1), calls=%async_computation.2 | async-start | bytes 3145728 | tf_op jit(solution)/shard_map/all_to_all | solution.py:385
  183.6 3.3 %collective-permute-start.13 = (f32[3,64,256]{2,1,0:T(8,128)S(1)}, f32[3,64,256]{2,1,0:T(8,128)S(1)}, u32[]{:S(2)}, u32[]{:S(2)}) collective-permute-start(f32[3,64,256]{2,1,0:T(8,128)S(1)} %slice.183), channel_id=1, source_target_pairs={{16,0},{32,16},{48,32},{64,48},{80,64},{96,80},{112,96},{17,1},{33... | collective-permute-start | bytes 589832 | tf_op jit(solution)/shard_map/ppermute | solution.py:344
  187.0 31.3 %copy-start.32 = (f32[3,64,256]{2,1,0:T(8,128)}, f32[3,64,256]{2,1,0:T(8,128)S(1)}, u32[]{:S(2)}) copy-start(f32[3,64,256]{2,1,0:T(8,128)S(1)} %get-tuple-element.65) | copy-start | bytes 589828
  187.0 31.2 %collective-permute-start.12 = (f32[3,64,256]{2,1,0:T(8,128)S(1)}, f32[3,64,256]{2,1,0:T(8,128)S(1)}, u32[]{:S(2)}, u32[]{:S(2)}) collective-permute-start(f32[3,64,256]{2,1,0:T(8,128)S(1)} %get-tuple-element.66), channel_id=1, source_target_pairs={{0,16},{16,32},{32,48},{48,64},{64,80},{80,96},{96,112},{1,17},{17... | collective-permute-start | bytes 589832 | tf_op jit(solution)/shard_map/ppermute | solution.py:343
  209.9 31.0 %all-to-all-start.3 = ((f32[128,8,256]{2,1,0:T(8,128)}), f32[128,8,256]{2,1,0:T(8,128)}, u32[]{:S(2)}, u32[]{:S(2)}) async-start(f32[128,8,256]{2,1,0:T(8,128)} %broadcast_in_dim.7), calls=%async_computation.3 | async-start | bytes 2097152 | tf_op jit(solution)/shard_map/all_to_all | solution.py:392
  219.1 17.2 %collective-permute-start.15 = (f32[3,128,64]{2,1,0:T(8,128)}, f32[3,128,64]{2,1,0:T(8,128)}, u32[]{:S(2)}, u32[]{:S(2)}) collective-permute-start(f32[3,128,64]{2,1,0:T(8,128)} %get-tuple-element.71), channel_id=1, source_target_pairs={{1,0},{2,1},{3,2},{4,3},{5,4},{6,5},{7,6},{8,7},{9,8},{10,9},{11,1... | collective-permute-start | bytes 294920 | tf_op jit(solution)/shard_map/ppermute | solution.py:344
  224.3 14.4 %collective-permute-start.14 = (f32[3,128,64]{2,1,0:T(8,128)}, f32[3,128,64]{2,1,0:T(8,128)}, u32[]{:S(2)}, u32[]{:S(2)}) collective-permute-start(f32[3,128,64]{2,1,0:T(8,128)} %get-tuple-element.72), channel_id=1, source_target_pairs={{0,1},{1,2},{2,3},{3,4},{4,5},{5,6},{6,7},{7,8},{8,9},{9,10},{10,1... | collective-permute-start | bytes 294920 | tf_op jit(solution)/shard_map/ppermute | solution.py:343
  (30 other events, 170.1 us)

commit v3 on v2

v3 whole, which is shorter than its diff:
```python
import functools
import math

import jax
import jax.numpy as jnp
import numpy as np
from jax import lax
from jax.experimental import pallas as pl
from jax.experimental.pallas import tpu as pltpu
from jax.sharding import PartitionSpec as P

PS = 128
MODES = 8
TILE = 128
PMAX = 32
ITERS = 2
EXT = TILE + PS
F32 = jnp.float32
BF16 = jnp.bfloat16
PAIRS = 4
LEAD = 33
ROWS = PS // 2


def split(x):
    hi = x.astype(BF16)
    lo = (x - hi.astype(F32)).astype(BF16)
    return hi, lo


def triple(x, axis):
    hi, lo = split(x)
    return jnp.concatenate([hi, lo, hi], axis=axis)


def dft_constants():
    ramp = np.arange(PS)
    angles = (ramp[:, None] * ramp[None, :] % PS) * (2.0 * math.pi / PS)
    cos = np.cos(angles) / math.sqrt(PS)
    sin = -np.sin(angles) / math.sqrt(PS)
    ahead = np.block([[cos, sin], [-sin, cos]])
    back = np.block([[cos, -sin], [sin, cos]])

    def parts(table):
        table = table.astype(np.float32)
        hi = table.astype(jnp.bfloat16)
        lo = (table - hi.astype(np.float32)).astype(jnp.bfloat16)
        return hi, lo

    def tall(table):
        hi, lo = parts(table)
        return np.concatenate([hi, hi, lo], axis=0)

    def wide(table):
        hi, lo = parts(table)
        return np.concatenate([hi, hi, lo], axis=1)

    return tall(ahead), wide(back), wide(ahead), tall(back)


def dot(a, b):
    return jnp.dot(a, b, preferred_element_type=F32)


def probe_kernel(half, near, far, coef, probe_r, probe_i):
    left = triple(coef[...], 1)
    for source, base in ((near, half[0] * ROWS), (far, (1 - half[0]) * ROWS)):

        def rows(y, _):
            m = source[y]
            h = m.astype(BF16).astype(F32)
            right = jnp.concatenate([h, h, m - h], axis=0).astype(BF16)
            out = dot(left, right)
            start = (base + y) * LEAD
            probe_r[pl.ds(start, PMAX), :] = out[:, :PS]
            probe_i[pl.ds(start, PMAX), :] = out[:, PS:]
            return 0

        lax.fori_loop(0, ROWS, rows, 0, unroll=8)


def wave_kernel(
    half, offs, ext, photons, probe_r, probe_i, coef, ahead_t, back_w, ahead_w, back_t,
    acc_rl, acc_rh, acc_il, acc_ih, acc_pl, acc_ph, out_r, out_i, out_p, near, far,
    patches, wave, field, cross_r, cross_i, power, sems,
):
    step = pl.program_id(0)
    lane = lax.broadcasted_iota(jnp.int32, (PS, PS), 1)
    sums = ((acc_rl, acc_rh), (acc_il, acc_ih), (acc_pl, acc_ph))

    @pl.when(step == 0)
    def _():
        for low, high in sums:
            low[...] = jnp.zeros_like(low)
            high[...] = jnp.zeros_like(high)

    def regroup(x):
        top = jnp.concatenate([x[:PS, :PS], x[PS:, :PS]], axis=1)
        low = jnp.concatenate([x[:PS, PS:], x[PS:, PS:]], axis=1)
        return jnp.concatenate([top, low], axis=0)

    def take(j, q):
        p = 2 * PAIRS * step + 2 * j + q
        return (
            probe_r[pl.ds(p, PS, stride=LEAD), :],
            probe_i[pl.ds(p, PS, stride=LEAD), :],
            patches[2 * j + q, 0],
            patches[2 * j + q, 1],
        )

    def cut(j, q):
        p = 2 * PAIRS * step + 2 * j + q
        top = offs[p, 0]
        left = offs[p, 1]
        turn = (PS - left) & (PS - 1)
        inside = lane < PS - left
        total = None
        for c in range(2):
            a = pltpu.roll(ext[c, 0, pl.ds(top, PS), :], turn, 1)
            b = pltpu.roll(ext[c, 1, pl.ds(top, PS), :], turn, 1)
            patch = jnp.where(inside, a, b)
            patches[2 * j + q, c] = patch
            total = patch * patch if total is None else total + patch * patch
        power[pl.ds(p, PS, stride=LEAD), :] = total

    def start(j):
        for q in range(2):
            cut(j, q)
            pr, pi, obj_r, obj_i = take(j, q)
            rows = slice(q * PS, (q + 1) * PS)
            wave[j, rows, :PS] = pr * obj_r - pi * obj_i
            wave[j, rows, PS:] = pr * obj_i + pi * obj_r

    def correct(j, there):
        count = jnp.concatenate([photons[2 * j], photons[2 * j + 1]], axis=1).astype(F32)
        far_r = there[:PS]
        far_i = there[PS:]
        size = jnp.maximum(far_r * far_r + far_i * far_i, 0.25)
        scale = count * lax.rsqrt(jnp.maximum(count * size, 0.0625)) * 0.03125
        return jnp.concatenate([far_r * scale, far_i * scale], axis=0)

    def finish(j):
        for q in range(2):
            p = 2 * PAIRS * step + 2 * j + q
            top = offs[p, 0]
            left = offs[p, 1]
            turn = left & (PS - 1)
            inside = lane >= left
            rows = slice(q * PS, (q + 1) * PS)
            diff_r = field[j, rows, :PS]
            diff_i = field[j, rows, PS:]
            pr, pi, obj_r, obj_i = take(j, q)
            cross_r[pl.ds(p, PS, stride=LEAD), :] = obj_r * diff_r + obj_i * diff_i
            cross_i[pl.ds(p, PS, stride=LEAD), :] = obj_r * diff_i - obj_i * diff_r
            pieces = (
                pr * diff_r + pi * diff_i,
                pr * diff_i - pi * diff_r,
                pr * pr + pi * pi,
            )
            for (low, high), piece in zip(sums, pieces):
                turned = pltpu.roll(piece, turn, 1)
                near = jnp.where(inside, turned, 0.0)
                low[pl.ds(top, PS), :] += near
                high[pl.ds(top, PS), :] += turned - near

    pairs = range(PAIRS)
    for j in pairs:
        start(j)
    x = [dot(triple(wave[j], 1), ahead_t[...]) for j in pairs]
    x = [dot(back_w[...], triple(regroup(x[j]), 0)) for j in pairs]
    x = [correct(j, x[j]) for j in pairs]
    x = [dot(ahead_w[...], triple(x[j], 0)) for j in pairs]
    for j in pairs:
        field[j] = dot(triple(regroup(x[j]), 1), back_t[...]) - wave[j]
    for j in pairs:
        finish(j)

    @pl.when(step == PMAX // (2 * PAIRS) - 1)
    def _():
        copies = [
            pltpu.make_async_copy(source, target, sems.at[i])
            for i, (source, target) in enumerate(
                ((cross_r, out_r), (cross_i, out_i), (power, out_p))
            )
        ]
        for copy in copies:
            copy.start()

        def stacked(x):
            hi, lo = split(x.T)
            zero = jnp.zeros_like(hi)
            return jnp.concatenate(
                [jnp.concatenate([hi, hi], axis=1), jnp.concatenate([lo, zero], axis=1)], axis=0
            )

        left = stacked(coef[...])
        left_square = stacked(coef[...] * coef[...])
        for target, base in ((near, half[0] * ROWS), (far, (1 - half[0]) * ROWS)):

            def rows(y, _):
                begin = (base + y) * LEAD
                pair = jnp.concatenate(
                    [cross_r[pl.ds(begin, PMAX), :], cross_i[pl.ds(begin, PMAX), :]], axis=1
                )
                h, l = split(pair)
                out = dot(left, jnp.concatenate([h, l], axis=0))
                target[y, :, : 2 * PS] = out[:MODES] + out[MODES:]
                h, l = split(power[pl.ds(begin, PMAX), :])
                out = dot(left_square, jnp.concatenate([h, l], axis=0))
                target[y, :, 2 * PS:] = out[:MODES] + out[MODES:]
                return 0

            lax.fori_loop(0, ROWS, rows, 0, unroll=8)
        for copy in copies:
            copy.wait()


CHUNK = 16


def coef_kernel(cross_r, cross_i, powers, modes, coef, out, num, den):
    step = pl.program_id(0)

    @pl.when(step == 0)
    def _():
        num[...] = jnp.zeros_like(num)
        den[...] = jnp.zeros_like(den)

    dims = (((1,), (1,)), ((), ()))

    def wide_dot(a, b):
        return lax.dot_general(a, b, dims, preferred_element_type=F32)

    top = jnp.zeros((PMAX, MODES), F32)
    low = jnp.zeros((PMAX, MODES), F32)
    for y in range(CHUNK):
        rows = slice(y * LEAD, y * LEAD + PMAX)
        cross = jnp.concatenate([cross_r[rows, :], cross_i[rows, :]], axis=1)
        m = modes[y]
        power = m[:, :PS] * m[:, :PS] + m[:, PS:] * m[:, PS:]
        h, l = split(m)
        top += wide_dot(triple(cross, 1), jnp.concatenate([h, h, l], axis=1))
        h, l = split(power)
        low += wide_dot(triple(powers[rows, :], 1), jnp.concatenate([h, h, l], axis=1))
    num[...] += top
    den[...] += low

    @pl.when(step == PS // CHUNK - 1)
    def _():
        out[...] = coef[...] + num[...] / (den[...] + 1.0)


SMEM = pl.BlockSpec(memory_space=pltpu.SMEM)
VMEM = pl.BlockSpec(memory_space=pltpu.VMEM)


def mix_probes(half, near, far, coef):
    grid = jax.ShapeDtypeStruct((PS * LEAD, PS), F32)
    return pl.pallas_call(
        probe_kernel,
        out_shape=(grid, grid),
        in_specs=[SMEM, VMEM, VMEM, VMEM],
        out_specs=(VMEM, VMEM),
        compiler_params=pltpu.CompilerParams(vmem_limit_bytes=2 << 20),
        name="probes",
    )(half, near, far, coef)


def waves(half, offs, ext, photons, probe_r, probe_i, coef, tables):
    part = jax.ShapeDtypeStruct((EXT, PS), F32)
    grid = jax.ShapeDtypeStruct((PS * LEAD, PS), F32)
    rows = jax.ShapeDtypeStruct((ROWS, MODES, 3 * PS), F32)
    square = pltpu.VMEM((PAIRS, 2 * PS, 2 * PS), F32)
    return pl.pallas_call(
        wave_kernel,
        grid=(PMAX // (2 * PAIRS),),
        out_shape=(*[part] * 6, *[grid] * 3, rows, rows),
        in_specs=[
            SMEM,
            SMEM,
            VMEM,
            pl.BlockSpec((2 * PAIRS, PS, PS), lambda i: (i, 0, 0)),
            VMEM,
            VMEM,
            VMEM,
            *[VMEM] * len(tables),
        ],
        out_specs=(*[VMEM] * 6, *[pl.BlockSpec(memory_space=pl.ANY)] * 3, VMEM, VMEM),
        scratch_shapes=[
            pltpu.VMEM((2 * PAIRS, 2, PS, PS), F32),
            square,
            square,
            *[pltpu.VMEM((PS * LEAD, PS), F32)] * 3,
            pltpu.SemaphoreType.DMA((3,)),
        ],
        compiler_params=pltpu.CompilerParams(
            dimension_semantics=("arbitrary",), vmem_limit_bytes=24 << 20
        ),
        name="waves",
    )(half, offs, ext, photons, probe_r, probe_i, coef, *tables)


def new_coefficients(cross_r, cross_i, powers, modes, coef):
    rows = pl.BlockSpec((CHUNK * LEAD, PS), lambda i: (i, 0))
    whole = pl.BlockSpec((PMAX, MODES), lambda i: (0, 0))
    return pl.pallas_call(
        coef_kernel,
        grid=(PS // CHUNK,),
        out_shape=jax.ShapeDtypeStruct((PMAX, MODES), F32),
        in_specs=[
            rows,
            rows,
            rows,
            pl.BlockSpec((CHUNK, MODES, 2 * PS), lambda i: (i, 0, 0)),
            whole,
        ],
        out_specs=whole,
        scratch_shapes=[pltpu.VMEM((PMAX, MODES), F32)] * 2,
        compiler_params=pltpu.CompilerParams(
            dimension_semantics=("arbitrary",), vmem_limit_bytes=6 << 20
        ),
        name="coefs",
    )(cross_r, cross_i, powers, modes, coef)


def shifted(x, move):
    rows, cols = lax.axis_size("row"), lax.axis_size("col")
    pairs = []
    for a in range(rows):
        for b in range(cols):
            c, d = a + move[0], b + move[1]
            if 0 <= c < rows and 0 <= d < cols:
                pairs.append((c * cols + d, a * cols + b))
    return lax.ppermute(x, ("row", "col"), pairs)


def extend(block):
    margin = PS // 2
    ends = {-1: slice(PS - margin, PS), 0: slice(0, PS), 1: slice(0, margin)}
    rows = []
    for a in (-1, 0, 1):
        row = [
            block if (a, b) == (0, 0) else shifted(block[:, ends[a], ends[b]], (a, b))
            for b in (-1, 0, 1)
        ]
        rows.append(jnp.concatenate(row, axis=2))
    full = jnp.concatenate(rows, axis=1)
    return jnp.stack([full[:, :, :PS], full[:, :, PS:]], axis=1)


def sum_extended(acc):
    low = shifted(jnp.stack([x[PS:] for x in acc]), (-1, 0))
    high = shifted(jnp.stack([x[:PS] for x in acc]), (1, 0))
    left = jnp.concatenate([jnp.stack(acc[::2])[:, :PS] + low[::2], jnp.stack(acc[::2])[:, PS:] + high[::2]], axis=1)
    right = jnp.concatenate([jnp.stack(acc[1::2])[:, :PS] + low[1::2], jnp.stack(acc[1::2])[:, PS:] + high[1::2]], axis=1)
    return jnp.stack([left + shifted(right, (0, -1)), right + shifted(left, (0, 1))], axis=1)


def inside_object():
    margin = PS // 2

    def axis(name, count):
        place = lax.axis_index(name) * TILE - margin + lax.iota(jnp.int32, EXT)
        return (place >= 0) & (place < count * TILE)

    rows = axis("row", lax.axis_size("row"))
    cols = axis("col", lax.axis_size("col")).reshape(2, 1, PS)
    return rows[None, :, None] & cols


def fold(acc):
    margin = PS // 2
    full = jnp.concatenate([jnp.stack(acc[::2]), jnp.stack(acc[1::2])], axis=2)
    low = shifted(full[:, -margin:], (-1, 0))
    high = shifted(full[:, :margin], (1, 0))
    mid = full[:, margin:-margin]
    mid = jnp.concatenate([mid[:, :margin] + low, mid[:, margin:] + high], axis=1)
    low = shifted(mid[:, :, -margin:], (0, -1))
    high = shifted(mid[:, :, :margin], (0, 1))
    mid = mid[:, :, margin:-margin]
    return jnp.concatenate([mid[:, :, :margin] + low, mid[:, :, margin:] + high], axis=2)


def shards(object_field, probe_modes, coefficients, offsets, counts, measured):
    tables = tuple(jnp.asarray(t) for t in dft_constants())
    offs = offsets[0, 0]
    photons = measured[0, 0]
    coef = coefficients[0, 0]
    live = (lax.iota(jnp.int32, PMAX) < counts[0, 0]).astype(F32)[:, None]
    rows, cols = lax.axis_size("row"), lax.axis_size("col")
    core = lax.axis_index("row") % 2
    half = core.reshape(1)
    groups = [[a * cols + b for a in range(k, rows, 2) for b in range(cols)] for k in range(2)]
    mates = [(a, a ^ 1) for a in range(rows)]
    place = lax.axis_index("row") // 2 * cols + lax.axis_index("col")

    def exchange(x):
        return lax.all_to_all(x, ("row", "col"), 0, 0, axis_index_groups=groups, tiled=True)

    modes = probe_modes.transpose(2, 0, 1, 3).reshape(PS, MODES, 2 * PS)
    near = lax.dynamic_slice_in_dim(modes, core * ROWS, ROWS, 0)
    far = lax.dynamic_slice_in_dim(modes, (1 - core) * ROWS, ROWS, 0)
    mine = lax.dynamic_index_in_dim(near, place, 0, keepdims=False)
    ext = extend(object_field)
    for iteration in range(ITERS):
        used = coef * live
        probe_r, probe_i = mix_probes(half, near, far, used)
        *acc, cross_r, cross_i, powers, kept, given = waves(
            half, offs, ext, photons, probe_r, probe_i, used, tables
        )
        sent = kept + lax.ppermute(given, "row", mates)
        total = jnp.sum(exchange(sent), axis=0)
        power = total[:, 2 * PS:] + 1.0
        mine = mine + total[:, : 2 * PS] / jnp.concatenate([power, power], axis=1)
        near = exchange(jnp.broadcast_to(mine[None], (ROWS, MODES, 2 * PS)))
        far = lax.ppermute(near, "row", mates)
        coef = new_coefficients(cross_r, cross_i, powers, modes, coef)
        modes = jnp.where(
            core == 0, jnp.concatenate([near, far]), jnp.concatenate([far, near])
        )
        if iteration < ITERS - 1:
            total = sum_extended(acc)
            step = total[0:2] / (total[2:3] + 1.0)
            ext = ext + jnp.where(inside_object()[None], step, 0.0)
        else:
            margin = PS // 2
            field = jnp.concatenate(
                [ext[:, 0, margin:-margin, margin:], ext[:, 1, margin:-margin, :margin]], axis=2
            )
            total = fold(acc)
            object_field = field + total[0:2] / (total[2:3] + 1.0)
    probe_modes = modes.reshape(PS, MODES, 2, PS).transpose(1, 2, 0, 3)
    return (object_field, probe_modes, coef[None, None])


def solution(mesh):
    placed = (
        P(None, "row", "col"),
        P(),
        P("row", "col", None, None),
        P("row", "col", None, None),
        P("row", "col"),
        P("row", "col", None, None, None),
    )
    return jax.shard_map(
        shards,
        mesh=mesh,
        in_specs=placed,
        out_specs=(P(None, "row", "col"), P(), P("row", "col", None, None)),
        check_vma=False,
    )
```

time: 245 us -> 228 us (0.931)
  waiting for transfers between devices: 29.8 us -> 8.38 us
  other arithmetic: 11.9 us -> 27.5 us
  starting transfers between devices: 112 us -> 99.6 us
  local copies, waits for them, and re-layouts: 36.9 us -> 41.6 us
  Pallas kernels: 50.7 us -> 46.6 us
    ppermute x16 -> x20, waiting for transfers between devices: 28.5 us -> 4.05 us  [the longest x16 2.07 us: shifted(): return lax.ppermute(x, ('row', 'col'), pairs)]
    all_to_all x4, starting transfers between devices: 50.4 us -> 35.6 us  [exchange(): lax.all_to_all(x, ('row', 'col'), 0, 0, axis_index_groups=groups, tiled=T...]
    add x2 -> x5, other arithmetic: 1.78 us -> 6.07 us  [the longest x1 2.05 us: sum_extended(): jnp.stack(acc[::2])[:, :PS] + low[::2]]
    pallas_call x6 -> x4, Pallas kernels: 43.1 us -> 39.1 us  [the longest x2 32.4 us: waves(): pl.pallas_call(wave_kernel, grid=(PMAX // (2 * PAIRS),), out_shape=(*[par...]
    another operation x4, other arithmetic: 0.61 us -> 4.61 us  [the longest x2 3.32 us: sum_extended(): jnp.stack([left + shifted(right, (0, -1)), right + shifted(left, (0, 1))]...]
    slice x6 -> x4, local copies, waits for them, and re-layouts: 1.22 us -> 4.87 us  [the longest x3 4.86 us: extend(): block[:, ends[a], ends[b]]]
    all_to_all x4, waiting for transfers between devices: 1.27 us -> 4.34 us  [exchange(): lax.all_to_all(x, ('row', 'col'), 0, 0, axis_index_groups=groups, tiled=T...]
    ppermute x16 -> x20, starting transfers between devices: 61.7 us -> 64 us  [the longest x16 58.7 us: shifted(): return lax.ppermute(x, ('row', 'col'), pairs)]
  transfers between devices with their start and end apart: 20 -> 24, of which waited for: 11 -> 4; matrix products, arithmetic and copies ran while one was open for 6% -> 17% of each run, Pallas kernels for 6% -> 5%
where the time goes in v3:
time: 228 us; the launch traced here: 226 us
  starting transfers between devices  99.6 us (44%)
  Pallas kernels  46.6 us (20%)
  local copies, waits for them, and re-layouts  41.6 us (18%)
  other arithmetic  27.5 us (12%)
  waiting for transfers between devices  8.38 us (4%)
    ppermute x16, starting transfers between devices, shifted(): return lax.ppermute(x, ('row', 'col'), pairs)  58.7 us
    all_to_all x4, starting transfers between devices, exchange(): lax.all_to_all(x, ('row', 'col'), 0, 0, axis_index_groups=groups, tiled=T...  35.6 us
    pallas_call x2, Pallas kernels, waves(): pl.pallas_call(wave_kernel, grid=(PMAX // (2 * PAIRS),), out_shape=(*[par...  32.4 us
    unnamed x134, local copies, waits for them, and re-layouts  30.8 us
    pallas_call x2, Pallas kernels, new_coefficients(): pl.pallas_call(coef_kernel, grid=(PS // CHUNK,), out_shape=jax.ShapeDtype...  7.53 us
    pallas_call x2, Pallas kernels, mix_probes(): pl.pallas_call(probe_kernel, out_shape=(grid, grid), in_specs=[SMEM, VMEM...  6.65 us
    ppermute x2, starting transfers between devices, shards(): sent = kept + lax.ppermute(given, 'row', mates)  5.3 us
    slice x3, local copies, waits for them, and re-layouts, extend(): block[:, ends[a], ends[b]]  4.86 us
  transfers between devices with their start and end apart: 24, of which 4 were waited for; matrix products, arithmetic and copies ran while one was open for 17% of the time, Pallas kernels for 5%

profile of v3, /device:TPU:2, one launch (start us, length us, event | category | flops | bytes accessed | tf_op | source)
XLA Modules:
  0.0 225.9 jit_solution(1346154191258909960)
XLA Ops:
  2.2 3.3 %collective-permute-start = (f32[2,64,64]{2,1,0:T(8,128)S(1)}, f32[2,64,64]{2,1,0:T(8,128)S(1)}, u32[]{:S(2)}, u32[]{:S(2)}) collective-permute-start(f32[2,64,64]{2,1,0:T(8,128)S(1)} %get-tuple-element.91), channel_id=1, source_target_pairs={{0,17},{1,18},{2,19},{3,20},{4,21},{5,22},{6,23},{7,24},{8,25},{9,... | collective-permute-start | bytes 98312 | tf_op jit(solution)/shard_map/ppermute | solution.py:334
  5.5 5.4 %collective-permute-start.2 = (f32[2,64,64]{2,1,0:T(8,128)S(1)}, f32[2,64,64]{2,1,0:T(8,128)S(1)}, u32[]{:S(2)}, u32[]{:S(2)}) collective-permute-start(f32[2,64,64]{2,1,0:T(8,128)S(1)} %get-tuple-element.93), channel_id=1, source_target_pairs={{1,16},{2,17},{3,18},{4,19},{5,20},{6,21},{7,22},{8,23},{9,24},{10... | collective-permute-start | bytes 98312 | tf_op jit(solution)/shard_map/ppermute | solution.py:334
  22.7 6.0 %collective-permute-start.4 = (f32[2,128,64]{2,1,0:T(8,128)}, f32[2,128,64]{2,1,0:T(8,128)}, u32[]{:S(2)}, u32[]{:S(2)}) collective-permute-start(f32[2,128,64]{2,1,0:T(8,128)} %get-tuple-element.98), channel_id=1, source_target_pairs={{1,0},{2,1},{3,2},{4,3},{5,4},{6,5},{7,6},{8,7},{9,8},{10,9},{11,1... | collective-permute-start | bytes 196616 | tf_op jit(solution)/shard_map/ppermute | solution.py:334
  28.8 4.6 %collective-permute-start.1 = (f32[2,64,128]{2,1,0:T(8,128)}, f32[2,64,128]{2,1,0:T(8,128)}, u32[]{:S(2)}, u32[]{:S(2)}) collective-permute-start(f32[2,64,128]{2,1,0:T(8,128)} %get-tuple-element.95), channel_id=1, source_target_pairs={{0,16},{1,17},{2,18},{3,19},{4,20},{5,21},{6,22},{7,23},{8,24},{9,... | collective-permute-start | bytes 196616 | tf_op jit(solution)/shard_map/ppermute | solution.py:334
  38.6 2.7 %probes.2 = (f32[4224,128]{1,0:T(8,128)S(1)}, f32[4224,128]{1,0:T(8,128)S(1)}) custom-call(s32[1]{0:T(128)} %bitcast.3.half, f32[64,8,256]{2,1,0:T(8,128)S(1)} %copy-done.16, f32[64,8,256]{2,1,0:T(8,128)S(1)} %copy-done.15, f32[32,8]{1,0:T(8,128)S(1)} %copy-done.30), custom_call_target="tpu_custom_call" | custom-call | tf_op jit(solution)/shard_map/probes/pallas_call | solution.py:259
  43.8 16.2 %waves.2 = (f32[256,128]{1,0:T(8,128)S(1)}, f32[256,128]{1,0:T(8,128)S(1)}, f32[256,128]{1,0:T(8,128)S(1)}, f32[256,128]{1,0:T(8,128)S(1)}, f32[256,128]{1,0:T(8...) custom-call(s32[1]{0:T(128)} %bitcast.3.half, ...), custom_call_target="tpu_custom_call" | custom-call | tf_op jit(solution)/shard_map/waves/pallas_call | solution.py:274
  64.1 4.7 %collective-permute-start.12 = (f32[64,8,384]{2,1,0:T(8,128)S(1)}, f32[64,8,384]{2,1,0:T(8,128)S(1)}, u32[]{:S(2)}, u32[]{:S(2)}) collective-permute-start(f32[64,8,384]{2,1,0:T(8,128)S(1)} %get-tuple-element.38), channel_id=1, source_target_pairs={{0,16},{16,0},{32,48},{48,32},{64,80},{80,64},{96,112},{112,96},{1... | collective-permute-start | bytes 2359304 | tf_op jit(solution)/shard_map/ppermute | solution.py:411
  72.8 3.2 %collective-permute-start.8 = (f32[6,128,128]{2,1,0:T(8,128)}, f32[6,128,128]{2,1,0:T(8,128)}, u32[]{:S(2)}, u32[]{:S(2)}) collective-permute-start(f32[6,128,128]{2,1,0:T(8,128)} %get-tuple-element.79), channel_id=1, source_target_pairs={{0,16},{1,17},{2,18},{3,19},{4,20},{5,21},{6,22},{7,23},{8,24},{9,... | collective-permute-start | bytes 1179656 | tf_op jit(solution)/shard_map/ppermute | solution.py:334
  78.3 9.8 %all-to-all-start = ((f32[64,8,384]{2,1,0:T(8,128)}), f32[64,8,384]{2,1,0:T(8,128)}, u32[]{:S(2)}, u32[]{:S(2)}) async-start(f32[64,8,384]{2,1,0:T(8,128)} %add.132), calls=%async_computation | async-start | bytes 1572864 | tf_op jit(solution)/shard_map/all_to_all | solution.py:398
  90.4 2.1 slice_add_fusion.5
  93.9 4.6 %collective-permute-start.11 = (f32[3,256,128]{2,1,0:T(8,128)}, f32[3,256,128]{2,1,0:T(8,128)}, u32[]{:S(2)}, u32[]{:S(2)}) collective-permute-start(f32[3,256,128]{2,1,0:T(8,128)} %pad_maximum_fusion.2), channel_id=1, source_target_pairs={{1,0},{2,1},{3,2},{4,3},{5,4},{6,5},{7,6},{8,7},{9,8},{10,9},{11,1... | collective-permute-start | bytes 1179656 | tf_op jit(solution)/shard_map/ppermute | solution.py:334
  98.5 4.3 %all-to-all-done = f32[64,8,384]{2,1,0:T(8,128)} async-done(((f32[64,8,384]{2,1,0:T(8,128)}), f32[64,8,384]{2,1,0:T(8,128)}, u32[]{:S(2)}, u32[]{:S(2)}) %all-to-all-start) | async-done | bytes 786464 | tf_op jit(solution)/shard_map/all_to_all | solution.py:398
  107.5 6.3 %all-to-all-start.1 = ((f32[64,8,256]{2,1,0:T(8,128)}), f32[64,8,256]{2,1,0:T(8,128)}, u32[]{:S(2)}, u32[]{:S(2)}) async-start(f32[64,8,256]{2,1,0:T(8,128)} %broadcast_in_dim.32), calls=%async_computation.1 | async-start | bytes 1048576 | tf_op jit(solution)/shard_map/all_to_all | solution.py:398
  113.8 2.1 add_bitcast_fusion
  116.0 3.4 %collective-permute-start.10 = (f32[3,256,128]{2,1,0:T(8,128)}, f32[3,256,128]{2,1,0:T(8,128)}, u32[]{:S(2)}, u32[]{:S(2)}) collective-permute-start(f32[3,256,128]{2,1,0:T(8,128)} %get-tuple-element.74), channel_id=1, source_target_pairs={{0,1},{1,2},{2,3},{3,4},{4,5},{5,6},{6,7},{7,8},{8,9},{9,10},{10,1... | collective-permute-start | bytes 1179656 | tf_op jit(solution)/shard_map/ppermute | solution.py:334
  126.2 3.8 %coefs.2.coef = f32[32,8]{1,0:T(8,128)S(1)} custom-call(f32[4224,128]{1,0:T(8,128)S(1)} %copy-done.2, f32[4224,128]{1,0:T(8,128)S(1)} %copy-done.4, f32[4224,128]{1,0:T(8,128)S(1)} %copy-done.6, f32[128,8,256]{2,1,0:T(8,128)S(1)} %bitcast.78, f32[32,8]{1,0:T(8,128)S(1)} %bitcast.87), custom_call_target="tpu_custom_call" | custom-call | tf_op jit(solution)/shard_map/coefs/pallas_call | solution.py:306
  134.8 3.9 %probes.3 = (f32[4224,128]{1,0:T(8,128)S(1)}, f32[4224,128]{1,0:T(8,128)S(1)}) custom-call(s32[1]{0:T(128)} %bitcast.3.half, f32[64,8,256]{2,1,0:T(8,128)} %all-to-all-done.1.near, f32[64,8,256]{2,1,0:T(8,128)S(1)} %collective-permute-done.13.far, f32[32,8]{1,0:T(8,128)S(1)} %copy-done.32), custom_call_target="tpu_custom_call" | custom-call | tf_op jit(solution)/shard_map/probes/pallas_call | solution.py:259
  138.8 16.2 %waves.3 = (f32[256,128]{1,0:T(8,128)S(1)}, f32[256,128]{1,0:T(8,128)S(1)}, f32[256,128]{1,0:T(8,128)S(1)}, f32[256,128]{1,0:T(8,128)S(1)}, f32[256,128]{1,0:T(8...) custom-call(s32[1]{0:T(128)} %bitcast.3.half, ...), custom_call_target="tpu_custom_call" | custom-call | tf_op jit(solution)/shard_map/waves/pallas_call | solution.py:274
  166.6 10.1 %all-to-all-start.2 = ((f32[64,8,384]{2,1,0:T(8,128)}), f32[64,8,384]{2,1,0:T(8,128)S(1)}, u32[]{:S(2)}, u32[]{:S(2)}) async-start(f32[64,8,384]{2,1,0:T(8,128)} %add.142), calls=%async_computation.2 | async-start | bytes 1572864 | tf_op jit(solution)/shard_map/all_to_all | solution.py:398
  180.9 11.9 %collective-permute-start.14 = (f32[3,64,256]{2,1,0:T(8,128)}, f32[3,64,256]{2,1,0:T(8,128)}, u32[]{:S(2)}, u32[]{:S(2)}) collective-permute-start(f32[3,64,256]{2,1,0:T(8,128)} %get-tuple-element.64), channel_id=1, source_target_pairs={{0,16},{1,17},{2,18},{3,19},{4,20},{5,21},{6,22},{7,23},{8,24},{9,... | collective-permute-start | bytes 589832 | tf_op jit(solution)/shard_map/ppermute | solution.py:334
  193.8 9.4 %all-to-all-start.3 = ((f32[64,8,256]{2,1,0:T(8,128)}), f32[64,8,256]{2,1,0:T(8,128)}, u32[]{:S(2)}, u32[]{:S(2)}) async-start(f32[64,8,256]{2,1,0:T(8,128)} %broadcast_in_dim.33), calls=%async_computation.3 | async-start | bytes 1048576 | tf_op jit(solution)/shard_map/all_to_all | solution.py:398
  205.8 3.4 %collective-permute-start.16 = (f32[3,128,64]{2,1,0:T(8,128)}, f32[3,128,64]{2,1,0:T(8,128)}, u32[]{:S(2)}, u32[]{:S(2)}) collective-permute-start(f32[3,128,64]{2,1,0:T(8,128)} %get-tuple-element.72), channel_id=1, source_target_pairs={{0,1},{1,2},{2,3},{3,4},{4,5},{5,6},{6,7},{7,8},{8,9},{9,10},{10,1... | collective-permute-start | bytes 294920 | tf_op jit(solution)/shard_map/ppermute | solution.py:334
  209.1 4.6 %collective-permute-start.17 = (f32[3,128,64]{2,1,0:T(8,128)}, f32[3,128,64]{2,1,0:T(8,128)}, u32[]{:S(2)}, u32[]{:S(2)}) collective-permute-start(f32[3,128,64]{2,1,0:T(8,128)} %get-tuple-element.71), channel_id=1, source_target_pairs={{1,0},{2,1},{3,2},{4,3},{5,4},{6,5},{7,6},{8,7},{9,8},{10,9},{11,1... | collective-permute-start | bytes 294920 | tf_op jit(solution)/shard_map/ppermute | solution.py:334
  216.7 3.8 %coefs.3 = f32[32,8]{1,0:T(8,128)S(1)} custom-call(f32[4224,128]{1,0:T(8,128)S(1)} %copy-done.8, f32[4224,128]{1,0:T(8,128)S(1)} %copy-done.10, f32[4224,128]{1,0:T(8,128)S(1)} %copy-done.12, f32[128,8,256]{2,1,0:T(8,128)S(1)} %maximum_select_fusion.1.modes, f32[32,8]{1,0:T(8,128)S(1)} %copy-done.36), custom_call_target="tpu_custom_call" | custom-call | tf_op jit(solution)/shard_map/coefs/pallas_call | solution.py:306
  (208 shorter events, 77.9 us)
Async XLA Ops:
  2.2 20.5 %collective-permute-start = (f32[2,64,64]{2,1,0:T(8,128)S(1)}, f32[2,64,64]{2,1,0:T(8,128)S(1)}, u32[]{:S(2)}, u32[]{:S(2)}) collective-permute-start(f32[2,64,64]{2,1,0:T(8,128)S(1)} %get-tuple-element.91), channel_id=1, source_target_pairs={{0,17},{1,18},{2,19},{3,20},{4,21},{5,22},{6,23},{7,24},{8,25},{9,... | collective-permute-start | bytes 98312 | tf_op jit(solution)/shard_map/ppermute | solution.py:334
  5.5 23.3 %collective-permute-start.2 = (f32[2,64,64]{2,1,0:T(8,128)S(1)}, f32[2,64,64]{2,1,0:T(8,128)S(1)}, u32[]{:S(2)}, u32[]{:S(2)}) collective-permute-start(f32[2,64,64]{2,1,0:T(8,128)S(1)} %get-tuple-element.93), channel_id=1, source_target_pairs={{1,16},{2,17},{3,18},{4,19},{5,20},{6,21},{7,22},{8,23},{9,24},{10... | collective-permute-start | bytes 98312 | tf_op jit(solution)/shard_map/ppermute | solution.py:334
  10.9 22.5 %collective-permute-start.5 = (f32[2,64,64]{2,1,0:T(8,128)S(1)}, f32[2,64,64]{2,1,0:T(8,128)S(1)}, u32[]{:S(2)}, u32[]{:S(2)}) collective-permute-start(f32[2,64,64]{2,1,0:T(8,128)S(1)} %get-tuple-element.92), channel_id=1, source_target_pairs={{16,1},{17,2},{18,3},{19,4},{20,5},{21,6},{22,7},{23,8},{24,9},{25... | collective-permute-start | bytes 98312 | tf_op jit(solution)/shard_map/ppermute | solution.py:334
  12.2 29.2 %collective-permute-start.7 = (f32[2,64,64]{2,1,0:T(8,128)}, f32[2,64,64]{2,1,0:T(8,128)}, u32[]{:S(2)}, u32[]{:S(2)}) collective-permute-start(f32[2,64,64]{2,1,0:T(8,128)} %get-tuple-element.94), channel_id=1, source_target_pairs={{17,0},{18,1},{19,2},{20,3},{21,4},{22,5},{23,6},{24,7},{25,8},{26... | collective-permute-start | bytes 98312 | tf_op jit(solution)/shard_map/ppermute | solution.py:334
  15.2 26.1 %collective-permute-start.3 = (f32[2,128,64]{2,1,0:T(8,128)}, f32[2,128,64]{2,1,0:T(8,128)}, u32[]{:S(2)}, u32[]{:S(2)}) collective-permute-start(f32[2,128,64]{2,1,0:T(8,128)} %get-tuple-element.97), channel_id=1, source_target_pairs={{0,1},{1,2},{2,3},{3,4},{4,5},{5,6},{6,7},{7,8},{8,9},{9,10},{10,1... | collective-permute-start | bytes 196616 | tf_op jit(solution)/shard_map/ppermute | solution.py:334
  22.7 18.7 %collective-permute-start.4 = (f32[2,128,64]{2,1,0:T(8,128)}, f32[2,128,64]{2,1,0:T(8,128)}, u32[]{:S(2)}, u32[]{:S(2)}) collective-permute-start(f32[2,128,64]{2,1,0:T(8,128)} %get-tuple-element.98), channel_id=1, source_target_pairs={{1,0},{2,1},{3,2},{4,3},{5,4},{6,5},{7,6},{8,7},{9,8},{10,9},{11,1... | collective-permute-start | bytes 196616 | tf_op jit(solution)/shard_map/ppermute | solution.py:334
  28.8 12.6 %collective-permute-start.1 = (f32[2,64,128]{2,1,0:T(8,128)}, f32[2,64,128]{2,1,0:T(8,128)}, u32[]{:S(2)}, u32[]{:S(2)}) collective-permute-start(f32[2,64,128]{2,1,0:T(8,128)} %get-tuple-element.95), channel_id=1, source_target_pairs={{0,16},{1,17},{2,18},{3,19},{4,20},{5,21},{6,22},{7,23},{8,24},{9,... | collective-permute-start | bytes 196616 | tf_op jit(solution)/shard_map/ppermute | solution.py:334
  33.4 8.0 %collective-permute-start.6 = (f32[2,64,128]{2,1,0:T(8,128)}, f32[2,64,128]{2,1,0:T(8,128)}, u32[]{:S(2)}, u32[]{:S(2)}) collective-permute-start(f32[2,64,128]{2,1,0:T(8,128)} %get-tuple-element.96), channel_id=1, source_target_pairs={{16,0},{17,1},{18,2},{19,3},{20,4},{21,5},{22,6},{23,7},{24,8},{25... | collective-permute-start | bytes 196616 | tf_op jit(solution)/shard_map/ppermute | solution.py:334
  64.1 13.2 %collective-permute-start.12 = (f32[64,8,384]{2,1,0:T(8,128)S(1)}, f32[64,8,384]{2,1,0:T(8,128)S(1)}, u32[]{:S(2)}, u32[]{:S(2)}) collective-permute-start(f32[64,8,384]{2,1,0:T(8,128)S(1)} %get-tuple-element.38), channel_id=1, source_target_pairs={{0,16},{16,0},{32,48},{48,32},{64,80},{80,64},{96,112},{112,96},{1... | collective-permute-start | bytes 2359304 | tf_op jit(solution)/shard_map/ppermute | solution.py:411
  72.8 17.7 %collective-permute-start.8 = (f32[6,128,128]{2,1,0:T(8,128)}, f32[6,128,128]{2,1,0:T(8,128)}, u32[]{:S(2)}, u32[]{:S(2)}) collective-permute-start(f32[6,128,128]{2,1,0:T(8,128)} %get-tuple-element.79), channel_id=1, source_target_pairs={{0,16},{1,17},{2,18},{3,19},{4,20},{5,21},{6,22},{7,23},{8,24},{9,... | collective-permute-start | bytes 1179656 | tf_op jit(solution)/shard_map/ppermute | solution.py:334
  76.0 14.4 %collective-permute-start.9 = (f32[6,128,128]{2,1,0:T(8,128)}, f32[6,128,128]{2,1,0:T(8,128)}, u32[]{:S(2)}, u32[]{:S(2)}) collective-permute-start(f32[6,128,128]{2,1,0:T(8,128)} %get-tuple-element.80), channel_id=1, source_target_pairs={{16,0},{17,1},{18,2},{19,3},{20,4},{21,5},{22,6},{23,7},{24,8},{25... | collective-permute-start | bytes 1179656 | tf_op jit(solution)/shard_map/ppermute | solution.py:334
  78.3 24.6 %all-to-all-start = ((f32[64,8,384]{2,1,0:T(8,128)}), f32[64,8,384]{2,1,0:T(8,128)}, u32[]{:S(2)}, u32[]{:S(2)}) async-start(f32[64,8,384]{2,1,0:T(8,128)} %add.132), calls=%async_computation | async-start | bytes 1572864 | tf_op jit(solution)/shard_map/all_to_all | solution.py:398
  93.9 19.9 %collective-permute-start.11 = (f32[3,256,128]{2,1,0:T(8,128)}, f32[3,256,128]{2,1,0:T(8,128)}, u32[]{:S(2)}, u32[]{:S(2)}) collective-permute-start(f32[3,256,128]{2,1,0:T(8,128)} %pad_maximum_fusion.2), channel_id=1, source_target_pairs={{1,0},{2,1},{3,2},{4,3},{5,4},{6,5},{7,6},{8,7},{9,8},{10,9},{11,1... | collective-permute-start | bytes 1179656 | tf_op jit(solution)/shard_map/ppermute | solution.py:334
  107.5 23.8 %all-to-all-start.1 = ((f32[64,8,256]{2,1,0:T(8,128)}), f32[64,8,256]{2,1,0:T(8,128)}, u32[]{:S(2)}, u32[]{:S(2)}) async-start(f32[64,8,256]{2,1,0:T(8,128)} %broadcast_in_dim.32), calls=%async_computation.1 | async-start | bytes 1048576 | tf_op jit(solution)/shard_map/all_to_all | solution.py:398
  116.0 15.4 %collective-permute-start.10 = (f32[3,256,128]{2,1,0:T(8,128)}, f32[3,256,128]{2,1,0:T(8,128)}, u32[]{:S(2)}, u32[]{:S(2)}) collective-permute-start(f32[3,256,128]{2,1,0:T(8,128)} %get-tuple-element.74), channel_id=1, source_target_pairs={{0,1},{1,2},{2,3},{3,4},{4,5},{5,6},{6,7},{7,8},{8,9},{9,10},{10,1... | collective-permute-start | bytes 1179656 | tf_op jit(solution)/shard_map/ppermute | solution.py:334
  131.3 3.5 %collective-permute-start.13 = (f32[64,8,256]{2,1,0:T(8,128)}, f32[64,8,256]{2,1,0:T(8,128)S(1)}, u32[]{:S(2)}, u32[]{:S(2)}) collective-permute-start(f32[64,8,256]{2,1,0:T(8,128)} %all-to-all-done.1.near), channel_id=1, source_target_pairs={{0,16},{16,0},{32,48},{48,32},{64,80},{80,64},{96,112},{112,96},{1... | collective-permute-start | bytes 1572872 | tf_op jit(solution)/shard_map/ppermute | solution.py:416
  163.0 2.5 %collective-permute-start.18 = (f32[64,8,384]{2,1,0:T(8,128)S(1)}, f32[64,8,384]{2,1,0:T(8,128)S(1)}, u32[]{:S(2)}, u32[]{:S(2)}) collective-permute-start(f32[64,8,384]{2,1,0:T(8,128)S(1)} %get-tuple-element.51), channel_id=1, source_target_pairs={{0,16},{16,0},{32,48},{48,32},{64,80},{80,64},{96,112},{112,96},{1... | collective-permute-start | bytes 2359304 | tf_op jit(solution)/shard_map/ppermute | solution.py:411
  166.6 26.3 %all-to-all-start.2 = ((f32[64,8,384]{2,1,0:T(8,128)}), f32[64,8,384]{2,1,0:T(8,128)S(1)}, u32[]{:S(2)}, u32[]{:S(2)}) async-start(f32[64,8,384]{2,1,0:T(8,128)} %add.142), calls=%async_computation.2 | async-start | bytes 1572864 | tf_op jit(solution)/shard_map/all_to_all | solution.py:398
  176.8 3.3 %collective-permute-start.15 = (f32[3,64,256]{2,1,0:T(8,128)S(1)}, f32[3,64,256]{2,1,0:T(8,128)S(1)}, u32[]{:S(2)}, u32[]{:S(2)}) collective-permute-start(f32[3,64,256]{2,1,0:T(8,128)S(1)} %slice.213), channel_id=1, source_target_pairs={{16,0},{17,1},{18,2},{19,3},{20,4},{21,5},{22,6},{23,7},{24,8},{25... | collective-permute-start | bytes 589832 | tf_op jit(solution)/shard_map/ppermute | solution.py:334
  180.9 23.0 %collective-permute-start.14 = (f32[3,64,256]{2,1,0:T(8,128)}, f32[3,64,256]{2,1,0:T(8,128)}, u32[]{:S(2)}, u32[]{:S(2)}) collective-permute-start(f32[3,64,256]{2,1,0:T(8,128)} %get-tuple-element.64), channel_id=1, source_target_pairs={{0,16},{1,17},{2,18},{3,19},{4,20},{5,21},{6,22},{7,23},{8,24},{9,... | collective-permute-start | bytes 589832 | tf_op jit(solution)/shard_map/ppermute | solution.py:334
  193.8 27.3 %all-to-all-start.3 = ((f32[64,8,256]{2,1,0:T(8,128)}), f32[64,8,256]{2,1,0:T(8,128)}, u32[]{:S(2)}, u32[]{:S(2)}) async-start(f32[64,8,256]{2,1,0:T(8,128)} %broadcast_in_dim.33), calls=%async_computation.3 | async-start | bytes 1048576 | tf_op jit(solution)/shard_map/all_to_all | solution.py:398
  205.8 15.4 %collective-permute-start.16 = (f32[3,128,64]{2,1,0:T(8,128)}, f32[3,128,64]{2,1,0:T(8,128)}, u32[]{:S(2)}, u32[]{:S(2)}) collective-permute-start(f32[3,128,64]{2,1,0:T(8,128)} %get-tuple-element.72), channel_id=1, source_target_pairs={{0,1},{1,2},{2,3},{3,4},{4,5},{5,6},{6,7},{7,8},{8,9},{9,10},{10,1... | collective-permute-start | bytes 294920 | tf_op jit(solution)/shard_map/ppermute | solution.py:334
  209.1 12.0 %collective-permute-start.17 = (f32[3,128,64]{2,1,0:T(8,128)}, f32[3,128,64]{2,1,0:T(8,128)}, u32[]{:S(2)}, u32[]{:S(2)}) collective-permute-start(f32[3,128,64]{2,1,0:T(8,128)} %get-tuple-element.71), channel_id=1, source_target_pairs={{1,0},{2,1},{3,2},{4,3},{5,4},{6,5},{7,6},{8,7},{9,8},{10,9},{11,1... | collective-permute-start | bytes 294920 | tf_op jit(solution)/shard_map/ppermute | solution.py:334
  221.1 2.1 collective-permute-start.19
  (63 other events, 382.0 us)

commit v4 on v3

--- a/solution.py
+++ b/solution.py
@@ -20,6 +20,7 @@
 PAIRS = 4
 LEAD = 33
 ROWS = PS // 2
+MARGIN = PS // 2
 
 
 def split(x):
@@ -64,10 +65,11 @@
 
 def probe_kernel(half, near, far, coef, probe_r, probe_i):
     left = triple(coef[...], 1)
-    for source, base in ((near, half[0] * ROWS), (far, (1 - half[0]) * ROWS)):
+    skip = far.shape[0] - ROWS
+    for source, base, skip in ((near, half[0] * ROWS, 0), (far, (1 - half[0]) * ROWS, skip)):
 
         def rows(y, _):
-            m = source[y]
+            m = source[skip + y]
             h = m.astype(BF16).astype(F32)
             right = jnp.concatenate([h, h, m - h], axis=0).astype(BF16)
             out = dot(left, right)
@@ -81,7 +83,8 @@
 
 def wave_kernel(
     half, offs, ext, photons, probe_r, probe_i, coef, ahead_t, back_w, ahead_w, back_t,
-    acc_rl, acc_rh, acc_il, acc_ih, acc_pl, acc_ph, out_r, out_i, out_p, near, far,
+    up, mid, down, out_r, out_i, out_p, near, far,
+    acc_rl, acc_rh, acc_il, acc_ih, acc_pl, acc_ph,
     patches, wave, field, cross_r, cross_i, power, sems,
 ):
     step = pl.program_id(0)
@@ -93,6 +96,9 @@
         for low, high in sums:
             low[...] = jnp.zeros_like(low)
             high[...] = jnp.zeros_like(high)
+
+    def own_lanes(left):
+        return (lane < left + MARGIN) & (lane >= left - MARGIN)
 
     def regroup(x):
         top = jnp.concatenate([x[:PS, :PS], x[PS:, :PS]], axis=1)
@@ -112,13 +118,14 @@
         p = 2 * PAIRS * step + 2 * j + q
         top = offs[p, 0]
         left = offs[p, 1]
-        turn = (PS - left) & (PS - 1)
-        inside = lane < PS - left
+        turn = (PS + MARGIN - left) & (PS - 1)
+        inside = own_lanes(left)
         total = None
         for c in range(2):
-            a = pltpu.roll(ext[c, 0, pl.ds(top, PS), :], turn, 1)
-            b = pltpu.roll(ext[c, 1, pl.ds(top, PS), :], turn, 1)
-            patch = jnp.where(inside, a, b)
+            patch = jnp.where(
+                inside, ext[c, 0, pl.ds(top, PS), :], ext[c, 1, pl.ds(top, PS), :]
+            )
+            patch = pltpu.roll(patch, turn, 1)
             patches[2 * j + q, c] = patch
             total = patch * patch if total is None else total + patch * patch
         power[pl.ds(p, PS, stride=LEAD), :] = total
@@ -144,8 +151,8 @@
             p = 2 * PAIRS * step + 2 * j + q
             top = offs[p, 0]
             left = offs[p, 1]
-            turn = left & (PS - 1)
-            inside = lane >= left
+            turn = (left + MARGIN) & (PS - 1)
+            inside = own_lanes(left)
             rows = slice(q * PS, (q + 1) * PS)
             diff_r = field[j, rows, :PS]
             diff_i = field[j, rows, PS:]
@@ -177,6 +184,12 @@
 
     @pl.when(step == PMAX // (2 * PAIRS) - 1)
     def _():
+        width = up.shape[1]
+        for i, piece in enumerate((acc_rl, acc_il, acc_pl, acc_rh, acc_ih, acc_ph)):
+            down[i] = piece[:width]
+            up[i] = piece[EXT - width:]
+            if width < PS:
+                mid[i] = piece[width : EXT - width]
         copies = [
             pltpu.make_async_copy(source, target, sems.at[i])
             for i, (source, target) in enumerate(
@@ -266,15 +279,16 @@
     )(half, near, far, coef)
 
 
-def waves(half, offs, ext, photons, probe_r, probe_i, coef, tables):
-    part = jax.ShapeDtypeStruct((EXT, PS), F32)
+def waves(half, offs, ext, photons, probe_r, probe_i, coef, tables, width):
+    edge = jax.ShapeDtypeStruct((6, width, PS), F32)
+    inner = jax.ShapeDtypeStruct((6, max(EXT - 2 * width, 8), PS), F32)
     grid = jax.ShapeDtypeStruct((PS * LEAD, PS), F32)
     rows = jax.ShapeDtypeStruct((ROWS, MODES, 3 * PS), F32)
     square = pltpu.VMEM((PAIRS, 2 * PS, 2 * PS), F32)
     return pl.pallas_call(
         wave_kernel,
         grid=(PMAX // (2 * PAIRS),),
-        out_shape=(*[part] * 6, *[grid] * 3, rows, rows),
+        out_shape=(edge, inner, edge, *[grid] * 3, rows, rows),
         in_specs=[
             SMEM,
             SMEM,
@@ -285,8 +299,9 @@
             VMEM,
             *[VMEM] * len(tables),
         ],
-        out_specs=(*[VMEM] * 6, *[pl.BlockSpec(memory_space=pl.ANY)] * 3, VMEM, VMEM),
+        out_specs=(*[VMEM] * 3, *[pl.BlockSpec(memory_space=pltpu.HBM)] * 3, VMEM, VMEM),
         scratch_shapes=[
+            *[pltpu.VMEM((EXT, PS), F32)] * 6,
             pltpu.VMEM((2 * PAIRS, 2, PS, PS), F32),
             square,
             square,
@@ -317,7 +332,7 @@
         out_specs=whole,
         scratch_shapes=[pltpu.VMEM((PMAX, MODES), F32)] * 2,
         compiler_params=pltpu.CompilerParams(
-            dimension_semantics=("arbitrary",), vmem_limit_bytes=6 << 20
+            dimension_semantics=("arbitrary",), vmem_limit_bytes=56 << 20
         ),
         name="coefs",
     )(cross_r, cross_i, powers, modes, coef)
@@ -334,51 +349,46 @@
     return lax.ppermute(x, ("row", "col"), pairs)
 
 
+def by_side(low, high):
+    lane = lax.broadcasted_iota(jnp.int32, low.shape, low.ndim - 1)
+    return jnp.where(lane < MARGIN, low, high)
+
+
 def extend(block):
-    margin = PS // 2
-    ends = {-1: slice(PS - margin, PS), 0: slice(0, PS), 1: slice(0, margin)}
-    rows = []
-    for a in (-1, 0, 1):
-        row = [
-            block if (a, b) == (0, 0) else shifted(block[:, ends[a], ends[b]], (a, b))
-            for b in (-1, 0, 1)
-        ]
-        rows.append(jnp.concatenate(row, axis=2))
-    full = jnp.concatenate(rows, axis=1)
-    return jnp.stack([full[:, :, :PS], full[:, :, PS:]], axis=1)
-
-
-def sum_extended(acc):
-    low = shifted(jnp.stack([x[PS:] for x in acc]), (-1, 0))
-    high = shifted(jnp.stack([x[:PS] for x in acc]), (1, 0))
-    left = jnp.concatenate([jnp.stack(acc[::2])[:, :PS] + low[::2], jnp.stack(acc[::2])[:, PS:] + high[::2]], axis=1)
-    right = jnp.concatenate([jnp.stack(acc[1::2])[:, :PS] + low[1::2], jnp.stack(acc[1::2])[:, PS:] + high[1::2]], axis=1)
-    return jnp.stack([left + shifted(right, (0, -1)), right + shifted(left, (0, 1))], axis=1)
+    beside = by_side(shifted(block, (0, 1)), shifted(block, (0, -1)))
+    both = jnp.stack([block, beside], axis=1)
+    above = shifted(both[:, :, -MARGIN:], (-1, 0))
+    below = shifted(both[:, :, :MARGIN], (1, 0))
+    return jnp.concatenate([above, both, below], axis=2)
+
+
+def sum_extended(up, down):
+    low = down + shifted(up, (-1, 0))
+    high = up + shifted(down, (1, 0))
+    full = jnp.concatenate([low, high], axis=1)
+    own, beside = full[:3], full[3:]
+    from_left = shifted(by_side(beside, own), (0, -1))
+    from_right = shifted(by_side(own, beside), (0, 1))
+    own = own + by_side(from_left, from_right)
+    beside = beside + by_side(from_right, from_left)
+    return jnp.stack([own, beside], axis=1)
 
 
 def inside_object():
-    margin = PS // 2
-
-    def axis(name, count):
-        place = lax.axis_index(name) * TILE - margin + lax.iota(jnp.int32, EXT)
-        return (place >= 0) & (place < count * TILE)
-
-    rows = axis("row", lax.axis_size("row"))
-    cols = axis("col", lax.axis_size("col")).reshape(2, 1, PS)
-    return rows[None, :, None] & cols
-
-
-def fold(acc):
-    margin = PS // 2
-    full = jnp.concatenate([jnp.stack(acc[::2]), jnp.stack(acc[1::2])], axis=2)
-    low = shifted(full[:, -margin:], (-1, 0))
-    high = shifted(full[:, :margin], (1, 0))
-    mid = full[:, margin:-margin]
-    mid = jnp.concatenate([mid[:, :margin] + low, mid[:, margin:] + high], axis=1)
-    low = shifted(mid[:, :, -margin:], (0, -1))
-    high = shifted(mid[:, :, :margin], (0, 1))
-    mid = mid[:, :, margin:-margin]
-    return jnp.concatenate([mid[:, :, :margin] + low, mid[:, :, margin:] + high], axis=2)
+    a, b = lax.axis_index("row"), lax.axis_index("col")
+    place = a * TILE - MARGIN + lax.iota(jnp.int32, EXT)
+    rows = (place >= 0) & (place < lax.axis_size("row") * TILE)
+    lane = lax.iota(jnp.int32, PS)
+    beside = ((lane < MARGIN) & (b < lax.axis_size("col") - 1)) | ((lane >= MARGIN) & (b > 0))
+    cols = jnp.stack([jnp.ones_like(beside), beside])
+    return rows[None, :, None] & cols[:, None, :]
+
+
+def fold(up, mid, down):
+    edges = jnp.concatenate([shifted(up, (-1, 0)), shifted(down, (1, 0))], axis=1)
+    mid = mid + edges
+    beside = mid[3:]
+    return mid[:3] + by_side(shifted(beside, (0, -1)), shifted(beside, (0, 1)))
 
 
 def shards(object_field, probe_modes, coefficients, offsets, counts, measured):
@@ -398,15 +408,17 @@
         return lax.all_to_all(x, ("row", "col"), 0, 0, axis_index_groups=groups, tiled=True)
 
     modes = probe_modes.transpose(2, 0, 1, 3).reshape(PS, MODES, 2 * PS)
-    near = lax.dynamic_slice_in_dim(modes, core * ROWS, ROWS, 0)
-    far = lax.dynamic_slice_in_dim(modes, (1 - core) * ROWS, ROWS, 0)
-    mine = lax.dynamic_index_in_dim(near, place, 0, keepdims=False)
+    mine = lax.dynamic_index_in_dim(modes, core * ROWS + place, 0, keepdims=False)
     ext = extend(object_field)
     for iteration in range(ITERS):
+        final = iteration == ITERS - 1
         used = coef * live
-        probe_r, probe_i = mix_probes(half, near, far, used)
-        *acc, cross_r, cross_i, powers, kept, given = waves(
-            half, offs, ext, photons, probe_r, probe_i, used, tables
+        if iteration == 0:
+            probe_r, probe_i = mix_probes(jnp.zeros_like(half), modes, modes, used)
+        else:
+            probe_r, probe_i = mix_probes(half, near, far, used)
+        up, mid, down, cross_r, cross_i, powers, kept, given = waves(
+            half, offs, ext, photons, probe_r, probe_i, used, tables, MARGIN if final else PS
         )
         sent = kept + lax.ppermute(given, "row", mates)
         total = jnp.sum(exchange(sent), axis=0)
@@ -418,17 +430,13 @@
         modes = jnp.where(
             core == 0, jnp.concatenate([near, far]), jnp.concatenate([far, near])
         )
-        if iteration < ITERS - 1:
-            total = sum_extended(acc)
+        if final:
+            total = fold(up, mid, down)
+            object_field = ext[:, 0, MARGIN:-MARGIN] + total[0:2] / (total[2:3] + 1.0)
+        else:
+            total = sum_extended(up, down)
             step = total[0:2] / (total[2:3] + 1.0)
             ext = ext + jnp.where(inside_object()[None], step, 0.0)
-        else:
-            margin = PS // 2
-            field = jnp.concatenate(
-                [ext[:, 0, margin:-margin, margin:], ext[:, 1, margin:-margin, :margin]], axis=2
-            )
-            total = fold(acc)
-            object_field = field + total[0:2] / (total[2:3] + 1.0)
     probe_modes = modes.reshape(PS, MODES, 2, PS).transpose(1, 2, 0, 3)
     return (object_field, probe_modes, coef[None, None])
 

time: 228 us -> 204 us (0.89)
  starting transfers between devices: 99.6 us -> 73.8 us
  local copies, waits for them, and re-layouts: 41.6 us -> 21.7 us
  waiting for transfers between devices: 8.38 us -> 25.2 us
  Pallas kernels: 46.6 us -> 52.9 us
    ppermute x16 -> x12, starting transfers between devices: 58.7 us -> 33.1 us  [shifted(): return lax.ppermute(x, ('row', 'col'), pairs)]
    all_to_all x4, waiting for transfers between devices: 4.34 us -> 19 us  [exchange(): lax.all_to_all(x, ('row', 'col'), 0, 0, axis_index_groups=groups, tiled=T...]
    unnamed x134 -> x79, local copies, waits for them, and re-layouts: 30.8 us -> 16.6 us
    pallas_call x2, Pallas kernels: 7.53 us -> 15.8 us  [new_coefficients(): pl.pallas_call(coef_kernel, grid=(PS // CHUNK,), out_shape=jax.ShapeDtype...]
    slice x4 -> x1, local copies, waits for them, and re-layouts: 4.87 us -> 0.01 us  [fold(): beside = mid[3:]]
    select_n x0 -> x1, other arithmetic: none -> 2.29 us  [by_side(): return jnp.where(lane < MARGIN, low, high)]
    another operation x4 -> x3, other arithmetic: 4.61 us -> 3.24 us  [the longest x2 1.93 us: extend(): both = jnp.stack([block, beside], axis=1)]
  transfers between devices with their start and end apart: 24 -> 20, of which waited for: 4 -> 7; matrix products, arithmetic and copies ran while one was open for 17% -> 12% of each run, Pallas kernels for 5% -> 9%
where the time goes in v4:
time: 204 us; the launch traced here: 201 us
  starting transfers between devices  73.8 us (36%)
  Pallas kernels  52.9 us (26%)
  other arithmetic  25.9 us (13%)
  waiting for transfers between devices  25.2 us (12%)
  local copies, waits for them, and re-layouts  21.7 us (11%)
    all_to_all x4, starting transfers between devices, exchange(): lax.all_to_all(x, ('row', 'col'), 0, 0, axis_index_groups=groups, tiled=T...  36.6 us
    ppermute x12, starting transfers between devices, shifted(): return lax.ppermute(x, ('row', 'col'), pairs)  33.1 us
    pallas_call x2, Pallas kernels, waves(): pl.pallas_call(wave_kernel, grid=(PMAX // (2 * PAIRS),), out_shape=(edge,...  31.7 us
    all_to_all x4, waiting for transfers between devices, exchange(): lax.all_to_all(x, ('row', 'col'), 0, 0, axis_index_groups=groups, tiled=T...  19 us
    unnamed x79, local copies, waits for them, and re-layouts  16.6 us
    pallas_call x2, Pallas kernels, new_coefficients(): pl.pallas_call(coef_kernel, grid=(PS // CHUNK,), out_shape=jax.ShapeDtype...  15.8 us
    pallas_call x2, Pallas kernels, mix_probes(): pl.pallas_call(probe_kernel, out_shape=(grid, grid), in_specs=[SMEM, VMEM...  5.42 us
    ppermute x2, starting transfers between devices, shards(): sent = kept + lax.ppermute(given, 'row', mates)  4.1 us
  transfers between devices with their start and end apart: 20, of which 7 were waited for; matrix products, arithmetic and copies ran while one was open for 12% of the time, Pallas kernels for 9%

profile of v4, /device:TPU:2, one launch (start us, length us, event | category | flops | bytes accessed | tf_op | source)
XLA Modules:
  0.0 201.4 jit_solution(8783402713332293464)
XLA Ops:
  0.6 5.9 %collective-permute-start = (f32[2,128,128]{2,1,0:T(8,128)}, f32[2,128,128]{2,1,0:T(8,128)}, u32[]{:S(2)}, u32[]{:S(2)}) collective-permute-start(f32[2,128,128]{2,1,0:T(8,128)} %param.10), channel_id=1, source_target_pairs={{1,0},{2,1},{3,2},{4,3},{5,4},{6,5},{7,6},{8,7},{9,8},{10,9},{11,1... | collective-permute-start | bytes 393224 | tf_op jit(solution)/shard_map/ppermute | solution.py:349
  6.6 1.9 collective-permute-start.1
  21.2 2.7 %probes.2 = (f32[4224,128]{1,0:T(8,128)S(1)}, f32[4224,128]{1,0:T(8,128)S(1)}) custom-call(s32[1]{0:T(128)} %constant.68.clone.1.half, f32[128,8,256]{2,1,0:T(8,128)S(1)} %bitcast.35, f32[128,8,256]{2,1,0:T(8,128)S(1)} %bitcast.36, f32[32,8]{1,0:T(8,128)S(1)} %broadcast_multiply_fusion.1.coef), custom_call_target="tpu_custom_call" | custom-call | tf_op jit(solution)/shard_map/probes/pallas_call | solution.py:272
  25.2 16.1 %waves.2 = (f32[6,128,128]{2,1,0:T(8,128)S(1)}, f32[6,8,128]{2,1,0:T(8,128)}, f32[6,128,128]{2,1,0:T(8,128)S(1)}, f32[4224,128]{1,0:T(8,128)S(1)}, f32[4224,128]...) custom-call(s32[1]{0:T(128)} %bitcast.2.half, ...), custom_call_target="tpu_custom_call" | custom-call | tf_op jit(solution)/shard_map/waves/pallas_call | solution.py:288
  47.0 3.6 %collective-permute-start.8 = (f32[64,8,384]{2,1,0:T(8,128)S(1)}, f32[64,8,384]{2,1,0:T(8,128)S(1)}, u32[]{:S(2)}, u32[]{:S(2)}) collective-permute-start(f32[64,8,384]{2,1,0:T(8,128)S(1)} %get-tuple-element.27), channel_id=1, source_target_pairs={{0,16},{16,0},{32,48},{48,32},{64,80},{80,64},{96,112},{112,96},{1... | collective-permute-start | bytes 2359304 | tf_op jit(solution)/shard_map/ppermute | solution.py:423
  50.5 1.9 collective-permute-done.8
  53.5 9.8 %all-to-all-start = ((f32[64,8,384]{2,1,0:T(8,128)}), f32[64,8,384]{2,1,0:T(8,128)}, u32[]{:S(2)}, u32[]{:S(2)}) async-start(f32[64,8,384]{2,1,0:T(8,128)} %add.93), calls=%async_computation | async-start | bytes 1572864 | tf_op jit(solution)/shard_map/all_to_all | solution.py:408
  63.3 2.5 %collective-permute-start.4 = (f32[6,128,128]{2,1,0:T(8,128)}, f32[6,128,128]{2,1,0:T(8,128)}, u32[]{:S(2)}, u32[]{:S(2)}) collective-permute-start(f32[6,128,128]{2,1,0:T(8,128)} %copy-done.17), channel_id=1, source_target_pairs={{0,16},{1,17},{2,18},{3,19},{4,20},{5,21},{6,22},{7,23},{8,24},{9,... | collective-permute-start | bytes 1179656 | tf_op jit(solution)/shard_map/ppermute | solution.py:349
  68.3 1.9 add.83
  72.2 6.6 %all-to-all-done = f32[64,8,384]{2,1,0:T(8,128)} async-done(((f32[64,8,384]{2,1,0:T(8,128)}), f32[64,8,384]{2,1,0:T(8,128)}, u32[]{:S(2)}, u32[]{:S(2)}) %all-to-all-start) | async-done | bytes 786464 | tf_op jit(solution)/shard_map/all_to_all | solution.py:408
  83.4 12.3 %all-to-all-start.1 = ((f32[64,8,256]{2,1,0:T(8,128)}), f32[64,8,256]{2,1,0:T(8,128)S(1)}, u32[]{:S(2)}, u32[]{:S(2)}) async-start(f32[64,8,256]{2,1,0:T(8,128)} %broadcast_in_dim.20), calls=%async_computation.1 | async-start | bytes 1048576 | tf_op jit(solution)/shard_map/all_to_all | solution.py:408
  95.8 2.3 %broadcast_select_fusion = (f32[3,256,128]{2,1,0:T(8,128)}, f32[3,256,128]{2,1,0:T(8,128)}) fusion(pred[128]{0:T(512)(128)(4,1)} %iota_compare_fusion, f32[6,128,128]{2,1,0:T(8,128)} %add.84, f32[6,128,128]{2,1,0:T(8,128)} %add.83), kind=kLoop, calls=%fused_computation.24 | loop fusion | flops 491520 | bytes 1572992 | tf_op jit(solution)/shard_map/jit(_where)/select_n | solution.py:354
  98.1 3.4 %collective-permute-start.6 = (f32[3,256,128]{2,1,0:T(8,128)}, f32[3,256,128]{2,1,0:T(8,128)}, u32[]{:S(2)}, u32[]{:S(2)}) collective-permute-start(f32[3,256,128]{2,1,0:T(8,128)} %get-tuple-element.50), channel_id=1, source_target_pairs={{0,1},{1,2},{2,3},{3,4},{4,5},{5,6},{6,7},{7,8},{8,9},{9,10},{10,1... | collective-permute-start | bytes 1179656 | tf_op jit(solution)/shard_map/ppermute | solution.py:349
  101.4 4.6 %collective-permute-start.7 = (f32[3,256,128]{2,1,0:T(8,128)}, f32[3,256,128]{2,1,0:T(8,128)}, u32[]{:S(2)}, u32[]{:S(2)}) collective-permute-start(f32[3,256,128]{2,1,0:T(8,128)} %get-tuple-element.49), channel_id=1, source_target_pairs={{1,0},{2,1},{3,2},{4,3},{5,4},{6,5},{7,6},{8,7},{9,8},{10,9},{11,1... | collective-permute-start | bytes 1179656 | tf_op jit(solution)/shard_map/ppermute | solution.py:349
  106.8 7.9 %coefs.2.coef = f32[32,8]{1,0:T(8,128)} custom-call(f32[4224,128]{1,0:T(8,128)} %copy-done.2, f32[4224,128]{1,0:T(8,128)} %copy-done.3, f32[4224,128]{1,0:T(8,128)} %copy-done.4, f32[128,8,256]{2,1,0:T(8,128)} %bitcast.38, f32[32,8]{1,0:T(8,128)} %bitcast.47), custom_call_target="tpu_custom_call" | custom-call | tf_op jit(solution)/shard_map/coefs/pallas_call | solution.py:321
  118.9 2.7 %probes.3 = (f32[4224,128]{1,0:T(8,128)S(1)}, f32[4224,128]{1,0:T(8,128)S(1)}) custom-call(s32[1]{0:T(128)} %bitcast.2.half, f32[64,8,256]{2,1,0:T(8,128)S(1)} %all-to-all-done.1.near, f32[64,8,256]{2,1,0:T(8,128)S(1)} %collective-permute-done.9.far, f32[32,8]{1,0:T(8,128)S(1)} %copy-done.21), custom_call_target="tpu_custom_call" | custom-call | tf_op jit(solution)/shard_map/probes/pallas_call | solution.py:272
  121.6 15.6 %waves.3 = (f32[6,64,128]{2,1,0:T(8,128)S(1)}, f32[6,128,128]{2,1,0:T(8,128)S(1)}, f32[6,64,128]{2,1,0:T(8,128)S(1)}, f32[4224,128]{1,0:T(8,128)S(1)}, f32[4224,...) custom-call(s32[1]{0:T(128)} %bitcast.2.half, ...), custom_call_target="tpu_custom_call" | custom-call | tf_op jit(solution)/shard_map/waves/pallas_call | solution.py:288
  144.0 1.9 collective-permute-done.14
  146.8 8.8 %all-to-all-start.2 = ((f32[64,8,384]{2,1,0:T(8,128)}), f32[64,8,384]{2,1,0:T(8,128)S(1)}, u32[]{:S(2)}, u32[]{:S(2)}) async-start(f32[64,8,384]{2,1,0:T(8,128)} %add.101), calls=%async_computation.2 | async-start | bytes 1572864 | tf_op jit(solution)/shard_map/all_to_all | solution.py:408
  158.6 12.4 %all-to-all-done.2 = f32[64,8,384]{2,1,0:T(8,128)S(1)} async-done(((f32[64,8,384]{2,1,0:T(8,128)}), f32[64,8,384]{2,1,0:T(8,128)S(1)}, u32[]{:S(2)}, u32[]{:S(2)}) %all-to-all-start.2) | async-done | bytes 786464 | tf_op jit(solution)/shard_map/all_to_all | solution.py:408
  174.0 5.7 %all-to-all-start.3 = ((f32[64,8,256]{2,1,0:T(8,128)}), f32[64,8,256]{2,1,0:T(8,128)S(1)}, u32[]{:S(2)}, u32[]{:S(2)}) async-start(f32[64,8,256]{2,1,0:T(8,128)} %broadcast_in_dim.34), calls=%async_computation.3 | async-start | bytes 1048576 | tf_op jit(solution)/shard_map/all_to_all | solution.py:408
  179.8 3.4 %collective-permute-start.12 = (f32[3,128,128]{2,1,0:T(8,128)S(1)}, f32[3,128,128]{2,1,0:T(8,128)S(1)}, u32[]{:S(2)}, u32[]{:S(2)}) collective-permute-start(f32[3,128,128]{2,1,0:T(8,128)S(1)} %slice.70), channel_id=1, source_target_pairs={{0,1},{1,2},{2,3},{3,4},{4,5},{5,6},{6,7},{7,8},{8,9},{9,10},{10,1... | collective-permute-start | bytes 589832 | tf_op jit(solution)/shard_map/ppermute | solution.py:349
  183.2 4.6 %collective-permute-start.13 = (f32[3,128,128]{2,1,0:T(8,128)S(1)}, f32[3,128,128]{2,1,0:T(8,128)}, u32[]{:S(2)}, u32[]{:S(2)}) collective-permute-start(f32[3,128,128]{2,1,0:T(8,128)S(1)} %slice.70), channel_id=1, source_target_pairs={{1,0},{2,1},{3,2},{4,3},{5,4},{6,5},{7,6},{8,7},{9,8},{10,9},{11,1... | collective-permute-start | bytes 589832 | tf_op jit(solution)/shard_map/ppermute | solution.py:349
  188.8 7.9 %coefs.3 = f32[32,8]{1,0:T(8,128)} custom-call(f32[4224,128]{1,0:T(8,128)} %copy-done.5, f32[4224,128]{1,0:T(8,128)} %copy-done.6, f32[4224,128]{1,0:T(8,128)} %copy-done.7, f32[128,8,256]{2,1,0:T(8,128)} %maximum_select_fusion.1.modes, f32[32,8]{1,0:T(8,128)} %coefs.2.coef), custom_call_target="tpu_custom_call" | custom-call | tf_op jit(solution)/shard_map/coefs/pallas_call | solution.py:321
  (137 shorter events, 53.1 us)
Async XLA Ops:
  0.6 13.3 %collective-permute-start = (f32[2,128,128]{2,1,0:T(8,128)}, f32[2,128,128]{2,1,0:T(8,128)}, u32[]{:S(2)}, u32[]{:S(2)}) collective-permute-start(f32[2,128,128]{2,1,0:T(8,128)} %param.10), channel_id=1, source_target_pairs={{1,0},{2,1},{3,2},{4,3},{5,4},{6,5},{7,6},{8,7},{9,8},{10,9},{11,1... | collective-permute-start | bytes 393224 | tf_op jit(solution)/shard_map/ppermute | solution.py:349
  6.6 9.3 %collective-permute-start.1 = (f32[2,128,128]{2,1,0:T(8,128)}, f32[2,128,128]{2,1,0:T(8,128)}, u32[]{:S(2)}, u32[]{:S(2)}) collective-permute-start(f32[2,128,128]{2,1,0:T(8,128)} %param.10), channel_id=1, source_target_pairs={{0,1},{1,2},{2,3},{3,4},{4,5},{5,6},{6,7},{7,8},{8,9},{9,10},{10,1... | collective-permute-start | bytes 393224 | tf_op jit(solution)/shard_map/ppermute | solution.py:349
  12.9 68.4 %copy-start = (f32[128,8,2,128]{3,1,2,0:T(8,128)}, f32[128,8,2,128]{3,1,2,0:T(8,128)S(1)}, u32[]{:S(2)}) copy-start(f32[128,8,2,128]{3,1,2,0:T(8,128)S(1)} %copy.27) | copy-start | bytes 3145732
  17.8 6.1 %collective-permute-start.2 = (f32[2,2,64,128]{3,2,1,0:T(8,128)S(1)}, f32[2,2,64,128]{3,2,1,0:T(8,128)S(1)}, u32[]{:S(2)}, u32[]{:S(2)}) collective-permute-start(f32[2,2,64,128]{3,2,1,0:T(8,128)S(1)} %get-tuple-element.51), channel_id=1, source_target_pairs={{0,16},{1,17},{2,18},{3,19},{4,20},{5,21},{6,22},{7,23},{8,24},{9,... | collective-permute-start | bytes 393224 | tf_op jit(solution)/shard_map/ppermute | solution.py:349
  19.1 5.0 %collective-permute-start.3 = (f32[2,2,64,128]{3,2,1,0:T(8,128)S(1)}, f32[2,2,64,128]{3,2,1,0:T(8,128)S(1)}, u32[]{:S(2)}, u32[]{:S(2)}) collective-permute-start(f32[2,2,64,128]{3,2,1,0:T(8,128)S(1)} %get-tuple-element.52), channel_id=1, source_target_pairs={{16,0},{17,1},{18,2},{19,3},{20,4},{21,5},{22,6},{23,7},{24,8},{25... | collective-permute-start | bytes 393224 | tf_op jit(solution)/shard_map/ppermute | solution.py:349
  47.0 5.5 %collective-permute-start.8 = (f32[64,8,384]{2,1,0:T(8,128)S(1)}, f32[64,8,384]{2,1,0:T(8,128)S(1)}, u32[]{:S(2)}, u32[]{:S(2)}) collective-permute-start(f32[64,8,384]{2,1,0:T(8,128)S(1)} %get-tuple-element.27), channel_id=1, source_target_pairs={{0,16},{16,0},{32,48},{48,32},{64,80},{80,64},{96,112},{112,96},{1... | collective-permute-start | bytes 2359304 | tf_op jit(solution)/shard_map/ppermute | solution.py:423
  53.5 25.3 %all-to-all-start = ((f32[64,8,384]{2,1,0:T(8,128)}), f32[64,8,384]{2,1,0:T(8,128)}, u32[]{:S(2)}, u32[]{:S(2)}) async-start(f32[64,8,384]{2,1,0:T(8,128)} %add.93), calls=%async_computation | async-start | bytes 1572864 | tf_op jit(solution)/shard_map/all_to_all | solution.py:408
  63.3 5.0 %collective-permute-start.4 = (f32[6,128,128]{2,1,0:T(8,128)}, f32[6,128,128]{2,1,0:T(8,128)}, u32[]{:S(2)}, u32[]{:S(2)}) collective-permute-start(f32[6,128,128]{2,1,0:T(8,128)} %copy-done.17), channel_id=1, source_target_pairs={{0,16},{1,17},{2,18},{3,19},{4,20},{5,21},{6,22},{7,23},{8,24},{9,... | collective-permute-start | bytes 1179656 | tf_op jit(solution)/shard_map/ppermute | solution.py:349
  65.8 4.5 %collective-permute-start.5 = (f32[6,128,128]{2,1,0:T(8,128)}, f32[6,128,128]{2,1,0:T(8,128)}, u32[]{:S(2)}, u32[]{:S(2)}) collective-permute-start(f32[6,128,128]{2,1,0:T(8,128)} %copy-done.18), channel_id=1, source_target_pairs={{16,0},{17,1},{18,2},{19,3},{20,4},{21,5},{22,6},{23,7},{24,8},{25... | collective-permute-start | bytes 1179656 | tf_op jit(solution)/shard_map/ppermute | solution.py:349
  83.4 32.6 %all-to-all-start.1 = ((f32[64,8,256]{2,1,0:T(8,128)}), f32[64,8,256]{2,1,0:T(8,128)S(1)}, u32[]{:S(2)}, u32[]{:S(2)}) async-start(f32[64,8,256]{2,1,0:T(8,128)} %broadcast_in_dim.20), calls=%async_computation.1 | async-start | bytes 1048576 | tf_op jit(solution)/shard_map/all_to_all | solution.py:408
  98.1 18.0 %collective-permute-start.6 = (f32[3,256,128]{2,1,0:T(8,128)}, f32[3,256,128]{2,1,0:T(8,128)}, u32[]{:S(2)}, u32[]{:S(2)}) collective-permute-start(f32[3,256,128]{2,1,0:T(8,128)} %get-tuple-element.50), channel_id=1, source_target_pairs={{0,1},{1,2},{2,3},{3,4},{4,5},{5,6},{6,7},{7,8},{8,9},{9,10},{10,1... | collective-permute-start | bytes 1179656 | tf_op jit(solution)/shard_map/ppermute | solution.py:349
  101.4 14.7 %collective-permute-start.7 = (f32[3,256,128]{2,1,0:T(8,128)}, f32[3,256,128]{2,1,0:T(8,128)}, u32[]{:S(2)}, u32[]{:S(2)}) collective-permute-start(f32[3,256,128]{2,1,0:T(8,128)} %get-tuple-element.49), channel_id=1, source_target_pairs={{1,0},{2,1},{3,2},{4,3},{5,4},{6,5},{7,6},{8,7},{9,8},{10,9},{11,1... | collective-permute-start | bytes 1179656 | tf_op jit(solution)/shard_map/ppermute | solution.py:349
  116.1 2.7 %collective-permute-start.9 = (f32[64,8,256]{2,1,0:T(8,128)S(1)}, f32[64,8,256]{2,1,0:T(8,128)S(1)}, u32[]{:S(2)}, u32[]{:S(2)}) collective-permute-start(f32[64,8,256]{2,1,0:T(8,128)S(1)} %all-to-all-done.1.near), channel_id=1, source_target_pairs={{0,16},{16,0},{32,48},{48,32},{64,80},{80,64},{96,112},{112,96},{1... | collective-permute-start | bytes 1572872 | tf_op jit(solution)/shard_map/ppermute | solution.py:428
  143.4 2.4 %collective-permute-start.14 = (f32[64,8,384]{2,1,0:T(8,128)S(1)}, f32[64,8,384]{2,1,0:T(8,128)S(1)}, u32[]{:S(2)}, u32[]{:S(2)}) collective-permute-start(f32[64,8,384]{2,1,0:T(8,128)S(1)} %get-tuple-element.37), channel_id=1, source_target_pairs={{0,16},{16,0},{32,48},{48,32},{64,80},{80,64},{96,112},{112,96},{1... | collective-permute-start | bytes 2359304 | tf_op jit(solution)/shard_map/ppermute | solution.py:423
  145.9 26.5 %copy-start.31 = (f32[8,256]{1,0:T(8,128)S(1)}, f32[8,256]{1,0:T(8,128)}, u32[]{:S(2)}) copy-start(f32[8,256]{1,0:T(8,128)} %copy-done.30) | copy-start | bytes 24580
  146.8 32.9 %copy-start.20 = (f32[6,128,128]{2,1,0:T(8,128)S(1)}, f32[6,128,128]{2,1,0:T(8,128)}, u32[]{:S(2)}) copy-start(f32[6,128,128]{2,1,0:T(8,128)} %copy-done.19) | copy-start | bytes 1179652
  146.8 24.2 %all-to-all-start.2 = ((f32[64,8,384]{2,1,0:T(8,128)}), f32[64,8,384]{2,1,0:T(8,128)S(1)}, u32[]{:S(2)}, u32[]{:S(2)}) async-start(f32[64,8,384]{2,1,0:T(8,128)} %add.101), calls=%async_computation.2 | async-start | bytes 1572864 | tf_op jit(solution)/shard_map/all_to_all | solution.py:408
  155.6 32.2 %copy-start.9 = (f32[64,8,256]{2,1,0:T(8,128)S(1)}, f32[64,8,256]{2,1,0:T(8,128)}, u32[]{:S(2)}) copy-start(f32[64,8,256]{2,1,0:T(8,128)} %copy-done.8) | copy-start | bytes 1572868
  155.6 24.1 %collective-permute-start.10 = (f32[6,64,128]{2,1,0:T(8,128)S(1)}, f32[6,64,128]{2,1,0:T(8,128)S(1)}, u32[]{:S(2)}, u32[]{:S(2)}) collective-permute-start(f32[6,64,128]{2,1,0:T(8,128)S(1)} %copy-done.25), channel_id=1, source_target_pairs={{0,16},{1,17},{2,18},{3,19},{4,20},{5,21},{6,22},{7,23},{8,24},{9,... | collective-permute-start | bytes 589832 | tf_op jit(solution)/shard_map/ppermute | solution.py:349
  157.3 22.4 %collective-permute-start.11 = (f32[6,64,128]{2,1,0:T(8,128)S(1)}, f32[6,64,128]{2,1,0:T(8,128)S(1)}, u32[]{:S(2)}, u32[]{:S(2)}) collective-permute-start(f32[6,64,128]{2,1,0:T(8,128)S(1)} %copy-done.23), channel_id=1, source_target_pairs={{16,0},{17,1},{18,2},{19,3},{20,4},{21,5},{22,6},{23,7},{24,8},{25... | collective-permute-start | bytes 589832 | tf_op jit(solution)/shard_map/ppermute | solution.py:349
  174.0 24.1 %all-to-all-start.3 = ((f32[64,8,256]{2,1,0:T(8,128)}), f32[64,8,256]{2,1,0:T(8,128)S(1)}, u32[]{:S(2)}, u32[]{:S(2)}) async-start(f32[64,8,256]{2,1,0:T(8,128)} %broadcast_in_dim.34), calls=%async_computation.3 | async-start | bytes 1048576 | tf_op jit(solution)/shard_map/all_to_all | solution.py:408
  179.8 18.3 %collective-permute-start.12 = (f32[3,128,128]{2,1,0:T(8,128)S(1)}, f32[3,128,128]{2,1,0:T(8,128)S(1)}, u32[]{:S(2)}, u32[]{:S(2)}) collective-permute-start(f32[3,128,128]{2,1,0:T(8,128)S(1)} %slice.70), channel_id=1, source_target_pairs={{0,1},{1,2},{2,3},{3,4},{4,5},{5,6},{6,7},{7,8},{8,9},{9,10},{10,1... | collective-permute-start | bytes 589832 | tf_op jit(solution)/shard_map/ppermute | solution.py:349
  183.2 14.9 %collective-permute-start.13 = (f32[3,128,128]{2,1,0:T(8,128)S(1)}, f32[3,128,128]{2,1,0:T(8,128)}, u32[]{:S(2)}, u32[]{:S(2)}) collective-permute-start(f32[3,128,128]{2,1,0:T(8,128)S(1)} %slice.70), channel_id=1, source_target_pairs={{1,0},{2,1},{3,2},{4,3},{5,4},{6,5},{7,6},{8,7},{9,8},{10,9},{11,1... | collective-permute-start | bytes 589832 | tf_op jit(solution)/shard_map/ppermute | solution.py:349
  198.1 1.9 collective-permute-start.15
  (34 other events, 213.8 us)

commit v5 on v4

--- a/solution.py
+++ b/solution.py
@@ -185,16 +185,15 @@
     @pl.when(step == PMAX // (2 * PAIRS) - 1)
     def _():
         width = up.shape[1]
+        moves = [(cross_r, out_r), (cross_i, out_i), (power, out_p)]
         for i, piece in enumerate((acc_rl, acc_il, acc_pl, acc_rh, acc_ih, acc_ph)):
-            down[i] = piece[:width]
-            up[i] = piece[EXT - width:]
+            moves.append((piece.at[:width], down.at[i]))
+            moves.append((piece.at[EXT - width:], up.at[i]))
             if width < PS:
-                mid[i] = piece[width : EXT - width]
+                moves.append((piece.at[width : EXT - width], mid.at[i]))
         copies = [
             pltpu.make_async_copy(source, target, sems.at[i])
-            for i, (source, target) in enumerate(
-                ((cross_r, out_r), (cross_i, out_i), (power, out_p))
-            )
+            for i, (source, target) in enumerate(moves)
         ]
         for copy in copies:
             copy.start()
@@ -263,6 +262,14 @@
         out[...] = coef[...] + num[...] / (den[...] + 1.0)
 
 
+def update_kernel(got, mine, new, copies):
+    total = jnp.sum(got[...], axis=0)
+    power = total[:, 2 * PS:] + 1.0
+    row = mine[...] + total[:, : 2 * PS] / jnp.concatenate([power, power], axis=1)
+    new[...] = row
+    copies[...] = jnp.broadcast_to(row[None], copies.shape)
+
+
 SMEM = pl.BlockSpec(memory_space=pltpu.SMEM)
 VMEM = pl.BlockSpec(memory_space=pltpu.VMEM)
 
@@ -280,9 +287,9 @@
 
 
 def waves(half, offs, ext, photons, probe_r, probe_i, coef, tables, width):
-    edge = jax.ShapeDtypeStruct((6, width, PS), F32)
-    inner = jax.ShapeDtypeStruct((6, max(EXT - 2 * width, 8), PS), F32)
-    grid = jax.ShapeDtypeStruct((PS * LEAD, PS), F32)
+    edge = pltpu.HBM((6, width, PS), F32)
+    inner = pltpu.HBM((6, max(EXT - 2 * width, 8), PS), F32)
+    grid = pltpu.HBM((PS * LEAD, PS), F32)
     rows = jax.ShapeDtypeStruct((ROWS, MODES, 3 * PS), F32)
     square = pltpu.VMEM((PAIRS, 2 * PS, 2 * PS), F32)
     return pl.pallas_call(
@@ -299,14 +306,14 @@
             VMEM,
             *[VMEM] * len(tables),
         ],
-        out_specs=(*[VMEM] * 3, *[pl.BlockSpec(memory_space=pltpu.HBM)] * 3, VMEM, VMEM),
+        out_specs=(*[pl.BlockSpec(memory_space=pltpu.HBM)] * 6, VMEM, VMEM),
         scratch_shapes=[
             *[pltpu.VMEM((EXT, PS), F32)] * 6,
             pltpu.VMEM((2 * PAIRS, 2, PS, PS), F32),
             square,
             square,
             *[pltpu.VMEM((PS * LEAD, PS), F32)] * 3,
-            pltpu.SemaphoreType.DMA((3,)),
+            pltpu.SemaphoreType.DMA((21,)),
         ],
         compiler_params=pltpu.CompilerParams(
             dimension_semantics=("arbitrary",), vmem_limit_bytes=24 << 20
@@ -338,6 +345,20 @@
     )(cross_r, cross_i, powers, modes, coef)
 
 
+def update_row(got, mine):
+    return pl.pallas_call(
+        update_kernel,
+        out_shape=(
+            jax.ShapeDtypeStruct((MODES, 2 * PS), F32),
+            jax.ShapeDtypeStruct((ROWS, MODES, 2 * PS), F32),
+        ),
+        in_specs=[VMEM, VMEM],
+        out_specs=(VMEM, VMEM),
+        compiler_params=pltpu.CompilerParams(vmem_limit_bytes=2 << 20),
+        name="update",
+    )(got, mine)
+
+
 def shifted(x, move):
     rows, cols = lax.axis_size("row"), lax.axis_size("col")
     pairs = []
@@ -362,10 +383,13 @@
     return jnp.concatenate([above, both, below], axis=2)
 
 
-def sum_extended(up, down):
+def sum_rows(up, down):
     low = down + shifted(up, (-1, 0))
     high = up + shifted(down, (1, 0))
-    full = jnp.concatenate([low, high], axis=1)
+    return jnp.concatenate([low, high], axis=1)
+
+
+def sum_columns(full):
     own, beside = full[:3], full[3:]
     from_left = shifted(by_side(beside, own), (0, -1))
     from_right = shifted(by_side(own, beside), (0, 1))
@@ -421,12 +445,14 @@
             half, offs, ext, photons, probe_r, probe_i, used, tables, MARGIN if final else PS
         )
         sent = kept + lax.ppermute(given, "row", mates)
-        total = jnp.sum(exchange(sent), axis=0)
-        power = total[:, 2 * PS:] + 1.0
-        mine = mine + total[:, : 2 * PS] / jnp.concatenate([power, power], axis=1)
-        near = exchange(jnp.broadcast_to(mine[None], (ROWS, MODES, 2 * PS)))
+        got = exchange(sent)
+        coef = new_coefficients(cross_r, cross_i, powers, modes, coef)
+        got, coef = lax.optimization_barrier((got, coef))
+        mine, copies = update_row(got, mine)
+        if not final:
+            full, copies = lax.optimization_barrier((sum_rows(up, down), copies))
+        near = exchange(copies)
         far = lax.ppermute(near, "row", mates)
-        coef = new_coefficients(cross_r, cross_i, powers, modes, coef)
         modes = jnp.where(
             core == 0, jnp.concatenate([near, far]), jnp.concatenate([far, near])
         )
@@ -434,7 +460,7 @@
             total = fold(up, mid, down)
             object_field = ext[:, 0, MARGIN:-MARGIN] + total[0:2] / (total[2:3] + 1.0)
         else:
-            total = sum_extended(up, down)
+            total = sum_columns(full)
             step = total[0:2] / (total[2:3] + 1.0)
             ext = ext + jnp.where(inside_object()[None], step, 0.0)
     probe_modes = modes.reshape(PS, MODES, 2, PS).transpose(1, 2, 0, 3)

time: 204 us -> 187 us (0.917)
  local copies, waits for them, and re-layouts: 21.7 us -> 7.57 us
  other arithmetic: 25.9 us -> 20.1 us
  starting transfers between devices: 73.8 us -> 79.3 us
  waiting for transfers between devices: 25.2 us -> 21.5 us
    unnamed x79 -> x66, local copies, waits for them, and re-layouts: 16.6 us -> 3.23 us
    all_to_all x4, waiting for transfers between devices: 19 us -> 8.14 us  [exchange(): lax.all_to_all(x, ('row', 'col'), 0, 0, axis_index_groups=groups, tiled=T...]
    ppermute x12, waiting for transfers between devices: 2.14 us -> 9.19 us  [shifted(): return lax.ppermute(x, ('row', 'col'), pairs)]
    all_to_all x4, starting transfers between devices: 36.6 us -> 42.7 us  [exchange(): lax.all_to_all(x, ('row', 'col'), 0, 0, axis_index_groups=groups, tiled=T...]
    add x6 -> x2, other arithmetic: 6.61 us -> 2.08 us  [the longest x1 1.04 us: sum_rows(): low = down + shifted(up, (-1, 0))]
    pallas_call x0 -> x2, Pallas kernels: none -> 2.96 us  [update_row(): pl.pallas_call(update_kernel, out_shape=(jax.ShapeDtypeStruct((MODES, 2 *...]
    reduce_sum x2 -> x0, other arithmetic: 2.51 us -> none  [shards(): total = jnp.sum(exchange(sent), axis=0)]
  transfers between devices with their start and end apart: 20 -> 20, of which waited for: 7 -> 8; matrix products, arithmetic and copies ran while one was open for 12% -> 11% of each run, Pallas kernels for 9% -> 11%
where the time goes in v5:
time: 187 us; the launch traced here: 185 us
  starting transfers between devices  79.3 us (42%)
  Pallas kernels  54.3 us (29%)
  waiting for transfers between devices  21.5 us (11%)
  other arithmetic  20.1 us (11%)
  local copies, waits for them, and re-layouts  7.57 us (4%)
  between operations  2 us (1%)
    all_to_all x4, starting transfers between devices, exchange(): lax.all_to_all(x, ('row', 'col'), 0, 0, axis_index_groups=groups, tiled=T...  42.7 us
    ppermute x12, starting transfers between devices, shifted(): return lax.ppermute(x, ('row', 'col'), pairs)  32.9 us
    pallas_call x2, Pallas kernels, waves(): pl.pallas_call(wave_kernel, grid=(PMAX // (2 * PAIRS),), out_shape=(edge,...  30 us
    pallas_call x2, Pallas kernels, new_coefficients(): pl.pallas_call(coef_kernel, grid=(PS // CHUNK,), out_shape=jax.ShapeDtype...  15.9 us
    ppermute x12, waiting for transfers between devices, shifted(): return lax.ppermute(x, ('row', 'col'), pairs)  9.19 us
    all_to_all x4, waiting for transfers between devices, exchange(): lax.all_to_all(x, ('row', 'col'), 0, 0, axis_index_groups=groups, tiled=T...  8.14 us
    pallas_call x2, Pallas kernels, mix_probes(): pl.pallas_call(probe_kernel, out_shape=(grid, grid), in_specs=[SMEM, VMEM...  5.42 us
    ppermute x2, waiting for transfers between devices, shards(): sent = kept + lax.ppermute(given, 'row', mates)  4.18 us
  transfers between devices with their start and end apart: 20, of which 8 were waited for; matrix products, arithmetic and copies ran while one was open for 11% of the time, Pallas kernels for 11%

profile of v5, /device:TPU:2, one launch (start us, length us, event | category | flops | bytes accessed | tf_op | source)
XLA Modules:
  0.0 184.7 jit_solution(987482117556532426)
XLA Ops:
  0.6 5.9 %collective-permute-start = (f32[2,128,128]{2,1,0:T(8,128)}, f32[2,128,128]{2,1,0:T(8,128)}, u32[]{:S(2)}, u32[]{:S(2)}) collective-permute-start(f32[2,128,128]{2,1,0:T(8,128)} %param.10), channel_id=1, source_target_pairs={{1,0},{2,1},{3,2},{4,3},{5,4},{6,5},{7,6},{8,7},{9,8},{10,9},{11,1... | collective-permute-start | bytes 393224 | tf_op jit(solution)/shard_map/ppermute | solution.py:370
  13.9 2.0 %collective-permute-done.1 = f32[2,128,128]{2,1,0:T(8,128)} collective-permute-done((f32[2,128,128]{2,1,0:T(8,128)}, f32[2,128,128]{2,1,0:T(8,128)}, u32[]{:S(2)}, u32[]{:S(2)}) %collective-permute-start.1) | collective-permute-done | bytes 131104 | tf_op jit(solution)/shard_map/ppermute | solution.py:370
  21.2 2.7 %probes.2 = (f32[4224,128]{1,0:T(8,128)S(1)}, f32[4224,128]{1,0:T(8,128)S(1)}) custom-call(s32[1]{0:T(128)} %constant.67.clone.1.half, f32[128,8,256]{2,1,0:T(8,128)S(1)} %bitcast.35, f32[128,8,256]{2,1,0:T(8,128)S(1)} %bitcast.36, f32[32,8]{1,0:T(8,128)S(1)} %broadcast_multiply_fusion.1.coef), custom_call_target="tpu_custom_call" | custom-call | tf_op jit(solution)/shard_map/probes/pallas_call | solution.py:279
  25.2 15.0 %waves.2 = (f32[6,128,128]{2,1,0:T(8,128)}, f32[6,8,128]{2,1,0:T(8,128)}, f32[6,128,128]{2,1,0:T(8,128)}, f32[4224,128]{1,0:T(8,128)}, f32[4224,128]{1,0:T(8,128...) custom-call(s32[1]{0:T(128)} %bitcast.2.half, s32[32,2]{1,0:T(8,128)S(1)} %copy.15.offs, ...), custom_call_target="tpu_custom_call" | custom-call | tf_op jit(solution)/shard_map/waves/pallas_call | solution.py:295
  40.2 3.6 %collective-permute-start.6 = (f32[64,8,384]{2,1,0:T(8,128)S(1)}, f32[64,8,384]{2,1,0:T(8,128)S(1)}, u32[]{:S(2)}, u32[]{:S(2)}) collective-permute-start(f32[64,8,384]{2,1,0:T(8,128)S(1)} %get-tuple-element.36), channel_id=1, source_target_pairs={{0,16},{16,0},{32,48},{48,32},{64,80},{80,64},{96,112},{112,96},{1... | collective-permute-start | bytes 2359304 | tf_op jit(solution)/shard_map/ppermute | solution.py:447
  46.8 9.7 %all-to-all-start = ((f32[64,8,384]{2,1,0:T(8,128)}), f32[64,8,384]{2,1,0:T(8,128)}, u32[]{:S(2)}, u32[]{:S(2)}) async-start(f32[64,8,384]{2,1,0:T(8,128)} %add.73), calls=%async_computation | async-start | bytes 1572864 | tf_op jit(solution)/shard_map/all_to_all | solution.py:432
  56.5 2.5 %collective-permute-start.4 = (f32[6,128,128]{2,1,0:T(8,128)}, f32[6,128,128]{2,1,0:T(8,128)}, u32[]{:S(2)}, u32[]{:S(2)}) collective-permute-start(f32[6,128,128]{2,1,0:T(8,128)} %get-tuple-element.34), channel_id=1, source_target_pairs={{0,16},{1,17},{2,18},{3,19},{4,20},{5,21},{6,22},{7,23},{8,24},{9,... | collective-permute-start | bytes 1179656 | tf_op jit(solution)/shard_map/ppermute | solution.py:370
  62.1 7.9 %coefs.2.coef = f32[32,8]{1,0:T(8,128)} custom-call(f32[4224,128]{1,0:T(8,128)} %get-tuple-element.37.cross_r, f32[4224,128]{1,0:T(8,128)} %get-tuple-element.38.cross_i, f32[4224,128]{1,0:T(8,128)} %get-tuple-element.39.powers, f32[128,8,256]{2,1,0:T(8,128)} %bitcast.38, f32[32,8]{1,0:T(8,128)} %bitcast.47), custom_call_target="tpu_custom_call" | custom-call | tf_op jit(solution)/shard_map/coefs/pallas_call | solution.py:328
  73.1 2.1 %update.2 = (f32[8,256]{1,0:T(8,128)S(1)}, f32[64,8,256]{2,1,0:T(8,128)}) custom-call(f32[64,8,384]{2,1,0:T(8,128)} %all-to-all-done.got, f32[8,256]{1,0:T(8,128)S(1)} %copy-done.13), custom_call_target="tpu_custom_call" | custom-call | tf_op jit(solution)/shard_map/update/pallas_call | solution.py:349
  75.7 12.1 %all-to-all-start.1 = ((f32[64,8,256]{2,1,0:T(8,128)}), f32[64,8,256]{2,1,0:T(8,128)S(1)}, u32[]{:S(2)}, u32[]{:S(2)}) async-start(f32[64,8,256]{2,1,0:T(8,128)} %get-tuple-element.43), calls=%async_computation.1 | async-start | bytes 1048576 | tf_op jit(solution)/shard_map/all_to_all | solution.py:432
  87.9 2.1 %slice_select_fusion = (f32[3,256,128]{2,1,0:T(8,128)}, f32[3,256,128]{2,1,0:T(8,128)}) fusion(f32[6,256,128]{2,1,0:T(8,128)} %pad_maximum_fusion, pred[128]{0:T(512)(128)(4,1)} %iota_compare_fusion), kind=kLoop, calls=%fused_computation.15 | loop fusion | flops 196608 | bytes 1572992 | tf_op jit(solution)/shard_map/jit(_where)/select_n | solution.py:375
  90.1 3.4 %collective-permute-start.7 = (f32[3,256,128]{2,1,0:T(8,128)}, f32[3,256,128]{2,1,0:T(8,128)}, u32[]{:S(2)}, u32[]{:S(2)}) collective-permute-start(f32[3,256,128]{2,1,0:T(8,128)} %get-tuple-element.65), channel_id=1, source_target_pairs={{0,1},{1,2},{2,3},{3,4},{4,5},{5,6},{6,7},{7,8},{8,9},{9,10},{10,1... | collective-permute-start | bytes 1179656 | tf_op jit(solution)/shard_map/ppermute | solution.py:370
  93.4 4.6 %collective-permute-start.8 = (f32[3,256,128]{2,1,0:T(8,128)}, f32[3,256,128]{2,1,0:T(8,128)}, u32[]{:S(2)}, u32[]{:S(2)}) collective-permute-start(f32[3,256,128]{2,1,0:T(8,128)} %get-tuple-element.64), channel_id=1, source_target_pairs={{1,0},{2,1},{3,2},{4,3},{5,4},{6,5},{7,6},{8,7},{9,8},{10,9},{11,1... | collective-permute-start | bytes 1179656 | tf_op jit(solution)/shard_map/ppermute | solution.py:370
  100.8 5.6 %collective-permute-done.7 = f32[3,256,128]{2,1,0:T(8,128)} collective-permute-done((f32[3,256,128]{2,1,0:T(8,128)}, f32[3,256,128]{2,1,0:T(8,128)}, u32[]{:S(2)}, u32[]{:S(2)}) %collective-permute-start.7) | collective-permute-done | bytes 393248 | tf_op jit(solution)/shard_map/ppermute | solution.py:370
  108.6 2.7 %probes.3 = (f32[4224,128]{1,0:T(8,128)S(1)}, f32[4224,128]{1,0:T(8,128)S(1)}) custom-call(s32[1]{0:T(128)} %bitcast.2.half, f32[64,8,256]{2,1,0:T(8,128)S(1)} %all-to-all-done.1.near, f32[64,8,256]{2,1,0:T(8,128)S(1)} %collective-permute-done.9.far, f32[32,8]{1,0:T(8,128)S(1)} %copy-done.12), custom_call_target="tpu_custom_call" | custom-call | tf_op jit(solution)/shard_map/probes/pallas_call | solution.py:279
  111.3 15.0 %waves.3 = (f32[6,64,128]{2,1,0:T(8,128)}, f32[6,128,128]{2,1,0:T(8,128)}, f32[6,64,128]{2,1,0:T(8,128)}, f32[4224,128]{1,0:T(8,128)}, f32[4224,128]{1,0:T(8,128...) custom-call(s32[1]{0:T(128)} %bitcast.2.half, s32[32,2]{1,0:T(8,128)S(1)} %copy.15.offs, ...), custom_call_target="tpu_custom_call" | custom-call | tf_op jit(solution)/shard_map/waves/pallas_call | solution.py:295
  126.5 2.3 %collective-permute-done.14 = f32[64,8,384]{2,1,0:T(8,128)S(1)} collective-permute-done((f32[64,8,384]{2,1,0:T(8,128)S(1)}, f32[64,8,384]{2,1,0:T(8,128)S(1)}, u32[]{:S(2)}, u32[]{:S(2)}) %collective-permute-start.14) | collective-permute-done | bytes 786464 | tf_op jit(solution)/shard_map/ppermute | solution.py:447
  129.8 11.1 %all-to-all-start.2 = ((f32[64,8,384]{2,1,0:T(8,128)}), f32[64,8,384]{2,1,0:T(8,128)S(1)}, u32[]{:S(2)}, u32[]{:S(2)}) async-start(f32[64,8,384]{2,1,0:T(8,128)} %add.87), calls=%async_computation.2 | async-start | bytes 1572864 | tf_op jit(solution)/shard_map/all_to_all | solution.py:432
  144.8 7.9 %coefs.3 = f32[32,8]{1,0:T(8,128)} custom-call(f32[4224,128]{1,0:T(8,128)} %get-tuple-element.52.cross_r, f32[4224,128]{1,0:T(8,128)} %get-tuple-element.53.cross_i, f32[4224,128]{1,0:T(8,128)} %get-tuple-element.54.powers, f32[128,8,256]{2,1,0:T(8,128)} %maximum_select_fusion.modes, f32[32,8]{1,0:T(8,128)} %coefs.2.coef), custom_call_target="tpu_custom_call" | custom-call | tf_op jit(solution)/shard_map/coefs/pallas_call | solution.py:328
  152.7 3.5 %all-to-all-done.2.got = f32[64,8,384]{2,1,0:T(8,128)S(1)} async-done(((f32[64,8,384]{2,1,0:T(8,128)}), f32[64,8,384]{2,1,0:T(8,128)S(1)}, u32[]{:S(2)}, u32[]{:S(2)}) %all-to-all-start.2) | async-done | bytes 786464 | tf_op jit(solution)/shard_map/all_to_all | solution.py:432
  157.1 9.8 %all-to-all-start.3 = ((f32[64,8,256]{2,1,0:T(8,128)}), f32[64,8,256]{2,1,0:T(8,128)S(1)}, u32[]{:S(2)}, u32[]{:S(2)}) async-start(f32[64,8,256]{2,1,0:T(8,128)} %get-tuple-element.57), calls=%async_computation.3 | async-start | bytes 1048576 | tf_op jit(solution)/shard_map/all_to_all | solution.py:432
  167.0 3.4 %collective-permute-start.12 = (f32[3,128,128]{2,1,0:T(8,128)S(1)}, f32[3,128,128]{2,1,0:T(8,128)S(1)}, u32[]{:S(2)}, u32[]{:S(2)}) collective-permute-start(f32[3,128,128]{2,1,0:T(8,128)S(1)} %slice.50), channel_id=1, source_target_pairs={{0,1},{1,2},{2,3},{3,4},{4,5},{5,6},{6,7},{7,8},{8,9},{9,10},{10,1... | collective-permute-start | bytes 589832 | tf_op jit(solution)/shard_map/ppermute | solution.py:370
  170.3 4.6 %collective-permute-start.13 = (f32[3,128,128]{2,1,0:T(8,128)S(1)}, f32[3,128,128]{2,1,0:T(8,128)S(1)}, u32[]{:S(2)}, u32[]{:S(2)}) collective-permute-start(f32[3,128,128]{2,1,0:T(8,128)S(1)} %slice.50), channel_id=1, source_target_pairs={{1,0},{2,1},{3,2},{4,3},{5,4},{6,5},{7,6},{8,7},{9,8},{10,9},{11,1... | collective-permute-start | bytes 589832 | tf_op jit(solution)/shard_map/ppermute | solution.py:370
  174.9 4.6 %all-to-all-done.3 = f32[64,8,256]{2,1,0:T(8,128)S(1)} async-done(((f32[64,8,256]{2,1,0:T(8,128)}), f32[64,8,256]{2,1,0:T(8,128)S(1)}, u32[]{:S(2)}, u32[]{:S(2)}) %all-to-all-start.3) | async-done | bytes 524320 | tf_op jit(solution)/shard_map/all_to_all | solution.py:432
  (122 shorter events, 38.6 us)
Async XLA Ops:
  0.6 13.2 %collective-permute-start = (f32[2,128,128]{2,1,0:T(8,128)}, f32[2,128,128]{2,1,0:T(8,128)}, u32[]{:S(2)}, u32[]{:S(2)}) collective-permute-start(f32[2,128,128]{2,1,0:T(8,128)} %param.10), channel_id=1, source_target_pairs={{1,0},{2,1},{3,2},{4,3},{5,4},{6,5},{7,6},{8,7},{9,8},{10,9},{11,1... | collective-permute-start | bytes 393224 | tf_op jit(solution)/shard_map/ppermute | solution.py:370
  6.6 9.3 %collective-permute-start.1 = (f32[2,128,128]{2,1,0:T(8,128)}, f32[2,128,128]{2,1,0:T(8,128)}, u32[]{:S(2)}, u32[]{:S(2)}) collective-permute-start(f32[2,128,128]{2,1,0:T(8,128)} %param.10), channel_id=1, source_target_pairs={{0,1},{1,2},{2,3},{3,4},{4,5},{5,6},{6,7},{7,8},{8,9},{9,10},{10,1... | collective-permute-start | bytes 393224 | tf_op jit(solution)/shard_map/ppermute | solution.py:370
  12.8 48.6 %copy-start = (f32[128,8,2,128]{3,1,2,0:T(8,128)}, f32[128,8,2,128]{3,1,2,0:T(8,128)S(1)}, u32[]{:S(2)}) copy-start(f32[128,8,2,128]{3,1,2,0:T(8,128)S(1)} %copy.24) | copy-start | bytes 3145732
  17.8 6.1 %collective-permute-start.2 = (f32[2,2,64,128]{3,2,1,0:T(8,128)S(1)}, f32[2,2,64,128]{3,2,1,0:T(8,128)S(1)}, u32[]{:S(2)}, u32[]{:S(2)}) collective-permute-start(f32[2,2,64,128]{3,2,1,0:T(8,128)S(1)} %get-tuple-element.66), channel_id=1, source_target_pairs={{0,16},{1,17},{2,18},{3,19},{4,20},{5,21},{6,22},{7,23},{8,24},{9,... | collective-permute-start | bytes 393224 | tf_op jit(solution)/shard_map/ppermute | solution.py:370
  19.1 5.0 %collective-permute-start.3 = (f32[2,2,64,128]{3,2,1,0:T(8,128)S(1)}, f32[2,2,64,128]{3,2,1,0:T(8,128)S(1)}, u32[]{:S(2)}, u32[]{:S(2)}) collective-permute-start(f32[2,2,64,128]{3,2,1,0:T(8,128)S(1)} %get-tuple-element.67), channel_id=1, source_target_pairs={{16,0},{17,1},{18,2},{19,3},{20,4},{21,5},{22,6},{23,7},{24,8},{25... | collective-permute-start | bytes 393224 | tf_op jit(solution)/shard_map/ppermute | solution.py:370
  40.2 5.5 %collective-permute-start.6 = (f32[64,8,384]{2,1,0:T(8,128)S(1)}, f32[64,8,384]{2,1,0:T(8,128)S(1)}, u32[]{:S(2)}, u32[]{:S(2)}) collective-permute-start(f32[64,8,384]{2,1,0:T(8,128)S(1)} %get-tuple-element.36), channel_id=1, source_target_pairs={{0,16},{16,0},{32,48},{48,32},{64,80},{80,64},{96,112},{112,96},{1... | collective-permute-start | bytes 2359304 | tf_op jit(solution)/shard_map/ppermute | solution.py:447
  46.8 26.3 %all-to-all-start = ((f32[64,8,384]{2,1,0:T(8,128)}), f32[64,8,384]{2,1,0:T(8,128)}, u32[]{:S(2)}, u32[]{:S(2)}) async-start(f32[64,8,384]{2,1,0:T(8,128)} %add.73), calls=%async_computation | async-start | bytes 1572864 | tf_op jit(solution)/shard_map/all_to_all | solution.py:432
  56.5 13.5 %collective-permute-start.4 = (f32[6,128,128]{2,1,0:T(8,128)}, f32[6,128,128]{2,1,0:T(8,128)}, u32[]{:S(2)}, u32[]{:S(2)}) collective-permute-start(f32[6,128,128]{2,1,0:T(8,128)} %get-tuple-element.34), channel_id=1, source_target_pairs={{0,16},{1,17},{2,18},{3,19},{4,20},{5,21},{6,22},{7,23},{8,24},{9,... | collective-permute-start | bytes 1179656 | tf_op jit(solution)/shard_map/ppermute | solution.py:370
  59.0 12.1 %collective-permute-start.5 = (f32[6,128,128]{2,1,0:T(8,128)}, f32[6,128,128]{2,1,0:T(8,128)}, u32[]{:S(2)}, u32[]{:S(2)}) collective-permute-start(f32[6,128,128]{2,1,0:T(8,128)} %get-tuple-element.33), channel_id=1, source_target_pairs={{16,0},{17,1},{18,2},{19,3},{20,4},{21,5},{22,6},{23,7},{24,8},{25... | collective-permute-start | bytes 1179656 | tf_op jit(solution)/shard_map/ppermute | solution.py:370
  75.7 25.1 %all-to-all-start.1 = ((f32[64,8,256]{2,1,0:T(8,128)}), f32[64,8,256]{2,1,0:T(8,128)S(1)}, u32[]{:S(2)}, u32[]{:S(2)}) async-start(f32[64,8,256]{2,1,0:T(8,128)} %get-tuple-element.43), calls=%async_computation.1 | async-start | bytes 1048576 | tf_op jit(solution)/shard_map/all_to_all | solution.py:432
  90.1 16.4 %collective-permute-start.7 = (f32[3,256,128]{2,1,0:T(8,128)}, f32[3,256,128]{2,1,0:T(8,128)}, u32[]{:S(2)}, u32[]{:S(2)}) collective-permute-start(f32[3,256,128]{2,1,0:T(8,128)} %get-tuple-element.65), channel_id=1, source_target_pairs={{0,1},{1,2},{2,3},{3,4},{4,5},{5,6},{6,7},{7,8},{8,9},{9,10},{10,1... | collective-permute-start | bytes 1179656 | tf_op jit(solution)/shard_map/ppermute | solution.py:370
  93.4 13.0 %collective-permute-start.8 = (f32[3,256,128]{2,1,0:T(8,128)}, f32[3,256,128]{2,1,0:T(8,128)}, u32[]{:S(2)}, u32[]{:S(2)}) collective-permute-start(f32[3,256,128]{2,1,0:T(8,128)} %get-tuple-element.64), channel_id=1, source_target_pairs={{1,0},{2,1},{3,2},{4,3},{5,4},{6,5},{7,6},{8,7},{9,8},{10,9},{11,1... | collective-permute-start | bytes 1179656 | tf_op jit(solution)/shard_map/ppermute | solution.py:370
  100.8 7.3 %collective-permute-start.9 = (f32[64,8,256]{2,1,0:T(8,128)S(1)}, f32[64,8,256]{2,1,0:T(8,128)S(1)}, u32[]{:S(2)}, u32[]{:S(2)}) collective-permute-start(f32[64,8,256]{2,1,0:T(8,128)S(1)} %all-to-all-done.1.near), channel_id=1, source_target_pairs={{0,16},{16,0},{32,48},{48,32},{64,80},{80,64},{96,112},{112,96},{1... | collective-permute-start | bytes 1572872 | tf_op jit(solution)/shard_map/ppermute | solution.py:455
  126.4 2.4 %collective-permute-start.14 = (f32[64,8,384]{2,1,0:T(8,128)S(1)}, f32[64,8,384]{2,1,0:T(8,128)S(1)}, u32[]{:S(2)}, u32[]{:S(2)}) collective-permute-start(f32[64,8,384]{2,1,0:T(8,128)S(1)} %get-tuple-element.51), channel_id=1, source_target_pairs={{0,16},{16,0},{32,48},{48,32},{64,80},{80,64},{96,112},{112,96},{1... | collective-permute-start | bytes 2359304 | tf_op jit(solution)/shard_map/ppermute | solution.py:447
  129.8 26.4 %all-to-all-start.2 = ((f32[64,8,384]{2,1,0:T(8,128)}), f32[64,8,384]{2,1,0:T(8,128)S(1)}, u32[]{:S(2)}, u32[]{:S(2)}) async-start(f32[64,8,384]{2,1,0:T(8,128)} %add.87), calls=%async_computation.2 | async-start | bytes 1572864 | tf_op jit(solution)/shard_map/all_to_all | solution.py:432
  140.9 26.0 %collective-permute-start.10 = (f32[6,64,128]{2,1,0:T(8,128)S(1)}, f32[6,64,128]{2,1,0:T(8,128)S(1)}, u32[]{:S(2)}, u32[]{:S(2)}) collective-permute-start(f32[6,64,128]{2,1,0:T(8,128)S(1)} %copy-done.31), channel_id=1, source_target_pairs={{0,16},{1,17},{2,18},{3,19},{4,20},{5,21},{6,22},{7,23},{8,24},{9,... | collective-permute-start | bytes 589832 | tf_op jit(solution)/shard_map/ppermute | solution.py:370
  142.4 24.5 %collective-permute-start.11 = (f32[6,64,128]{2,1,0:T(8,128)S(1)}, f32[6,64,128]{2,1,0:T(8,128)S(1)}, u32[]{:S(2)}, u32[]{:S(2)}) collective-permute-start(f32[6,64,128]{2,1,0:T(8,128)S(1)} %copy-done.30), channel_id=1, source_target_pairs={{16,0},{17,1},{18,2},{19,3},{20,4},{21,5},{22,6},{23,7},{24,8},{25... | collective-permute-start | bytes 589832 | tf_op jit(solution)/shard_map/ppermute | solution.py:370
  144.8 22.1 %copy-start.25 = (f32[6,128,128]{2,1,0:T(8,128)S(1)}, f32[6,128,128]{2,1,0:T(8,128)}, u32[]{:S(2)}) copy-start(f32[6,128,128]{2,1,0:T(8,128)} %get-tuple-element.47) | copy-start | bytes 1179652
  152.7 28.3 %copy-start.28 = (pred[128]{0:T(512)(128)(4,1)S(1)}, pred[128]{0:T(512)(128)(4,1)}, u32[]{:S(2)}) copy-start(pred[128]{0:T(512)(128)(4,1)} %iota_compare_fusion) | copy-start | bytes 388
  157.1 25.5 %copy-start.27 = (f32[32,8]{1,0:T(8,128)S(1)}, f32[32,8]{1,0:T(8,128)}, u32[]{:S(2)}) copy-start(f32[32,8]{1,0:T(8,128)} %coefs.3) | copy-start | bytes 3076
  157.1 22.5 %all-to-all-start.3 = ((f32[64,8,256]{2,1,0:T(8,128)}), f32[64,8,256]{2,1,0:T(8,128)S(1)}, u32[]{:S(2)}, u32[]{:S(2)}) async-start(f32[64,8,256]{2,1,0:T(8,128)} %get-tuple-element.57), calls=%async_computation.3 | async-start | bytes 1048576 | tf_op jit(solution)/shard_map/all_to_all | solution.py:432
  167.0 14.0 %collective-permute-start.12 = (f32[3,128,128]{2,1,0:T(8,128)S(1)}, f32[3,128,128]{2,1,0:T(8,128)S(1)}, u32[]{:S(2)}, u32[]{:S(2)}) collective-permute-start(f32[3,128,128]{2,1,0:T(8,128)S(1)} %slice.50), channel_id=1, source_target_pairs={{0,1},{1,2},{2,3},{3,4},{4,5},{5,6},{6,7},{7,8},{8,9},{9,10},{10,1... | collective-permute-start | bytes 589832 | tf_op jit(solution)/shard_map/ppermute | solution.py:370
  170.3 10.6 %collective-permute-start.13 = (f32[3,128,128]{2,1,0:T(8,128)S(1)}, f32[3,128,128]{2,1,0:T(8,128)S(1)}, u32[]{:S(2)}, u32[]{:S(2)}) collective-permute-start(f32[3,128,128]{2,1,0:T(8,128)S(1)} %slice.50), channel_id=1, source_target_pairs={{1,0},{2,1},{3,2},{4,3},{5,4},{6,5},{7,6},{8,7},{9,8},{10,9},{11,1... | collective-permute-start | bytes 589832 | tf_op jit(solution)/shard_map/ppermute | solution.py:370
  179.6 3.9 %collective-permute-start.15 = (f32[64,8,256]{2,1,0:T(8,128)S(1)}, f32[64,8,256]{2,1,0:T(8,128)S(1)}, u32[]{:S(2)}, u32[]{:S(2)}) collective-permute-start(f32[64,8,256]{2,1,0:T(8,128)S(1)} %all-to-all-done.3), channel_id=1, source_target_pairs={{0,16},{16,0},{32,48},{48,32},{64,80},{80,64},{96,112},{112,96},{1... | collective-permute-start | bytes 1572872 | tf_op jit(solution)/shard_map/ppermute | solution.py:455
  (28 other events, 293.9 us)

commit v6 on v5

--- a/solution.py
+++ b/solution.py
@@ -63,36 +63,49 @@
     return jnp.dot(a, b, preferred_element_type=F32)
 
 
-def probe_kernel(half, near, far, coef, probe_r, probe_i):
-    left = triple(coef[...], 1)
-    skip = far.shape[0] - ROWS
-    for source, base, skip in ((near, half[0] * ROWS, 0), (far, (1 - half[0]) * ROWS, skip)):
-
-        def rows(y, _):
-            m = source[skip + y]
-            h = m.astype(BF16).astype(F32)
-            right = jnp.concatenate([h, h, m - h], axis=0).astype(BF16)
-            out = dot(left, right)
-            start = (base + y) * LEAD
-            probe_r[pl.ds(start, PMAX), :] = out[:, :PS]
-            probe_i[pl.ds(start, PMAX), :] = out[:, PS:]
-            return 0
-
-        lax.fori_loop(0, ROWS, rows, 0, unroll=8)
-
-
-def wave_kernel(
-    half, offs, ext, photons, probe_r, probe_i, coef, ahead_t, back_w, ahead_w, back_t,
-    up, mid, down, out_r, out_i, out_p, near, far,
-    acc_rl, acc_rh, acc_il, acc_ih, acc_pl, acc_ph,
-    patches, wave, field, cross_r, cross_i, power, sems,
-):
+def live_only(coef, counts):
+    slot = lax.broadcasted_iota(jnp.int32, coef.shape, 1)
+    return jnp.where(slot < counts[0, 0], coef[...], 0.0)
+
+
+def probe_kernel(base, counts, modes, coef, *refs):
+    probe_r, probe_i = refs[-2:]
+    left = triple(live_only(coef, counts).T, 1)
+
+    def rows(y, _):
+        m = modes[y]
+        h = m.astype(BF16).astype(F32)
+        right = jnp.concatenate([h, h, m - h], axis=0).astype(BF16)
+        out = dot(left, right)
+        start = (base[0] + y) * LEAD
+        probe_r[pl.ds(start, PMAX), :] = out[:, :PS]
+        probe_i[pl.ds(start, PMAX), :] = out[:, PS:]
+        return 0
+
+    lax.fori_loop(0, modes.shape[0], rows, 0, unroll=8)
+
+
+def wave_kernel(half, counts, offs, *refs):
+    (
+        photons, probe_r, probe_i, coef, ahead_t, back_w, ahead_w, back_t,
+        up, mid, down, out_r, out_i, out_p, near, far,
+        acc_rl, acc_rh, acc_il, acc_ih, acc_pl, acc_ph,
+        patches, wave, field, cross_r, cross_i, power, sems, ext,
+    ) = refs[-30:]
+    pieces = refs[:-30]
     step = pl.program_id(0)
     lane = lax.broadcasted_iota(jnp.int32, (PS, PS), 1)
+    if len(pieces) == 1:
+        ext = pieces[0]
     sums = ((acc_rl, acc_rh), (acc_il, acc_ih), (acc_pl, acc_ph))
 
     @pl.when(step == 0)
     def _():
+        if len(pieces) == 3:
+            row = 0
+            for piece in pieces:
+                ext[:, :, row : row + piece.shape[2]] = piece[...]
+                row += piece.shape[2]
         for low, high in sums:
             low[...] = jnp.zeros_like(low)
             high[...] = jnp.zeros_like(high)
@@ -116,8 +129,8 @@
 
     def cut(j, q):
         p = 2 * PAIRS * step + 2 * j + q
-        top = offs[p, 0]
-        left = offs[p, 1]
+        top = offs[0, p]
+        left = offs[1, p]
         turn = (PS + MARGIN - left) & (PS - 1)
         inside = own_lanes(left)
         total = None
@@ -149,8 +162,8 @@
     def finish(j):
         for q in range(2):
             p = 2 * PAIRS * step + 2 * j + q
-            top = offs[p, 0]
-            left = offs[p, 1]
+            top = offs[0, p]
+            left = offs[1, p]
             turn = (left + MARGIN) & (PS - 1)
             inside = own_lanes(left)
             rows = slice(q * PS, (q + 1) * PS)
@@ -199,14 +212,15 @@
             copy.start()
 
         def stacked(x):
-            hi, lo = split(x.T)
+            hi, lo = split(x)
             zero = jnp.zeros_like(hi)
             return jnp.concatenate(
                 [jnp.concatenate([hi, hi], axis=1), jnp.concatenate([lo, zero], axis=1)], axis=0
             )
 
-        left = stacked(coef[...])
-        left_square = stacked(coef[...] * coef[...])
+        used = live_only(coef, counts)
+        left = stacked(used)
+        left_square = stacked(used * used)
         for target, base in ((near, half[0] * ROWS), (far, (1 - half[0]) * ROWS)):
 
             def rows(y, _):
@@ -259,7 +273,7 @@
 
     @pl.when(step == PS // CHUNK - 1)
     def _():
-        out[...] = coef[...] + num[...] / (den[...] + 1.0)
+        out[...] = coef[...] + (num[...] / (den[...] + 1.0)).T
 
 
 def update_kernel(got, mine, new, copies):
@@ -270,23 +284,58 @@
     copies[...] = jnp.broadcast_to(row[None], copies.shape)
 
 
+def beside_kernel(block, right, left, both, first, last):
+    lane = lax.broadcasted_iota(jnp.int32, (PS, PS), 1)
+    for c in range(2):
+        beside = jnp.where(lane < MARGIN, right[c], left[c])
+        for i, plane in ((0, block[c]), (1, beside)):
+            both[c, i] = plane
+            first[c, i] = plane[:MARGIN]
+            last[c, i] = plane[MARGIN:]
+
+
+def rows_kernel(up, down, from_above, from_below, full, to_right, to_left):
+    lane = lax.broadcasted_iota(jnp.int32, (PS, PS), 1)
+    for c in range(3):
+        for rows, own, other in ((slice(0, PS), down, from_above), (slice(PS, EXT), up, from_below)):
+            centre = own[c] + other[c]
+            beside = own[3 + c] + other[3 + c]
+            full[c, rows] = centre
+            full[3 + c, rows] = beside
+            to_right[c, rows] = jnp.where(lane < MARGIN, beside, centre)
+            to_left[c, rows] = jnp.where(lane < MARGIN, centre, beside)
+
+
 SMEM = pl.BlockSpec(memory_space=pltpu.SMEM)
 VMEM = pl.BlockSpec(memory_space=pltpu.VMEM)
 
 
-def mix_probes(half, near, far, coef):
+def mix_probes(base, counts, modes, coef, *before):
     grid = jax.ShapeDtypeStruct((PS * LEAD, PS), F32)
     return pl.pallas_call(
         probe_kernel,
         out_shape=(grid, grid),
-        in_specs=[SMEM, VMEM, VMEM, VMEM],
+        in_specs=[SMEM, SMEM, VMEM, VMEM, *[VMEM] * len(before)],
         out_specs=(VMEM, VMEM),
+        input_output_aliases={4: 0, 5: 1} if before else {},
         compiler_params=pltpu.CompilerParams(vmem_limit_bytes=2 << 20),
         name="probes",
-    )(half, near, far, coef)
-
-
-def waves(half, offs, ext, photons, probe_r, probe_i, coef, tables, width):
+    )(base, counts, modes, coef, *before)
+
+
+def sum_rows(up, down):
+    side = jax.ShapeDtypeStruct((3, EXT, PS), F32)
+    return pl.pallas_call(
+        rows_kernel,
+        out_shape=(jax.ShapeDtypeStruct((6, EXT, PS), F32), side, side),
+        in_specs=[VMEM] * 4,
+        out_specs=(VMEM,) * 3,
+        compiler_params=pltpu.CompilerParams(vmem_limit_bytes=2 << 20),
+        name="rows",
+    )(up, down, shifted(up, (-1, 0)), shifted(down, (1, 0)))
+
+
+def waves(half, counts, offs, pieces, photons, probe_r, probe_i, coef, tables, width):
     edge = pltpu.HBM((6, width, PS), F32)
     inner = pltpu.HBM((6, max(EXT - 2 * width, 8), PS), F32)
     grid = pltpu.HBM((PS * LEAD, PS), F32)
@@ -299,7 +348,8 @@
         in_specs=[
             SMEM,
             SMEM,
-            VMEM,
+            SMEM,
+            *[VMEM] * len(pieces),
             pl.BlockSpec((2 * PAIRS, PS, PS), lambda i: (i, 0, 0)),
             VMEM,
             VMEM,
@@ -314,21 +364,22 @@
             square,
             *[pltpu.VMEM((PS * LEAD, PS), F32)] * 3,
             pltpu.SemaphoreType.DMA((21,)),
+            pltpu.VMEM((2, 2, EXT, PS), F32),
         ],
         compiler_params=pltpu.CompilerParams(
             dimension_semantics=("arbitrary",), vmem_limit_bytes=24 << 20
         ),
         name="waves",
-    )(half, offs, ext, photons, probe_r, probe_i, coef, *tables)
+    )(half, counts, offs, *pieces, photons, probe_r, probe_i, coef, *tables)
 
 
 def new_coefficients(cross_r, cross_i, powers, modes, coef):
     rows = pl.BlockSpec((CHUNK * LEAD, PS), lambda i: (i, 0))
-    whole = pl.BlockSpec((PMAX, MODES), lambda i: (0, 0))
+    whole = pl.BlockSpec((MODES, PMAX), lambda i: (0, 0))
     return pl.pallas_call(
         coef_kernel,
         grid=(PS // CHUNK,),
-        out_shape=jax.ShapeDtypeStruct((PMAX, MODES), F32),
+        out_shape=jax.ShapeDtypeStruct((MODES, PMAX), F32),
         in_specs=[
             rows,
             rows,
@@ -376,25 +427,21 @@
 
 
 def extend(block):
-    beside = by_side(shifted(block, (0, 1)), shifted(block, (0, -1)))
-    both = jnp.stack([block, beside], axis=1)
-    above = shifted(both[:, :, -MARGIN:], (-1, 0))
-    below = shifted(both[:, :, :MARGIN], (1, 0))
-    return jnp.concatenate([above, both, below], axis=2)
-
-
-def sum_rows(up, down):
-    low = down + shifted(up, (-1, 0))
-    high = up + shifted(down, (1, 0))
-    return jnp.concatenate([low, high], axis=1)
-
-
-def sum_columns(full):
-    own, beside = full[:3], full[3:]
-    from_left = shifted(by_side(beside, own), (0, -1))
-    from_right = shifted(by_side(own, beside), (0, 1))
-    own = own + by_side(from_left, from_right)
-    beside = beside + by_side(from_right, from_left)
+    strip = jax.ShapeDtypeStruct((2, 2, MARGIN, PS), F32)
+    both, first, last = pl.pallas_call(
+        beside_kernel,
+        out_shape=(jax.ShapeDtypeStruct((2, 2, PS, PS), F32), strip, strip),
+        in_specs=[VMEM] * 3,
+        out_specs=(VMEM,) * 3,
+        compiler_params=pltpu.CompilerParams(vmem_limit_bytes=2 << 20),
+        name="beside",
+    )(block, shifted(block, (0, 1)), shifted(block, (0, -1)))
+    return shifted(last, (-1, 0)), both, shifted(first, (1, 0))
+
+
+def sum_columns(full, from_left, from_right):
+    own = full[:3] + by_side(from_left, from_right)
+    beside = full[3:] + by_side(from_right, from_left)
     return jnp.stack([own, beside], axis=1)
 
 
@@ -417,10 +464,9 @@
 
 def shards(object_field, probe_modes, coefficients, offsets, counts, measured):
     tables = tuple(jnp.asarray(t) for t in dft_constants())
-    offs = offsets[0, 0]
+    offs = offsets[0, 0].T
     photons = measured[0, 0]
-    coef = coefficients[0, 0]
-    live = (lax.iota(jnp.int32, PMAX) < counts[0, 0]).astype(F32)[:, None]
+    coef = coefficients[0, 0].T
     rows, cols = lax.axis_size("row"), lax.axis_size("col")
     core = lax.axis_index("row") % 2
     half = core.reshape(1)
@@ -433,24 +479,32 @@
 
     modes = probe_modes.transpose(2, 0, 1, 3).reshape(PS, MODES, 2 * PS)
     mine = lax.dynamic_index_in_dim(modes, core * ROWS + place, 0, keepdims=False)
-    ext = extend(object_field)
+    pieces = extend(object_field)
+    ext = jnp.concatenate(pieces, axis=2)
     for iteration in range(ITERS):
         final = iteration == ITERS - 1
-        used = coef * live
         if iteration == 0:
-            probe_r, probe_i = mix_probes(jnp.zeros_like(half), modes, modes, used)
+            probe_r, probe_i = mix_probes(jnp.zeros_like(half), counts, modes, coef)
         else:
-            probe_r, probe_i = mix_probes(half, near, far, used)
+            probe_r, probe_i = mix_probes(half * ROWS, counts, near, coef)
+            probe_r, probe_i = mix_probes((1 - half) * ROWS, counts, far, coef, probe_r, probe_i)
         up, mid, down, cross_r, cross_i, powers, kept, given = waves(
-            half, offs, ext, photons, probe_r, probe_i, used, tables, MARGIN if final else PS
+            half, counts, offs, pieces, photons, probe_r, probe_i, coef, tables, MARGIN if final else PS
         )
         sent = kept + lax.ppermute(given, "row", mates)
         got = exchange(sent)
-        coef = new_coefficients(cross_r, cross_i, powers, modes, coef)
-        got, coef = lax.optimization_barrier((got, coef))
-        mine, copies = update_row(got, mine)
-        if not final:
-            full, copies = lax.optimization_barrier((sum_rows(up, down), copies))
+        if final:
+            coef = new_coefficients(cross_r, cross_i, powers, modes, coef)
+            got, coef = lax.optimization_barrier((got, coef))
+            mine, copies = update_row(got, mine)
+        else:
+            full, to_right, to_left = sum_rows(up, down)
+            from_left = shifted(to_right, (0, -1))
+            from_right = shifted(to_left, (0, 1))
+            got, full = lax.optimization_barrier((got, full))
+            mine, copies = update_row(got, mine)
+            copies, cross_r = lax.optimization_barrier((copies, cross_r))
+            coef = new_coefficients(cross_r, cross_i, powers, modes, coef)
         near = exchange(copies)
         far = lax.ppermute(near, "row", mates)
         modes = jnp.where(
@@ -460,11 +514,12 @@
             total = fold(up, mid, down)
             object_field = ext[:, 0, MARGIN:-MARGIN] + total[0:2] / (total[2:3] + 1.0)
         else:
-            total = sum_columns(full)
+            total = sum_columns(full, from_left, from_right)
             step = total[0:2] / (total[2:3] + 1.0)
             ext = ext + jnp.where(inside_object()[None], step, 0.0)
+            pieces = (ext,)
     probe_modes = modes.reshape(PS, MODES, 2, PS).transpose(1, 2, 0, 3)
-    return (object_field, probe_modes, coef[None, None])
+    return (object_field, probe_modes, coef.T[None, None])
 
 
 def solution(mesh):

time: 187 us -> 189 us (1.011)
  other arithmetic: 20.1 us -> 8.51 us
  waiting for transfers between devices: 21.5 us -> 31 us
  local copies, waits for them, and re-layouts: 7.57 us -> 11.5 us
  starting transfers between devices: 79.3 us -> 76.3 us
  Pallas kernels: 54.3 us -> 56.8 us
    ppermute x12, waiting for transfers between devices: 9.19 us -> 15.3 us  [shifted(): return lax.ppermute(x, ('row', 'col'), pairs)]
    unnamed x66 -> x52, local copies, waits for them, and re-layouts: 3.23 us -> 9.25 us
    all_to_all x4, waiting for transfers between devices: 8.14 us -> 11.5 us  [exchange(): lax.all_to_all(x, ('row', 'col'), 0, 0, axis_index_groups=groups, tiled=T...]
    all_to_all x4, starting transfers between devices: 42.7 us -> 40.3 us  [exchange(): lax.all_to_all(x, ('row', 'col'), 0, 0, axis_index_groups=groups, tiled=T...]
    pallas_call x2 -> x5, Pallas kernels: 5.42 us -> 7.75 us  [the longest x3 5.73 us: mix_probes(): pl.pallas_call(probe_kernel, out_shape=(grid, grid), in_specs=[SMEM, SMEM...]
    mul x2 -> x0, other arithmetic: 2.17 us -> none  [shards(): used = coef * live]
    select_n x1 -> x0, other arithmetic: 2.14 us -> none  [by_side(): return jnp.where(lane < MARGIN, low, high)]
    add x2 -> x0, other arithmetic: 2.08 us -> none  [the longest x1 1.04 us: sum_rows(): low = down + shifted(up, (-1, 0))]
  transfers between devices with their start and end apart: 20 -> 20, of which waited for: 8 -> 10; matrix products, arithmetic and copies ran while one was open for 11% -> 4% of each run, Pallas kernels for 11% -> 12%
where the time goes in v6:
time: 189 us; the launch traced here: 186 us
  starting transfers between devices  76.3 us (40%)
  Pallas kernels  56.8 us (30%)
  waiting for transfers between devices  31 us (16%)
  local copies, waits for them, and re-layouts  11.5 us (6%)
  other arithmetic  8.51 us (5%)
  between operations  1.92 us (1%)
    all_to_all x4, starting transfers between devices, exchange(): lax.all_to_all(x, ('row', 'col'), 0, 0, axis_index_groups=groups, tiled=T...  40.3 us
    ppermute x12, starting transfers between devices, shifted(): return lax.ppermute(x, ('row', 'col'), pairs)  33.4 us
    pallas_call x2, Pallas kernels, waves(): pl.pallas_call(wave_kernel, grid=(PMAX // (2 * PAIRS),), out_shape=(edge,...  30.3 us
    pallas_call x2, Pallas kernels, new_coefficients(): pl.pallas_call(coef_kernel, grid=(PS // CHUNK,), out_shape=jax.ShapeDtype...  15.7 us
    ppermute x12, waiting for transfers between devices, shifted(): return lax.ppermute(x, ('row', 'col'), pairs)  15.3 us
    all_to_all x4, waiting for transfers between devices, exchange(): lax.all_to_all(x, ('row', 'col'), 0, 0, axis_index_groups=groups, tiled=T...  11.5 us
    unnamed x52, local copies, waits for them, and re-layouts  9.25 us
    pallas_call x3, Pallas kernels, mix_probes(): pl.pallas_call(probe_kernel, out_shape=(grid, grid), in_specs=[SMEM, SMEM...  5.73 us
  transfers between devices with their start and end apart: 20, of which 10 were waited for; matrix products, arithmetic and copies ran while one was open for 4% of the time, Pallas kernels for 12%

profile of v6, /device:TPU:2, one launch (start us, length us, event | category | flops | bytes accessed | tf_op | source)
XLA Modules:
  0.0 186.0 jit_solution(176959642464996537)
XLA Ops:
  0.7 6.0 %collective-permute-start = (f32[2,128,128]{2,1,0:T(8,128)}, f32[2,128,128]{2,1,0:T(8,128)S(1)}, u32[]{:S(2)}, u32[]{:S(2)}) collective-permute-start(f32[2,128,128]{2,1,0:T(8,128)} %block.1), channel_id=1, source_target_pairs={{1,0},{2,1},{3,2},{4,3},{5,4},{6,5},{7,6},{8,7},{9,8},{10,9},{11,1... | collective-permute-start | bytes 393224 | tf_op jit(solution)/shard_map/ppermute | solution.py:421
  9.8 6.1 %collective-permute-done.1.left = f32[2,128,128]{2,1,0:T(8,128)S(1)} collective-permute-done((f32[2,128,128]{2,1,0:T(8,128)}, f32[2,128,128]{2,1,0:T(8,128)S(1)}, u32[]{:S(2)}, u32[]{:S(2)}) %collective-permute-start.1) | collective-permute-done | bytes 131104 | tf_op jit(solution)/shard_map/ppermute | solution.py:421
  24.0 2.8 %probes.3 = (f32[4224,128]{1,0:T(8,128)S(1)}, f32[4224,128]{1,0:T(8,128)S(1)}) custom-call(s32[1]{0:T(128)} %constant.68.clone.1.base, s32[1,1]{1,0:T(1,128)S(6)} %copy.25.counts, f32[128,8,256]{2,1,0:T(8,128)S(1)} %bitcast.35, f32[8,32]{1,0:T(8,128)S(1)} %bitcast.41), custom_call_target="tpu_custom_call" | custom-call | tf_op jit(solution)/shard_map/probes/pallas_call | solution.py:315
  30.8 15.3 %waves.2 = (f32[6,128,128]{2,1,0:T(8,128)}, f32[6,8,128]{2,1,0:T(8,128)}, f32[6,128,128]{2,1,0:T(8,128)}, f32[4224,128]{1,0:T(8,128)}, f32[4224,128]{1,0:T(8,128...) custom-call(s32[1]{0:T(128)} %bitcast.half, s32[1,1]{1,0:T(1,128)S(6)} %copy.25.counts, ...), custom_call_target="tpu_custom_call" | custom-call | tf_op jit(solution)/shard_map/waves/pallas_call | solution.py:344
  46.1 2.4 %collective-permute-start.4 = (f32[64,8,384]{2,1,0:T(8,128)S(1)}, f32[64,8,384]{2,1,0:T(8,128)S(1)}, u32[]{:S(2)}, u32[]{:S(2)}) collective-permute-start(f32[64,8,384]{2,1,0:T(8,128)S(1)} %get-tuple-element.45), channel_id=1, source_target_pairs={{0,16},{16,0},{32,48},{48,32},{64,80},{80,64},{96,112},{112,96},{1... | collective-permute-start | bytes 2359304 | tf_op jit(solution)/shard_map/ppermute | solution.py:494
  51.4 8.6 %all-to-all-start = ((f32[64,8,384]{2,1,0:T(8,128)}), f32[64,8,384]{2,1,0:T(8,128)}, u32[]{:S(2)}, u32[]{:S(2)}) async-start(f32[64,8,384]{2,1,0:T(8,128)} %add.65), calls=%async_computation | async-start | bytes 1572864 | tf_op jit(solution)/shard_map/all_to_all | solution.py:478
  60.1 2.3 %collective-permute-start.5 = (f32[6,128,128]{2,1,0:T(8,128)}, f32[6,128,128]{2,1,0:T(8,128)}, u32[]{:S(2)}, u32[]{:S(2)}) collective-permute-start(f32[6,128,128]{2,1,0:T(8,128)} %get-tuple-element.46.up), channel_id=1, source_target_pairs={{0,16},{1,17},{2,18},{3,19},{4,20},{5,21},{6,22},{7,23},{8,24},{9,... | collective-permute-start | bytes 1179656 | tf_op jit(solution)/shard_map/ppermute | solution.py:421
  63.7 3.4 %collective-permute-done.6.from_below = f32[6,128,128]{2,1,0:T(8,128)} collective-permute-done((f32[6,128,128]{2,1,0:T(8,128)}, f32[6,128,128]{2,1,0:T(8,128)}, u32[]{:S(2)}, u32[]{:S(2)}) %collective-permute-start.6) | collective-permute-done | bytes 393248 | tf_op jit(solution)/shard_map/ppermute | solution.py:421
  72.0 3.3 %all-to-all-done.got = f32[64,8,384]{2,1,0:T(8,128)} async-done(((f32[64,8,384]{2,1,0:T(8,128)}), f32[64,8,384]{2,1,0:T(8,128)}, u32[]{:S(2)}, u32[]{:S(2)}) %all-to-all-start) | async-done | bytes 786464 | tf_op jit(solution)/shard_map/all_to_all | solution.py:478
  75.3 2.1 %update.2 = (f32[8,256]{1,0:T(8,128)S(1)}, f32[64,8,256]{2,1,0:T(8,128)}) custom-call(f32[64,8,384]{2,1,0:T(8,128)} %all-to-all-done.got, f32[8,256]{1,0:T(8,128)S(1)} %dynamic-slice_bitcast_fusion.mine), custom_call_target="tpu_custom_call" | custom-call | tf_op jit(solution)/shard_map/update/pallas_call | solution.py:400
  77.4 13.4 %all-to-all-start.1 = ((f32[64,8,256]{2,1,0:T(8,128)}), f32[64,8,256]{2,1,0:T(8,128)S(1)}, u32[]{:S(2)}, u32[]{:S(2)}) async-start(f32[64,8,256]{2,1,0:T(8,128)} %get-tuple-element.55), calls=%async_computation.1 | async-start | bytes 1048576 | tf_op jit(solution)/shard_map/all_to_all | solution.py:478
  90.8 3.4 %collective-permute-start.7 = (f32[3,256,128]{2,1,0:T(8,128)}, f32[3,256,128]{2,1,0:T(8,128)}, u32[]{:S(2)}, u32[]{:S(2)}) collective-permute-start(f32[3,256,128]{2,1,0:T(8,128)} %copy-done.22), channel_id=1, source_target_pairs={{0,1},{1,2},{2,3},{3,4},{4,5},{5,6},{6,7},{7,8},{8,9},{9,10},{10,1... | collective-permute-start | bytes 1179656 | tf_op jit(solution)/shard_map/ppermute | solution.py:421
  94.2 4.6 %collective-permute-start.8 = (f32[3,256,128]{2,1,0:T(8,128)S(1)}, f32[3,256,128]{2,1,0:T(8,128)}, u32[]{:S(2)}, u32[]{:S(2)}) collective-permute-start(f32[3,256,128]{2,1,0:T(8,128)S(1)} %get-tuple-element.51), channel_id=1, source_target_pairs={{1,0},{2,1},{3,2},{4,3},{5,4},{6,5},{7,6},{8,7},{9,8},{10,9},{11,1... | collective-permute-start | bytes 1179656 | tf_op jit(solution)/shard_map/ppermute | solution.py:421
  99.0 7.8 %coefs.2.coef.refs_4_ = f32[8,32]{1,0:T(8,128)} custom-call(f32[4224,128]{1,0:T(8,128)} %get-tuple-element.56.cross_r, f32[4224,128]{1,0:T(8,128)} %get-tuple-element.57.cross_i, f32[4224,128]{1,0:T(8,128)} %get-tuple-element.58.powers, f32[128,8,256]{2,1,0:T(8,128)} %bitcast.37, f32[8,32]{1,0:T(8,128)} %bitcast.40), custom_call_target="tpu_custom_call" | custom-call | tf_op jit(solution)/shard_map/coefs/pallas_call | solution.py:379
  106.9 3.3 %collective-permute-done.7 = f32[3,256,128]{2,1,0:T(8,128)} collective-permute-done((f32[3,256,128]{2,1,0:T(8,128)}, f32[3,256,128]{2,1,0:T(8,128)}, u32[]{:S(2)}, u32[]{:S(2)}) %collective-permute-start.7) | collective-permute-done | bytes 393248 | tf_op jit(solution)/shard_map/ppermute | solution.py:421
  115.9 15.0 %waves.3 = (f32[6,64,128]{2,1,0:T(8,128)}, f32[6,128,128]{2,1,0:T(8,128)}, f32[6,64,128]{2,1,0:T(8,128)}, f32[4224,128]{1,0:T(8,128)}, f32[4224,128]{1,0:T(8,128...) custom-call(s32[1]{0:T(128)} %bitcast.half, s32[1,1]{1,0:T(1,128)S(6)} %copy.25.counts, ...), custom_call_target="tpu_custom_call" | custom-call | tf_op jit(solution)/shard_map/waves/pallas_call | solution.py:344
  131.0 2.3 %collective-permute-done.14 = f32[64,8,384]{2,1,0:T(8,128)S(1)} collective-permute-done((f32[64,8,384]{2,1,0:T(8,128)S(1)}, f32[64,8,384]{2,1,0:T(8,128)S(1)}, u32[]{:S(2)}, u32[]{:S(2)}) %collective-permute-start.14) | collective-permute-done | bytes 786464 | tf_op jit(solution)/shard_map/ppermute | solution.py:494
  134.3 8.7 %all-to-all-start.2 = ((f32[64,8,384]{2,1,0:T(8,128)}), f32[64,8,384]{2,1,0:T(8,128)S(1)}, u32[]{:S(2)}, u32[]{:S(2)}) async-start(f32[64,8,384]{2,1,0:T(8,128)} %add.79), calls=%async_computation.2 | async-start | bytes 1572864 | tf_op jit(solution)/shard_map/all_to_all | solution.py:478
  146.9 7.9 %coefs.3 = f32[8,32]{1,0:T(8,128)} custom-call(f32[4224,128]{1,0:T(8,128)} %get-tuple-element.68.cross_r, f32[4224,128]{1,0:T(8,128)} %get-tuple-element.69.cross_i, f32[4224,128]{1,0:T(8,128)} %get-tuple-element.70.powers, f32[128,8,256]{2,1,0:T(8,128)} %maximum_select_fusion.modes, f32[8,32]{1,0:T(8,128)} %coefs.2.coef.refs_4_), custom_call_target="tpu_custom_call" | custom-call | tf_op jit(solution)/shard_map/coefs/pallas_call | solution.py:379
  154.8 3.5 %all-to-all-done.2.got = f32[64,8,384]{2,1,0:T(8,128)S(1)} async-done(((f32[64,8,384]{2,1,0:T(8,128)}), f32[64,8,384]{2,1,0:T(8,128)S(1)}, u32[]{:S(2)}, u32[]{:S(2)}) %all-to-all-start.2) | async-done | bytes 786464 | tf_op jit(solution)/shard_map/all_to_all | solution.py:478
  159.2 9.6 %all-to-all-start.3 = ((f32[64,8,256]{2,1,0:T(8,128)}), f32[64,8,256]{2,1,0:T(8,128)S(1)}, u32[]{:S(2)}, u32[]{:S(2)}) async-start(f32[64,8,256]{2,1,0:T(8,128)} %get-tuple-element.73), calls=%async_computation.3 | async-start | bytes 1048576 | tf_op jit(solution)/shard_map/all_to_all | solution.py:478
  168.9 3.4 %collective-permute-start.12 = (f32[3,128,128]{2,1,0:T(8,128)S(1)}, f32[3,128,128]{2,1,0:T(8,128)S(1)}, u32[]{:S(2)}, u32[]{:S(2)}) collective-permute-start(f32[3,128,128]{2,1,0:T(8,128)S(1)} %slice.40), channel_id=1, source_target_pairs={{0,1},{1,2},{2,3},{3,4},{4,5},{5,6},{6,7},{7,8},{8,9},{9,10},{10,1... | collective-permute-start | bytes 589832 | tf_op jit(solution)/shard_map/ppermute | solution.py:421
  172.3 4.6 %collective-permute-start.13 = (f32[3,128,128]{2,1,0:T(8,128)S(1)}, f32[3,128,128]{2,1,0:T(8,128)S(1)}, u32[]{:S(2)}, u32[]{:S(2)}) collective-permute-start(f32[3,128,128]{2,1,0:T(8,128)S(1)} %slice.40), channel_id=1, source_target_pairs={{1,0},{2,1},{3,2},{4,3},{5,4},{6,5},{7,6},{8,7},{9,8},{10,9},{11,1... | collective-permute-start | bytes 589832 | tf_op jit(solution)/shard_map/ppermute | solution.py:421
  176.9 4.6 %all-to-all-done.3 = f32[64,8,256]{2,1,0:T(8,128)S(1)} async-done(((f32[64,8,256]{2,1,0:T(8,128)}), f32[64,8,256]{2,1,0:T(8,128)S(1)}, u32[]{:S(2)}, u32[]{:S(2)}) %all-to-all-start.3) | async-done | bytes 524320 | tf_op jit(solution)/shard_map/all_to_all | solution.py:478
  (100 shorter events, 39.6 us)
Async XLA Ops:
  0.6 26.2 %copy-start.5 = (bf16[768,256]{1,0:T(8,128)(2,1)S(1)}, bf16[768,256]{1,0:T(8,128)(2,1)}, u32[]{:S(2)}) copy-start(bf16[768,256]{1,0:T(8,128)(2,1)} %constant.75.clone.refs_7_.refs_5_) | copy-start | bytes 1179652
  0.6 26.2 %copy-start.1 = (s32[1,1,32,128,128]{4,3,2,1,0:T(8,128)S(1)}, s32[1,1,32,128,128]{4,3,2,1,0:T(8,128)}, u32[]{:S(2)}) copy-start(s32[1,1,32,128,128]{4,3,2,1,0:T(8,128)} %param.15) | copy-start | bytes 6291460
  0.7 9.1 %collective-permute-start = (f32[2,128,128]{2,1,0:T(8,128)}, f32[2,128,128]{2,1,0:T(8,128)S(1)}, u32[]{:S(2)}, u32[]{:S(2)}) collective-permute-start(f32[2,128,128]{2,1,0:T(8,128)} %block.1), channel_id=1, source_target_pairs={{1,0},{2,1},{3,2},{4,3},{5,4},{6,5},{7,6},{8,7},{9,8},{10,9},{11,1... | collective-permute-start | bytes 393224 | tf_op jit(solution)/shard_map/ppermute | solution.py:421
  6.7 9.2 %collective-permute-start.1 = (f32[2,128,128]{2,1,0:T(8,128)}, f32[2,128,128]{2,1,0:T(8,128)S(1)}, u32[]{:S(2)}, u32[]{:S(2)}) collective-permute-start(f32[2,128,128]{2,1,0:T(8,128)} %block.1), channel_id=1, source_target_pairs={{0,1},{1,2},{2,3},{3,4},{4,5},{5,6},{6,7},{7,8},{8,9},{9,10},{10,1... | collective-permute-start | bytes 393224 | tf_op jit(solution)/shard_map/ppermute | solution.py:421
  18.2 8.6 %collective-permute-start.2 = (f32[2,2,64,128]{3,2,1,0:T(8,128)}, f32[2,2,64,128]{3,2,1,0:T(8,128)}, u32[]{:S(2)}, u32[]{:S(2)}) collective-permute-start(f32[2,2,64,128]{3,2,1,0:T(8,128)} %get-tuple-element.39), channel_id=1, source_target_pairs={{0,16},{1,17},{2,18},{3,19},{4,20},{5,21},{6,22},{7,23},{8,24},{9,... | collective-permute-start | bytes 393224 | tf_op jit(solution)/shard_map/ppermute | solution.py:421
  20.2 6.6 %collective-permute-start.3 = (f32[2,2,64,128]{3,2,1,0:T(8,128)}, f32[2,2,64,128]{3,2,1,0:T(8,128)}, u32[]{:S(2)}, u32[]{:S(2)}) collective-permute-start(f32[2,2,64,128]{3,2,1,0:T(8,128)} %get-tuple-element.41), channel_id=1, source_target_pairs={{16,0},{17,1},{18,2},{19,3},{20,4},{21,5},{22,6},{23,7},{24,8},{25... | collective-permute-start | bytes 393224 | tf_op jit(solution)/shard_map/ppermute | solution.py:421
  24.0 39.7 %copy-start = (f32[128,8,2,128]{3,1,2,0:T(8,128)}, f32[128,8,2,128]{3,1,2,0:T(8,128)S(1)}, u32[]{:S(2)}) copy-start(f32[128,8,2,128]{3,1,2,0:T(8,128)S(1)} %copy.22) | copy-start | bytes 3145732
  46.1 4.3 %collective-permute-start.4 = (f32[64,8,384]{2,1,0:T(8,128)S(1)}, f32[64,8,384]{2,1,0:T(8,128)S(1)}, u32[]{:S(2)}, u32[]{:S(2)}) collective-permute-start(f32[64,8,384]{2,1,0:T(8,128)S(1)} %get-tuple-element.45), channel_id=1, source_target_pairs={{0,16},{16,0},{32,48},{48,32},{64,80},{80,64},{96,112},{112,96},{1... | collective-permute-start | bytes 2359304 | tf_op jit(solution)/shard_map/ppermute | solution.py:494
  51.4 23.9 %all-to-all-start = ((f32[64,8,384]{2,1,0:T(8,128)}), f32[64,8,384]{2,1,0:T(8,128)}, u32[]{:S(2)}, u32[]{:S(2)}) async-start(f32[64,8,384]{2,1,0:T(8,128)} %add.65), calls=%async_computation | async-start | bytes 1572864 | tf_op jit(solution)/shard_map/all_to_all | solution.py:478
  60.1 3.6 %collective-permute-start.5 = (f32[6,128,128]{2,1,0:T(8,128)}, f32[6,128,128]{2,1,0:T(8,128)}, u32[]{:S(2)}, u32[]{:S(2)}) collective-permute-start(f32[6,128,128]{2,1,0:T(8,128)} %get-tuple-element.46.up), channel_id=1, source_target_pairs={{0,16},{1,17},{2,18},{3,19},{4,20},{5,21},{6,22},{7,23},{8,24},{9,... | collective-permute-start | bytes 1179656 | tf_op jit(solution)/shard_map/ppermute | solution.py:421
  62.3 4.7 %collective-permute-start.6 = (f32[6,128,128]{2,1,0:T(8,128)}, f32[6,128,128]{2,1,0:T(8,128)}, u32[]{:S(2)}, u32[]{:S(2)}) collective-permute-start(f32[6,128,128]{2,1,0:T(8,128)} %get-tuple-element.47.down), channel_id=1, source_target_pairs={{16,0},{17,1},{18,2},{19,3},{20,4},{21,5},{22,6},{23,7},{24,8},{25... | collective-permute-start | bytes 1179656 | tf_op jit(solution)/shard_map/ppermute | solution.py:421
  77.4 29.4 %all-to-all-start.1 = ((f32[64,8,256]{2,1,0:T(8,128)}), f32[64,8,256]{2,1,0:T(8,128)S(1)}, u32[]{:S(2)}, u32[]{:S(2)}) async-start(f32[64,8,256]{2,1,0:T(8,128)} %get-tuple-element.55), calls=%async_computation.1 | async-start | bytes 1048576 | tf_op jit(solution)/shard_map/all_to_all | solution.py:478
  90.8 19.4 %collective-permute-start.7 = (f32[3,256,128]{2,1,0:T(8,128)}, f32[3,256,128]{2,1,0:T(8,128)}, u32[]{:S(2)}, u32[]{:S(2)}) collective-permute-start(f32[3,256,128]{2,1,0:T(8,128)} %copy-done.22), channel_id=1, source_target_pairs={{0,1},{1,2},{2,3},{3,4},{4,5},{5,6},{6,7},{7,8},{8,9},{9,10},{10,1... | collective-permute-start | bytes 1179656 | tf_op jit(solution)/shard_map/ppermute | solution.py:421
  94.2 16.0 %collective-permute-start.8 = (f32[3,256,128]{2,1,0:T(8,128)S(1)}, f32[3,256,128]{2,1,0:T(8,128)}, u32[]{:S(2)}, u32[]{:S(2)}) collective-permute-start(f32[3,256,128]{2,1,0:T(8,128)S(1)} %get-tuple-element.51), channel_id=1, source_target_pairs={{1,0},{2,1},{3,2},{4,3},{5,4},{6,5},{7,6},{8,7},{9,8},{10,9},{11,1... | collective-permute-start | bytes 1179656 | tf_op jit(solution)/shard_map/ppermute | solution.py:421
  106.8 7.4 %collective-permute-start.9 = (f32[64,8,256]{2,1,0:T(8,128)S(1)}, f32[64,8,256]{2,1,0:T(8,128)S(1)}, u32[]{:S(2)}, u32[]{:S(2)}) collective-permute-start(f32[64,8,256]{2,1,0:T(8,128)S(1)} %all-to-all-done.1.modes), channel_id=1, source_target_pairs={{0,16},{16,0},{32,48},{48,32},{64,80},{80,64},{96,112},{112,96},{1... | collective-permute-start | bytes 1572872 | tf_op jit(solution)/shard_map/ppermute | solution.py:509
  130.9 2.4 %collective-permute-start.14 = (f32[64,8,384]{2,1,0:T(8,128)S(1)}, f32[64,8,384]{2,1,0:T(8,128)S(1)}, u32[]{:S(2)}, u32[]{:S(2)}) collective-permute-start(f32[64,8,384]{2,1,0:T(8,128)S(1)} %get-tuple-element.67), channel_id=1, source_target_pairs={{0,16},{16,0},{32,48},{48,32},{64,80},{80,64},{96,112},{112,96},{1... | collective-permute-start | bytes 2359304 | tf_op jit(solution)/shard_map/ppermute | solution.py:494
  134.3 24.0 %all-to-all-start.2 = ((f32[64,8,384]{2,1,0:T(8,128)}), f32[64,8,384]{2,1,0:T(8,128)S(1)}, u32[]{:S(2)}, u32[]{:S(2)}) async-start(f32[64,8,384]{2,1,0:T(8,128)} %add.79), calls=%async_computation.2 | async-start | bytes 1572864 | tf_op jit(solution)/shard_map/all_to_all | solution.py:478
  143.0 25.8 %collective-permute-start.10 = (f32[6,64,128]{2,1,0:T(8,128)S(1)}, f32[6,64,128]{2,1,0:T(8,128)S(1)}, u32[]{:S(2)}, u32[]{:S(2)}) collective-permute-start(f32[6,64,128]{2,1,0:T(8,128)S(1)} %copy-done.25), channel_id=1, source_target_pairs={{0,16},{1,17},{2,18},{3,19},{4,20},{5,21},{6,22},{7,23},{8,24},{9,... | collective-permute-start | bytes 589832 | tf_op jit(solution)/shard_map/ppermute | solution.py:421
  144.5 24.3 %collective-permute-start.11 = (f32[6,64,128]{2,1,0:T(8,128)S(1)}, f32[6,64,128]{2,1,0:T(8,128)S(1)}, u32[]{:S(2)}, u32[]{:S(2)}) collective-permute-start(f32[6,64,128]{2,1,0:T(8,128)S(1)} %copy-done.24), channel_id=1, source_target_pairs={{16,0},{17,1},{18,2},{19,3},{20,4},{21,5},{22,6},{23,7},{24,8},{25... | collective-permute-start | bytes 589832 | tf_op jit(solution)/shard_map/ppermute | solution.py:421
  146.9 21.9 %copy-start.23 = (f32[6,128,128]{2,1,0:T(8,128)S(1)}, f32[6,128,128]{2,1,0:T(8,128)}, u32[]{:S(2)}) copy-start(f32[6,128,128]{2,1,0:T(8,128)} %get-tuple-element.63) | copy-start | bytes 1179652
  159.2 22.3 %all-to-all-start.3 = ((f32[64,8,256]{2,1,0:T(8,128)}), f32[64,8,256]{2,1,0:T(8,128)S(1)}, u32[]{:S(2)}, u32[]{:S(2)}) async-start(f32[64,8,256]{2,1,0:T(8,128)} %get-tuple-element.73), calls=%async_computation.3 | async-start | bytes 1048576 | tf_op jit(solution)/shard_map/all_to_all | solution.py:478
  168.9 14.0 %collective-permute-start.12 = (f32[3,128,128]{2,1,0:T(8,128)S(1)}, f32[3,128,128]{2,1,0:T(8,128)S(1)}, u32[]{:S(2)}, u32[]{:S(2)}) collective-permute-start(f32[3,128,128]{2,1,0:T(8,128)S(1)} %slice.40), channel_id=1, source_target_pairs={{0,1},{1,2},{2,3},{3,4},{4,5},{5,6},{6,7},{7,8},{8,9},{9,10},{10,1... | collective-permute-start | bytes 589832 | tf_op jit(solution)/shard_map/ppermute | solution.py:421
  172.3 10.6 %collective-permute-start.13 = (f32[3,128,128]{2,1,0:T(8,128)S(1)}, f32[3,128,128]{2,1,0:T(8,128)S(1)}, u32[]{:S(2)}, u32[]{:S(2)}) collective-permute-start(f32[3,128,128]{2,1,0:T(8,128)S(1)} %slice.40), channel_id=1, source_target_pairs={{1,0},{2,1},{3,2},{4,3},{5,4},{6,5},{7,6},{8,7},{9,8},{10,9},{11,1... | collective-permute-start | bytes 589832 | tf_op jit(solution)/shard_map/ppermute | solution.py:421
  181.5 3.2 %collective-permute-start.15 = (f32[64,8,256]{2,1,0:T(8,128)S(1)}, f32[64,8,256]{2,1,0:T(8,128)S(1)}, u32[]{:S(2)}, u32[]{:S(2)}) collective-permute-start(f32[64,8,256]{2,1,0:T(8,128)S(1)} %all-to-all-done.3), channel_id=1, source_target_pairs={{0,16},{16,0},{32,48},{48,32},{64,80},{80,64},{96,112},{112,96},{1... | collective-permute-start | bytes 1572872 | tf_op jit(solution)/shard_map/ppermute | solution.py:509
  (22 other events, 82.2 us)
